TPU v7x, 128 devices: a whole 4x4x4 slice. The times are simulated.
128 devices in a mesh: seq: 32 (over x, y, core), chan: 4 (over z).
Axes of the slice: x: 4, y: 4, z: 4, core: 2. Of those that a mesh axis runs over, the one named last changes fastest.
Arguments:
- tokens: bfloat16 [16384, 8192], P('seq'), may hold values from -6 to 6
- proj_weight: bfloat16 [8192, 3, 2048], P('seq', None, 'chan'), may hold values from -0.0625 to 0.0625
- residues: float32 [16, 2048], P(None, 'chan'), may hold values from -1.5 to 1.5
- decay_rates: float32 [16, 2048], P(None, 'chan'), may hold values from 3.0517578e-05 to 0.05
- skip_gain: float32 [2048], P('chan'), may hold values from -3 to 3
- grad_out: bfloat16 [16384, 2048], P('seq', 'chan'), may hold values from -6 to 6
Outputs:
- gated_output: bfloat16 [16384, 2048], P('seq', 'chan')
- grad_tokens: bfloat16 [16384, 8192], P('seq', 'chan')
All inputs are finite; a program needn't handle non-finite values.
Results may differ from a plain program's by a relative error of at most 0.022.
Values may be sent and summed in bfloat16 or wider, within the bound.
A program may use at most 128 MiB of HBM per device.

v0:
```python
import math

import jax
import jax.numpy as jnp
from jax import lax
from jax.sharding import PartitionSpec as P

f32 = jnp.float32
bf16 = jnp.bfloat16


def dft_tables(block_len):
    n_len = 2 * block_len
    k = jnp.arange(block_len, dtype=jnp.int32)[:, None]
    n = jnp.arange(block_len, dtype=jnp.int32)[None, :]
    phase = (k * n) % n_len
    angle = (2.0 * math.pi / n_len) * phase.astype(f32)
    cos_rows = jnp.cos(angle)
    sin_rows = jnp.sin(angle)
    nyquist = jnp.where(n % 2 == 0, 1.0, -1.0).astype(f32)
    sin_rows = jnp.where(k == 0, nyquist, sin_rows)
    fwd = jnp.concatenate([cos_rows, sin_rows], axis=0)
    weight = jnp.where(k == 0, 1.0, 2.0).astype(f32) / n_len
    inv = (jnp.concatenate([cos_rows * weight, sin_rows * weight], axis=0)).T
    return fwd, inv


def spectral_conv(signal, fwd, inv, h_a, h_a2, h_b):
    block_len = signal.shape[0]
    spec = jnp.dot(fwd, signal.astype(bf16), preferred_element_type=f32)
    xc = spec[:block_len]
    xs = spec[block_len:]
    pr = xc * h_a - xs * h_b
    pi = xc * h_b + xs * h_a2
    prod = jnp.concatenate([pr, pi], axis=0).astype(bf16)
    return jnp.dot(inv, prod, preferred_element_type=f32)


def local(tokens, proj_weight, residues, decay_rates, skip_gain, grad_out):
    tok_rows = tokens.shape[0]
    chan_count = skip_gain.shape[0]
    seq_count = lax.axis_size("seq")
    me = lax.axis_index("seq")
    flat_w = proj_weight.reshape(proj_weight.shape[0], 3 * chan_count)
    whole_w = lax.all_gather(flat_w, "seq", axis=0, tiled=True)
    projected = jnp.dot(tokens, whole_w, preferred_element_type=f32)
    proj_vals = (
        lax.optimization_barrier(projected.astype(bf16))
        .astype(f32)
        .reshape(tok_rows, 3, chan_count)
    )
    query_in = proj_vals[:, 0]
    key_in = proj_vals[:, 1]
    value_in = proj_vals[:, 2]
    mixed_in = key_in * value_in
    grad_gate = grad_out.astype(f32)
    grad_mix = grad_gate * query_in

    rates = decay_rates
    mode_gain = residues * jnp.sqrt(-jnp.expm1(-2.0 * rates))
    steps = jnp.arange(tok_rows, dtype=f32)

    fwd_w = jnp.exp(-rates[:, None, :] * (tok_rows - 1 - steps)[None, :, None])
    bwd_w = jnp.exp(-rates[:, None, :] * steps[None, :, None])
    end_fwd = jnp.sum(fwd_w * mixed_in[None], axis=1)
    end_bwd = jnp.sum(bwd_w * grad_mix[None], axis=1)
    states = jnp.stack([end_fwd, end_bwd])
    every = lax.all_gather(states, "seq")

    others = jnp.arange(seq_count, dtype=jnp.int32)
    gap_f = me - 1 - others
    gap_b = others - me - 1
    span = rates[None] * float(tok_rows)
    w_f = jnp.where(
        (gap_f >= 0)[:, None, None],
        jnp.exp(-span * jnp.maximum(gap_f, 0).astype(f32)[:, None, None]),
        0.0,
    )
    w_b = jnp.where(
        (gap_b >= 0)[:, None, None],
        jnp.exp(-span * jnp.maximum(gap_b, 0).astype(f32)[:, None, None]),
        0.0,
    )
    into_f = jnp.sum(w_f * every[:, 0], axis=0) * mode_gain
    into_b = jnp.sum(w_b * every[:, 1], axis=0) * mode_gain

    taps = jnp.sum(mode_gain[:, None, :] * bwd_w, axis=0)
    fwd, inv = dft_tables(tok_rows)
    fwd_b = fwd.astype(bf16)
    inv_b = inv.astype(bf16)
    spec = jnp.dot(fwd, taps, precision=lax.Precision.HIGHEST)
    row0 = (jnp.arange(tok_rows) == 0)[:, None]
    h_a = spec[:tok_rows]
    h_a2 = jnp.where(row0, spec[tok_rows:tok_rows + 1], h_a)
    h_b = jnp.where(row0, 0.0, spec[tok_rows:])

    local_f = spectral_conv(mixed_in, fwd_b, inv_b, h_a, h_a2, h_b)
    carry_f = jnp.sum(into_f[:, None, :] * jnp.exp(-rates[:, None, :] * (steps + 1.0)[None, :, None]), axis=0)
    filtered = local_f + carry_f + skip_gain[None, :] * mixed_in
    gated_output = (query_in * filtered).astype(bf16)
    grad_query = grad_gate * filtered

    local_b = spectral_conv(grad_mix, fwd_b[:, ::-1], inv_b[::-1, :], h_a, h_a2, h_b)
    carry_b = jnp.sum(
        into_b[:, None, :] * jnp.exp(-rates[:, None, :] * (tok_rows - steps)[None, :, None]), axis=0
    )
    grad_conv = local_b + carry_b + skip_gain[None, :] * grad_mix

    grad_proj = jnp.stack([grad_query, grad_conv * value_in, grad_conv * key_in], axis=1).astype(bf16)
    grad_proj = grad_proj.reshape(tok_rows, 3 * chan_count)
    contract = (((1,), (1,)), ((), ()))
    dx_terms = lax.dot_general(grad_proj, whole_w, contract, preferred_element_type=f32)
    grad_tokens = lax.psum_scatter(dx_terms.astype(bf16), "chan", scatter_dimension=1, tiled=True)
    return (gated_output, grad_tokens)


def solution(mesh):
    placed = (
        P("seq", None),
        P("seq", None, "chan"),
        P(None, "chan"),
        P(None, "chan"),
        P("chan"),
        P("seq", "chan"),
    )
    return jax.shard_map(
        local,
        mesh=mesh,
        in_specs=placed,
        out_specs=(P("seq", "chan"), P("seq", "chan")),
        check_vma=False,
    )
```

profile of v0, /device:TPU:32, one launch (start us, length us, event | category | flops | bytes accessed | tf_op | source)
XLA Modules:
  0.0 340.9 jit_solution(16622616147997129211)
XLA Ops:
  7.2 0.0 copy-start.18
  7.2 0.0 all-gather.4.cloned.1.call-start
  7.2 2.3 copy.29
  9.5 0.0 all-gather.4.cloned.1.call-update
  9.5 0.0 all-gather.6.cloned.1.call-start
  9.6 2.0 copy.32
  11.6 0.0 copy-done.18
  11.7 104.1 %all-gather.4.cloned.1.call-done = bf16[8192,1536]{0,1:T(8,128)(2,1)} async-done(((bf16[256,1536]{0,1:T(8,128)(2,1)}), bf16[8192,1536]{0,1:T(8,128)(2,1)}) %all-gather.4.cloned.1.call-update) | async-done | bytes 25165840 | tf_op jit(solution)/shard_map/all_gather | solution.py:45
  115.8 20.1 %convolution_convert_fusion.1 = bf16[512,1536]{1,0:T(8,128)(2,1)} fusion(bf16[512,8192]{1,0:T(8,128)(2,1)} %param.6, bf16[8192,1536]{0,1:T(8,128)(2,1)} %all-gather.4.cloned.1.call-done), kind=kOutput, calls=%fused_computation.7 | convolution fusion | flops 12885688320 | bytes 35127296 | tf_op jit(solution)/shard_map/dot_general | solution.py:46
  135.9 1.7 copy.30
  137.7 2.8 convert_multiply_fusion.1
  140.5 2.5 copy.31
  143.0 2.6 copy.33
  145.6 7.2 %multiply_reduce_fusion.3 = (f32[16,512]{1,0:T(8,128)S(1)}, f32[16,512]{1,0:T(8,128)S(1)}) fusion(f32[512,512]{1,0:T(8,128)} %copy.31, f32[512]{0:T(512)S(1)} %iota_subtract_fusion.1, f32[16,512]{1,0:T(8,128)S(1)} %get-tuple-element.32, f32[512,512]{1,0:T(8,128)} %copy.33), kind=kLoop, calls=%fused_computation.3 | loop fusion | flops 25149440 | bytes 2197504 | tf_op jit(solution)/shard_map/reduce_sum | solution.py:65
  152.8 0.6 pad_maximum_fusion.5
  153.4 0.0 all-gather.6.cloned.1.call-update
  153.5 0.2 reduce-scatter.2.cloned.1.call-start
  153.7 3.8 %fusion.30 = f32[512,512]{1,0:T(8,128)S(1)} fusion(), kind=kLoop, calls=%fused_computation.64 | loop fusion | flops 3670016 | bytes 1048576 | tf_op jit(solution)/shard_map/cos | solution.py:18
  157.5 0.0 copy-start.4
  157.5 4.3 %multiply_convert_fusion.3 = (bf16[512,512]{1,0:T(8,128)(2,1)S(1)}, f32[512,512]{1,0:T(8,128)S(1)}, bf16[512,512]{1,0:T(8,128)(2,1)S(1)}) fusion(f32[512]{0:T(512)S(1)} %select_multiply_fusion, f32[512]{0:T(512)S(1)} %fusion.34, pred[512]{0:T(512)(128)(4,1)S(1)} %iota_compare_fusion), kind=kLoop, calls=%fused_computation.49 | loop fusion | flops 4980736 | bytes 2101760 | tf_op jit(solution)/shard_map/convert.12
  161.9 0.0 copy-start.2
  161.9 0.0 copy-start.12
  161.9 0.0 copy-start.14
  161.9 1.0 copy-done.2
  162.9 1.5 fusion.1
  164.4 0.0 copy-done.4
  164.4 0.0 copy-done.12
  164.4 0.0 copy-done.14
  164.4 16.5 %rev.7 = bf16[1024,512]{1,0:T(8,128)(2,1)} reverse(bf16[1024,512]{1,0:T(8,128)(2,1)} %get-tuple-element.42), dimensions={1} | reverse | bytes 2097152 | tf_op jit(solution)/shard_map/rev | solution.py:103
  180.9 16.3 %rev.6 = bf16[512,1024]{0,1:T(8,128)(2,1)} reverse(bf16[512,1024]{0,1:T(8,128)(2,1)} %get-tuple-element.43), dimensions={0} | reverse | bytes 2097152 | tf_op jit(solution)/shard_map/rev | solution.py:103
  197.3 3.7 %fusion.28 = f32[1024,512]{1,0:T(8,128)} fusion(bf16[1024,512]{1,0:T(8,128)(2,1)} %get-tuple-element.42, f32[512,512]{0,1:T(8,128)} %get-tuple-element.27), kind=kOutput, calls=%fused_computation.62 | convolution fusion | flops 537133056 | bytes 4194304 | tf_op jit(solution)/shard_map/dot_general | solution.py:30
  201.0 0.0 copy-done
  201.0 0.0 copy-done.11
  201.1 2.1 fusion.26
  203.1 2.1 fusion.9
  205.2 0.0 copy-done.19
  205.3 0.0 copy-start.3
  205.3 0.0 copy-start.5
  205.3 10.4 %multiply_reduce_fusion = (f32[512,512]{1,0:T(8,128)}, f32[512,512]{1,0:T(8,128)}, f32[512,512]{1,0:T(8,128)S(1)}) fusion(f32[512]{0:T(512)S(1)} %get-tuple-element.40, f32[16,512]{1,0:T(8,128)S(1)} %mul.307, f32[16,512]{1,0:T(8,128)S(1)} %get-tuple-element.32, f32[512]{0:T(512)S(1)} %get-tuple-element.41, f32[16,512]{1,0:T(8,128)S(1)} %get-tuple-element.17, ...), kind=kLoop, calls=%fused_computation | loop fusion | flops 36962304 | bytes 3280896 | tf_op jit(solution)/shard_map/reduce_sum | solution.py:104
  215.7 0.0 copy-done.3
  215.7 0.0 copy-done.5
  215.7 3.4 %fusion = f32[1024,512]{1,0:T(8,128)S(1)} fusion(f32[512,512]{1,0:T(8,128)S(1)} %get-tuple-element.14, f32[512,512]{1,0:T(8,128)S(1)} %copy-done.3, f32[512,512]{1,0:T(8,128)S(1)} %copy-done.5), kind=kOutput, calls=%fused_computation.9 | convolution fusion | flops 3221749760 | bytes 5242880 | tf_op jit(solution)/shard_map/dot_general | solution.py:91
  219.1 0.0 copy-start.7
  219.1 1.4 copy-done.7
  220.5 2.6 copy.35
  223.1 2.6 copy.36
  225.6 0.0 copy-start.20
  225.6 3.6 %subtract_convert_fusion.1 = (bf16[512,512]{1,0:T(8,128)(2,1)S(1)}, bf16[512,512]{1,0:T(8,128)(2,1)S(1)}, bf16[512,512]{1,0:T(8,128)(2,1)S(1)}, bf16[512,512]{1,0:T(8,128)(2,1)S(1)}) fusion(f32[1024,512]{1,0:T(8,128)} %fusion.28, f32[1024,512]{1,0:T(8,128)} %copy-done.7, pred[512]{0:T(512)(128)(4,1)S(1)} %iota_compare_fusion, f32[512]{0:T(512)S(1)} %bitcast.66, ...), kind=kLoop, calls=%fused_computation.48 | loop fusion | flops 4718592 | bytes 8391168 | tf_op jit(solution)/shard_map/convert.9
  229.2 0.0 copy-done.6
  229.2 0.1 copy-done.17
  229.3 0.0 copy-done.20
  229.4 0.0 copy-start.10
  229.4 0.8 fusion.3
  230.1 0.4 copy-done.1
  230.6 0.1 copy-done.8
  230.7 0.3 copy-done.9
  231.1 0.3 copy-done.10
  231.4 1.9 fusion.23
  233.2 0.2 pad_maximum_fusion.2
  233.4 20.5 %convolution_convert_fusion = bf16[512,8192]{1,0:T(8,128)(2,1)} fusion(bf16[512,1536]{0,1:T(8,128)(2,1)S(1)} %bitcast.63, bf16[8192,1536]{0,1:T(8,128)(2,1)} %all-gather.4.cloned.1.call-done), kind=kOutput, calls=%fused_computation.6 | convolution fusion | flops 12889096192 | bytes 35127296 | tf_op jit(solution)/shard_map/dot_general | solution.py:112
  254.0 0.0 reduce-scatter.2.cloned.1.call-update
  254.0 1.0 copy-done.16
  255.0 1.0 copy.37
  256.0 78.4 %reduce-scatter.2.cloned.1.call-done = bf16[512,2048]{1,0:T(8,128)(2,1)} async-done(((bf16[512,8192]{1,0:T(8,128)(2,1)}), bf16[512,2048]{1,0:T(8,128)(2,1)}) %reduce-scatter.2.cloned.1.call-update) | async-done | bytes 2097168 | tf_op jit(solution)/shard_map/reduce_scatter | solution.py:113
  (25 shorter events, 0.1 us)
Async XLA Ops:
  7.2 4.5 %copy-start.18 = (f32[16,512]{1,0:T(8,128)S(1)}, f32[16,512]{1,0:T(8,128)}, u32[]{:S(2)}) copy-start(f32[16,512]{1,0:T(8,128)} %param.9) | copy-start | bytes 98308
  7.2 108.6 %all-gather.4.cloned.1.call-start = ((), (), s32[]{:S(2)}) async-start(), calls=%async_computation.1 | async-start | bytes 25952256 | tf_op jit(solution)/shard_map/all_gather | solution.py:45
  9.5 193.6 %all-gather.6.cloned.1.call-start = ((), (), s32[]{:S(2)}) async-start(), calls=%async_computation.3 | async-start | bytes 2162688 | tf_op jit(solution)/shard_map/all_gather | solution.py:68
  153.5 180.9 %reduce-scatter.2.cloned.1.call-start = ((), (), s32[]{:S(2)}) async-start(), calls=%async_computation.2 | async-start | bytes 10485760 | tf_op jit(solution)/shard_map/reduce_scatter | solution.py:113
  157.5 6.9 %copy-start.4 = (f32[512,512]{1,0:T(8,128)}, f32[512,512]{1,0:T(8,128)S(1)}, u32[]{:S(2)}) copy-start(f32[512,512]{1,0:T(8,128)S(1)} %fusion.30) | copy-start | bytes 3145732
  161.9 1.0 copy-start.2
  161.9 2.5 copy-start.12
  161.9 2.5 copy-start.14
  197.3 3.8 %copy-start = (f32[512,512]{0,1:T(8,128)S(1)}, f32[512,512]{0,1:T(8,128)}, u32[]{:S(2)}) copy-start(f32[512,512]{0,1:T(8,128)} %get-tuple-element.26) | copy-start | bytes 3145732
  197.3 3.8 %copy-start.11 = (bf16[1024,512]{1,0:T(8,128)(2,1)S(1)}, bf16[1024,512]{1,0:T(8,128)(2,1)}, u32[]{:S(2)}) copy-start(bf16[1024,512]{1,0:T(8,128)(2,1)} %rev.7) | copy-start | bytes 3145732
  201.0 4.2 %copy-start.19 = (f32[16,512]{1,0:T(8,128)S(1)}, f32[16,512]{1,0:T(8,128)}, u32[]{:S(2)}) copy-start(f32[16,512]{1,0:T(8,128)} %param.8) | copy-start | bytes 98308
  205.3 10.4 %copy-start.3 = (f32[512,512]{1,0:T(8,128)S(1)}, f32[512,512]{1,0:T(8,128)}, u32[]{:S(2)}) copy-start(f32[512,512]{1,0:T(8,128)} %copy-done.2) | copy-start | bytes 3145732
  205.3 10.4 %copy-start.5 = (f32[512,512]{1,0:T(8,128)S(1)}, f32[512,512]{1,0:T(8,128)}, u32[]{:S(2)}) copy-start(f32[512,512]{1,0:T(8,128)} %copy-done.4) | copy-start | bytes 3145732
  219.1 1.4 copy-start.7
  225.6 3.6 %copy-start.6 = (f32[512,512]{0,1:T(8,128)S(1)}, f32[512,512]{0,1:T(8,128)}, u32[]{:S(2)}) copy-start(f32[512,512]{0,1:T(8,128)} %get-tuple-element.27) | copy-start | bytes 3145732
  225.6 3.6 %copy-start.13 = (bf16[512,512]{1,0:T(8,128)(2,1)S(1)}, bf16[512,512]{1,0:T(8,128)(2,1)}, u32[]{:S(2)}) copy-start(bf16[512,512]{1,0:T(8,128)(2,1)} %copy-done.12) | copy-start | bytes 1572868
  225.6 3.6 %copy-start.15 = (bf16[512,512]{1,0:T(8,128)(2,1)S(1)}, bf16[512,512]{1,0:T(8,128)(2,1)}, u32[]{:S(2)}) copy-start(bf16[512,512]{1,0:T(8,128)(2,1)} %copy-done.14) | copy-start | bytes 1572868
  225.6 3.7 %copy-start.17 = (f32[512,512]{0,1:T(8,128)S(1)}, f32[512,512]{0,1:T(8,128)}, u32[]{:S(2)}) copy-start(f32[512,512]{0,1:T(8,128)} %copy.35) | copy-start | bytes 3145732
  225.6 3.7 %copy-start.20 = (f32[512]{0:T(512)S(1)}, f32[512]{0:T(512)}, u32[]{:S(2)}) copy-start(f32[512]{0:T(512)} %param.10) | copy-start | bytes 6148
  229.4 1.2 copy-start.1
  229.4 1.4 copy-start.8
  229.4 1.7 copy-start.9
  229.4 2.0 copy-start.10
  254.0 1.0 copy-start.16
Sparse Core Ops, SparseCore 0:
  10.8 104.9 all-gather.3
  153.6 44.6 all-gather.5
  254.1 80.2 reduce-scatter.1
where the time goes:
time: 348 us; the launch traced here: 341 us
  waiting for transfers between devices  183 us (53%)
  local copies, waits for them, and re-layouts  54.9 us (16%)
  matrix products  52.6 us (15%)
  other arithmetic  36.5 us (10%)
  between operations  14 us (4%)
    all_gather x1, waiting for transfers between devices, local(): whole_w = lax.all_gather(flat_w, 'seq', axis=0, tiled=True)  104 us
    reduce_scatter x1, waiting for transfers between devices, local(): lax.psum_scatter(dx_terms.astype(bf16), 'chan', scatter_dimension=1, tile...  78.4 us
    dot_general x1, matrix products, local(): lax.dot_general(grad_proj, whole_w, contract, preferred_element_type=f32)  20.5 us
    dot_general x1, matrix products, local(): projected = jnp.dot(tokens, whole_w, preferred_element_type=f32)  20.1 us
    rev x1, local copies, waits for them, and re-layouts, local(): fwd_b[:, ::-1]  16.5 us
    rev x1, local copies, waits for them, and re-layouts, local(): inv_b[::-1, :]  16.3 us
    reduce_sum x1, other arithmetic, local(): jnp.sum(into_b[:, None, :] * jnp.exp(-rates[:, None, :] * (tok_rows - ste...  10.4 us
    unnamed x45, local copies, waits for them, and re-layouts  10.1 us
  transfers between devices with their start and end apart: 3, of which 2 were waited for; matrix products, arithmetic and copies ran while one was open for 15% of the time, Pallas kernels for 0%

commit v1 on v0

--- a/solution.py
+++ b/solution.py
@@ -9,10 +9,12 @@
 bf16 = jnp.bfloat16
 
 
-def dft_tables(block_len):
+def dft_tables(block_len, flip=False):
     n_len = 2 * block_len
     k = jnp.arange(block_len, dtype=jnp.int32)[:, None]
     n = jnp.arange(block_len, dtype=jnp.int32)[None, :]
+    if flip:
+        n = block_len - 1 - n
     phase = (k * n) % n_len
     angle = (2.0 * math.pi / n_len) * phase.astype(f32)
     cos_rows = jnp.cos(angle)
@@ -39,10 +41,14 @@
 def local(tokens, proj_weight, residues, decay_rates, skip_gain, grad_out):
     tok_rows = tokens.shape[0]
     chan_count = skip_gain.shape[0]
-    seq_count = lax.axis_size("seq")
-    me = lax.axis_index("seq")
+    seq_count = lax.axis_size(SEQ)
+    me = lax.axis_index(SEQ)
     flat_w = proj_weight.reshape(proj_weight.shape[0], 3 * chan_count)
-    whole_w = lax.all_gather(flat_w, "seq", axis=0, tiled=True)
+    half = 3 * chan_count // 2
+    pair_w = lax.all_gather(flat_w, "core", axis=0, tiled=True)
+    mine_w = lax.dynamic_slice_in_dim(pair_w, lax.axis_index("core") * half, half, axis=1)
+    plane_w = lax.all_gather(mine_w, "xy", axis=0, tiled=True)
+    whole_w = lax.all_gather(plane_w, "core", axis=1, tiled=True)
     projected = jnp.dot(tokens, whole_w, preferred_element_type=f32)
     proj_vals = (
         lax.optimization_barrier(projected.astype(bf16))
@@ -65,7 +71,7 @@
     end_fwd = jnp.sum(fwd_w * mixed_in[None], axis=1)
     end_bwd = jnp.sum(bwd_w * grad_mix[None], axis=1)
     states = jnp.stack([end_fwd, end_bwd])
-    every = lax.all_gather(states, "seq")
+    every = lax.all_gather(states, SEQ)
 
     others = jnp.arange(seq_count, dtype=jnp.int32)
     gap_f = me - 1 - others
@@ -88,6 +94,7 @@
     fwd, inv = dft_tables(tok_rows)
     fwd_b = fwd.astype(bf16)
     inv_b = inv.astype(bf16)
+    fwd_r, inv_r = dft_tables(tok_rows, flip=True)
     spec = jnp.dot(fwd, taps, precision=lax.Precision.HIGHEST)
     row0 = (jnp.arange(tok_rows) == 0)[:, None]
     h_a = spec[:tok_rows]
@@ -100,7 +107,7 @@
     gated_output = (query_in * filtered).astype(bf16)
     grad_query = grad_gate * filtered
 
-    local_b = spectral_conv(grad_mix, fwd_b[:, ::-1], inv_b[::-1, :], h_a, h_a2, h_b)
+    local_b = spectral_conv(grad_mix, fwd_r.astype(bf16), inv_r.astype(bf16), h_a, h_a2, h_b)
     carry_b = jnp.sum(
         into_b[:, None, :] * jnp.exp(-rates[:, None, :] * (tok_rows - steps)[None, :, None]), axis=0
     )
@@ -114,19 +121,27 @@
     return (gated_output, grad_tokens)
 
 
+SEQ = ("xy", "core")
+
+
 def solution(mesh):
+    cores = 2
+    split = jax.sharding.Mesh(
+        mesh.devices.reshape(mesh.shape["seq"] // cores, cores, mesh.shape["chan"]),
+        ("xy", "core", "chan"),
+    )
     placed = (
-        P("seq", None),
-        P("seq", None, "chan"),
+        P(SEQ, None),
+        P(SEQ, None, "chan"),
         P(None, "chan"),
         P(None, "chan"),
         P("chan"),
-        P("seq", "chan"),
+        P(SEQ, "chan"),
     )
     return jax.shard_map(
         local,
-        mesh=mesh,
+        mesh=split,
         in_specs=placed,
-        out_specs=(P("seq", "chan"), P("seq", "chan")),
+        out_specs=(P(SEQ, "chan"), P(SEQ, "chan")),
         check_vma=False,
     )

time: 348 us -> 391 us (1.12)
  waiting for transfers between devices: 183 us -> 258 us
  local copies, waits for them, and re-layouts: 54.9 us -> 21.6 us
  other arithmetic: 36.5 us -> 41.3 us
    all_gather x2 -> x4, waiting for transfers between devices: 104 us -> 182 us  [the longest x1 101 us: local(): plane_w = lax.all_gather(mine_w, 'xy', axis=0, tiled=True)]
    rev x2 -> x0, local copies, waits for them, and re-layouts: 32.8 us -> none  [the longest x1 16.5 us: local(): fwd_b[:, ::-1]]
    another operation x2 -> x3, other arithmetic: 7.89 us -> 14.4 us
  transfers between devices with their start and end apart: 3 -> 5, of which waited for: 2 -> 5; matrix products, arithmetic and copies ran while one was open for 15% -> 6% of each run, Pallas kernels for 0% -> 0%
where the time goes in v1:
time: 391 us; the launch traced here: 388 us
  waiting for transfers between devices  258 us (66%)
  matrix products  52.1 us (13%)
  other arithmetic  41.3 us (11%)
  local copies, waits for them, and re-layouts  21.6 us (6%)
  between operations  14.1 us (4%)
    all_gather x1, waiting for transfers between devices, local(): plane_w = lax.all_gather(mine_w, 'xy', axis=0, tiled=True)  101 us
    reduce_scatter x1, waiting for transfers between devices, local(): lax.psum_scatter(dx_terms.astype(bf16), 'chan', scatter_dimension=1, tile...  76.7 us
    all_gather x1, waiting for transfers between devices, local(): whole_w = lax.all_gather(plane_w, 'core', axis=1, tiled=True)  42.1 us
    all_gather x1, waiting for transfers between devices, local(): every = lax.all_gather(states, SEQ)  22.9 us
    dot_general x1, matrix products, local(): lax.dot_general(grad_proj, whole_w, contract, preferred_element_type=f32)  20.5 us
    dot_general x1, matrix products, local(): projected = jnp.dot(tokens, whole_w, preferred_element_type=f32)  19.4 us
    all_gather x1, waiting for transfers between devices, local(): pair_w = lax.all_gather(flat_w, 'core', axis=0, tiled=True)  15.2 us
    another operation x3, other arithmetic  14.4 us
  transfers between devices with their start and end apart: 5, of which 5 were waited for; matrix products, arithmetic and copies ran while one was open for 6% of the time, Pallas kernels for 0%

profile of v1, /device:TPU:32, one launch (start us, length us, event | category | flops | bytes accessed | tf_op | source)
XLA Modules:
  0.0 387.7 jit_solution(8192776830825825899)
XLA Ops:
  7.2 0.0 all-gather.6.cloned.1.call-start
  7.2 2.3 copy.24
  9.5 0.0 all-gather.6.cloned.1.call-update
  9.5 0.0 all-gather.8.cloned.1.call-start
  9.6 15.2 %all-gather.6.cloned.1.call-done = bf16[512,1536]{0,1:T(8,128)(2,1)} async-done(((bf16[256,1536]{0,1:T(8,128)(2,1)}), bf16[512,1536]{0,1:T(8,128)(2,1)}) %all-gather.6.cloned.1.call-update) | async-done | bytes 1572880 | tf_op jit(solution)/shard_map/all_gather | solution.py:48
  24.7 2.1 constant_dynamic-slice_fusion
  26.8 0.0 all-gather.8.cloned.1.call-update
  26.8 0.0 all-gather.10.cloned.1.call-start
  26.9 101.4 %all-gather.8.cloned.1.call-done = bf16[8192,768]{0,1:T(8,128)(2,1)} async-done(((bf16[512,768]{0,1:T(8,128)(2,1)}), bf16[8192,768]{0,1:T(8,128)(2,1)}) %all-gather.8.cloned.1.call-update) | async-done | bytes 12582928 | tf_op jit(solution)/shard_map/all_gather | solution.py:50
  128.2 0.0 all-gather.10.cloned.1.call-update
  128.3 0.0 all-gather.12.cloned.1.call-start
  128.3 1.0 copy-done.15
  129.3 1.0 copy.26
  130.3 0.0 copy-done.18
  130.3 42.1 %all-gather.10.cloned.1.call-done = bf16[8192,1536]{0,1:T(8,128)(2,1)} async-done(((bf16[8192,768]{0,1:T(8,128)(2,1)}), bf16[8192,1536]{0,1:T(8,128)(2,1)}) %all-gather.10.cloned.1.call-update) | async-done | bytes 25165840 | tf_op jit(solution)/shard_map/all_gather | solution.py:51
  172.4 19.4 %fusion = bf16[512,1536]{0,1:T(8,128)(2,1)S(1)} fusion(bf16[8192,1536]{0,1:T(8,128)(2,1)} %all-gather.10.cloned.1.call-done, bf16[512,8192]{1,0:T(8,128)(2,1)} %param.6), kind=kOutput, calls=%fused_computation.8 | convolution fusion | flops 12885688320 | bytes 35127296 | tf_op jit(solution)/shard_map/dot_general | solution.py:52
  191.8 0.0 copy-start.8
  191.8 0.4 convert.56
  192.2 0.6 copy-done.8
  192.8 1.8 convert_multiply_fusion.1
  194.6 2.6 copy.27
  197.2 2.5 copy.25
  199.7 7.2 %multiply_reduce_fusion.3 = (f32[16,512]{1,0:T(8,128)S(1)}, f32[16,512]{1,0:T(8,128)S(1)}) fusion(f32[512,512]{1,0:T(8,128)} %copy.25, f32[512]{0:T(512)S(1)} %iota_subtract_fusion.2, f32[16,512]{1,0:T(8,128)S(1)} %get-tuple-element.32, f32[512,512]{1,0:T(8,128)} %copy.27), kind=kLoop, calls=%fused_computation.3 | loop fusion | flops 25149440 | bytes 2197504 | tf_op jit(solution)/shard_map/reduce_sum | solution.py:71
  206.9 0.6 pad_maximum_fusion.3
  207.5 0.0 all-gather.12.cloned.1.call-update
  207.6 0.2 reduce-scatter.2.cloned.1.call-start
  207.9 3.8 fusion.48
  211.7 0.0 copy-start.2
  211.7 0.0 copy-start
  211.7 4.1 %fusion.41 = bf16[512,512]{1,0:T(8,128)(2,1)S(1)} fusion(f32[512]{0:T(512)S(1)} %fusion.57, s32[512]{0:T(512)S(1)} %iota_subtract_fusion.1, pred[512]{0:T(512)(128)(4,1)S(1)} %iota_compare_fusion), kind=kLoop, calls=%fused_computation.79 | loop fusion | flops 3932160 | bytes 528896 | tf_op jit(solution)/shard_map/convert.10
  215.8 9.7 %multiply_convert_fusion.3 = (bf16[512,512]{1,0:T(8,128)(2,1)}, bf16[512,512]{1,0:T(8,128)(2,1)}, bf16[512,512]{1,0:T(8,128)(2,1)}, f32[512,512]{1,0:T(8,128)S(1...) fusion(f32[512]{0:T(512)S(1)} %get-tuple-element.41, s32[512]{0:T(512)S(1)} %iota_subtract_fusion.1, ...), kind=kLoop, calls=%fused_computation.65 | loop fusion | flops 10223616 | bytes 3678720 | tf_op jit(solution)/shard_map/convert.11
  225.6 0.0 copy-done.2
  225.6 0.0 copy-done
  225.6 0.0 copy-start.4
  225.6 2.1 fusion.12
  227.7 0.0 copy-done.3
  227.7 0.0 copy-done.4
  227.7 2.1 fusion.27
  229.8 22.9 %all-gather.12.cloned.1.call-done = f32[64,16,512]{2,1,0:T(8,128)} async-done(((f32[2,16,512]{2,1,0:T(8,128)}), f32[64,16,512]{2,1,0:T(8,128)}) %all-gather.12.cloned.1.call-update) | async-done | bytes 2097168 | tf_op jit(solution)/shard_map/all_gather | solution.py:74
  252.7 2.1 fusion.15
  254.8 0.0 copy-done.19
  254.8 10.7 %multiply_reduce_fusion = (f32[512,512]{1,0:T(8,128)}, f32[512,512]{1,0:T(8,128)}, f32[512,512]{1,0:T(8,128)}) fusion(f32[512]{0:T(512)S(1)} %get-tuple-element.39, f32[16,512]{1,0:T(8,128)S(1)} %mul.373, f32[16,512]{1,0:T(8,128)S(1)} %get-tuple-element.32, f32[512]{0:T(512)S(1)} %get-tuple-element.40, f32[16,512]{1,0:T(8,128)S(1)} %get-tuple-element.17, ...), kind=kLoop, calls=%fused_computation | loop fusion | flops 36962304 | bytes 3280896 | tf_op jit(solution)/shard_map/reduce_sum | solution.py:111
  265.5 2.6 copy.30
  268.1 2.5 copy.29
  270.6 5.4 %fusion.1 = f32[1024,512]{1,0:T(8,128)S(1)} fusion(f32[512,512]{1,0:T(8,128)} %get-tuple-element.14, f32[512,512]{1,0:T(8,128)} %copy-done.3, f32[512,512]{1,0:T(8,128)} %copy-done.2), kind=kOutput, calls=%fused_computation.10 | convolution fusion | flops 3221749760 | bytes 5242880 | tf_op jit(solution)/shard_map/dot_general | solution.py:98
  276.1 0.0 copy-start.20
  276.1 0.6 subtract_convert_fusion.1
  276.8 0.6 copy-done.5
  277.3 0.3 copy-done.14
  277.6 0.1 copy-done.16
  277.8 0.2 copy-done.17
  277.9 0.8 fusion.3
  278.7 0.4 copy-done.1
  279.1 0.1 copy-done.9
  279.3 0.3 copy-done.10
  279.6 0.1 copy-done.12
  279.8 0.2 copy-done.13
  279.9 1.8 fusion.42
  281.7 0.2 pad_maximum_fusion.2
  281.9 20.5 %convolution_convert_fusion = bf16[512,8192]{1,0:T(8,128)(2,1)} fusion(bf16[512,1536]{0,1:T(8,128)(2,1)S(1)} %bitcast.59, bf16[8192,1536]{0,1:T(8,128)(2,1)} %all-gather.10.cloned.1.call-done), kind=kOutput, calls=%fused_computation.6 | convolution fusion | flops 12889096192 | bytes 35127296 | tf_op jit(solution)/shard_map/dot_general | solution.py:119
  302.4 0.0 reduce-scatter.2.cloned.1.call-update
  302.4 1.0 copy-done.11
  303.4 1.0 copy.31
  304.4 76.7 %reduce-scatter.2.cloned.1.call-done = bf16[512,2048]{1,0:T(8,128)(2,1)} async-done(((bf16[512,8192]{1,0:T(8,128)(2,1)}), bf16[512,2048]{1,0:T(8,128)(2,1)}) %reduce-scatter.2.cloned.1.call-update) | async-done | bytes 2097168 | tf_op jit(solution)/shard_map/reduce_scatter | solution.py:120
  (33 shorter events, 0.2 us)
Async XLA Ops:
  7.2 17.6 %all-gather.6.cloned.1.call-start = ((), (), s32[]{:S(2)}) async-start(), calls=%async_computation.1 | async-start | bytes 2359296 | tf_op jit(solution)/shard_map/all_gather | solution.py:48
  9.5 118.7 %all-gather.8.cloned.1.call-start = ((), (), s32[]{:S(2)}) async-start(), calls=%async_computation.2 | async-start | bytes 13369344 | tf_op jit(solution)/shard_map/all_gather | solution.py:50
  26.8 145.6 %all-gather.10.cloned.1.call-start = ((), (), s32[]{:S(2)}) async-start(), calls=%async_computation.3 | async-start | bytes 37748736 | tf_op jit(solution)/shard_map/all_gather | solution.py:51
  128.2 1.0 copy-start.15
  128.2 2.1 copy-start.18
  128.3 124.4 %all-gather.12.cloned.1.call-start = ((), (), s32[]{:S(2)}) async-start(), calls=%async_computation.5 | async-start | bytes 2162688 | tf_op jit(solution)/shard_map/all_gather | solution.py:74
  191.8 1.0 copy-start.8
  207.6 173.6 %reduce-scatter.2.cloned.1.call-start = ((), (), s32[]{:S(2)}) async-start(), calls=%async_computation.4 | async-start | bytes 10485760 | tf_op jit(solution)/shard_map/reduce_scatter | solution.py:120
  211.7 13.9 %copy-start.2 = (f32[512,512]{1,0:T(8,128)}, f32[512,512]{1,0:T(8,128)S(1)}, u32[]{:S(2)}) copy-start(f32[512,512]{1,0:T(8,128)S(1)} %fusion.48) | copy-start | bytes 3145732
  211.7 13.9 %copy-start = (f32[512,512]{0,1:T(8,128)S(1)}, f32[512,512]{0,1:T(8,128)}, u32[]{:S(2)}) copy-start(f32[512,512]{0,1:T(8,128)} %get-tuple-element.27) | copy-start | bytes 3145732
  225.6 2.1 copy-start.3
  225.6 2.1 copy-start.4
  229.8 24.9 %copy-start.19 = (f32[16,512]{1,0:T(8,128)S(1)}, f32[16,512]{1,0:T(8,128)}, u32[]{:S(2)}) copy-start(f32[16,512]{1,0:T(8,128)} %param.8) | copy-start | bytes 98308
  270.6 5.5 %copy-start.6 = (f32[1024,512]{1,0:T(8,128)S(1)}, f32[1024,512]{1,0:T(8,128)}, u32[]{:S(2)}) copy-start(f32[1024,512]{1,0:T(8,128)} %fusion.12) | copy-start | bytes 6291460
  270.6 5.5 %copy-start.7 = (f32[1024,512]{1,0:T(8,128)S(1)}, f32[1024,512]{1,0:T(8,128)}, u32[]{:S(2)}) copy-start(f32[1024,512]{1,0:T(8,128)} %fusion.27) | copy-start | bytes 6291460
  276.1 1.2 copy-start.5
  276.1 1.5 copy-start.14
  276.1 1.7 copy-start.16
  276.1 1.8 copy-start.17
  276.1 1.8 copy-start.20
  277.9 1.2 copy-start.1
  277.9 1.4 copy-start.9
  277.9 1.7 copy-start.10
  277.9 1.8 copy-start.12
  277.9 2.0 copy-start.13
  302.4 1.0 copy-start.11
Sparse Core Ops, SparseCore 0:
  10.2 14.4 all-gather.5
  27.4 100.7 all-gather.7
  129.9 42.4 all-gather.9
  207.7 44.9 all-gather.11
  302.5 78.5 reduce-scatter.1

commit v2 on v1

--- a/solution.py
+++ b/solution.py
@@ -38,17 +38,20 @@
     return jnp.dot(inv, prod, preferred_element_type=f32)
 
 
+def mode_sum(amp, rates, lag):
+    total = amp[0] * jnp.exp(-rates[0] * lag)
+    for r in range(1, rates.shape[0]):
+        total = total + amp[r] * jnp.exp(-rates[r] * lag)
+    return total
+
+
 def local(tokens, proj_weight, residues, decay_rates, skip_gain, grad_out):
     tok_rows = tokens.shape[0]
     chan_count = skip_gain.shape[0]
     seq_count = lax.axis_size(SEQ)
     me = lax.axis_index(SEQ)
     flat_w = proj_weight.reshape(proj_weight.shape[0], 3 * chan_count)
-    half = 3 * chan_count // 2
-    pair_w = lax.all_gather(flat_w, "core", axis=0, tiled=True)
-    mine_w = lax.dynamic_slice_in_dim(pair_w, lax.axis_index("core") * half, half, axis=1)
-    plane_w = lax.all_gather(mine_w, "xy", axis=0, tiled=True)
-    whole_w = lax.all_gather(plane_w, "core", axis=1, tiled=True)
+    whole_w = lax.all_gather(flat_w, SEQ, axis=0, tiled=True)
     projected = jnp.dot(tokens, whole_w, preferred_element_type=f32)
     proj_vals = (
         lax.optimization_barrier(projected.astype(bf16))
@@ -63,13 +66,17 @@
     grad_mix = grad_gate * query_in
 
     rates = decay_rates
+    modes = rates.shape[0]
     mode_gain = residues * jnp.sqrt(-jnp.expm1(-2.0 * rates))
     steps = jnp.arange(tok_rows, dtype=f32)
 
-    fwd_w = jnp.exp(-rates[:, None, :] * (tok_rows - 1 - steps)[None, :, None])
-    bwd_w = jnp.exp(-rates[:, None, :] * steps[None, :, None])
-    end_fwd = jnp.sum(fwd_w * mixed_in[None], axis=1)
-    end_bwd = jnp.sum(bwd_w * grad_mix[None], axis=1)
+    col = steps[:, None]
+    end_fwd = jnp.stack(
+        [jnp.sum(jnp.exp(-rates[r] * (tok_rows - 1 - col)) * mixed_in, axis=0) for r in range(modes)]
+    )
+    end_bwd = jnp.stack(
+        [jnp.sum(jnp.exp(-rates[r] * col) * grad_mix, axis=0) for r in range(modes)]
+    )
     states = jnp.stack([end_fwd, end_bwd])
     every = lax.all_gather(states, SEQ)
 
@@ -90,7 +97,7 @@
     into_f = jnp.sum(w_f * every[:, 0], axis=0) * mode_gain
     into_b = jnp.sum(w_b * every[:, 1], axis=0) * mode_gain
 
-    taps = jnp.sum(mode_gain[:, None, :] * bwd_w, axis=0)
+    taps = mode_sum(mode_gain, rates, col)
     fwd, inv = dft_tables(tok_rows)
     fwd_b = fwd.astype(bf16)
     inv_b = inv.astype(bf16)
@@ -102,15 +109,13 @@
     h_b = jnp.where(row0, 0.0, spec[tok_rows:])
 
     local_f = spectral_conv(mixed_in, fwd_b, inv_b, h_a, h_a2, h_b)
-    carry_f = jnp.sum(into_f[:, None, :] * jnp.exp(-rates[:, None, :] * (steps + 1.0)[None, :, None]), axis=0)
+    carry_f = mode_sum(into_f, rates, col + 1.0)
     filtered = local_f + carry_f + skip_gain[None, :] * mixed_in
     gated_output = (query_in * filtered).astype(bf16)
     grad_query = grad_gate * filtered
 
     local_b = spectral_conv(grad_mix, fwd_r.astype(bf16), inv_r.astype(bf16), h_a, h_a2, h_b)
-    carry_b = jnp.sum(
-        into_b[:, None, :] * jnp.exp(-rates[:, None, :] * (tok_rows - steps)[None, :, None]), axis=0
-    )
+    carry_b = mode_sum(into_b, rates, tok_rows - col)
     grad_conv = local_b + carry_b + skip_gain[None, :] * grad_mix
 
     grad_proj = jnp.stack([grad_query, grad_conv * value_in, grad_conv * key_in], axis=1).astype(bf16)

time: 391 us -> 321 us (0.82)
  waiting for transfers between devices: 258 us -> 206 us
  local copies, waits for them, and re-layouts: 21.6 us -> 8.01 us
  other arithmetic: 41.3 us -> 30.5 us
  matrix products: 52.1 us -> 59 us
    all_gather x3 -> x1, waiting for transfers between devices: 159 us -> 105 us  [local(): whole_w = lax.all_gather(flat_w, SEQ, axis=0, tiled=True)]
    reduce_sum x2 -> x1, other arithmetic: 17.9 us -> 9.15 us  [local(): jnp.sum(jnp.exp(-rates[r] * col) * grad_mix, axis=0)]
    dot_general x2, matrix products: 2.53 us -> 8.88 us  [spectral_conv(): return jnp.dot(inv, prod, preferred_element_type=f32)]
    mul x2 -> x0, local copies, waits for them, and re-layouts: 5.14 us -> none  [the longest x1 2.61 us: local(): grad_mix = grad_gate * query_in]
    reduce_sum x2 -> x0, local copies, waits for them, and re-layouts: 5.09 us -> none  [the longest x1 2.55 us: local(): jnp.sum(into_b[:, None, :] * jnp.exp(-rates[:, None, :] * (tok_rows - ste...]
    unnamed x45 -> x37, local copies, waits for them, and re-layouts: 9.29 us -> 6.04 us
  transfers between devices with their start and end apart: 5 -> 3, of which waited for: 5 -> 3; matrix products, arithmetic and copies ran while one was open for 6% -> 7% of each run, Pallas kernels for 0% -> 0%
where the time goes in v2:
time: 321 us; the launch traced here: 318 us
  waiting for transfers between devices  206 us (64%)
  matrix products  59 us (18%)
  other arithmetic  30.5 us (10%)
  between operations  14.1 us (4%)
  local copies, waits for them, and re-layouts  8.01 us (2%)
    all_gather x1, waiting for transfers between devices, local(): whole_w = lax.all_gather(flat_w, SEQ, axis=0, tiled=True)  105 us
    reduce_scatter x1, waiting for transfers between devices, local(): lax.psum_scatter(dx_terms.astype(bf16), 'chan', scatter_dimension=1, tile...  77.7 us
    all_gather x1, waiting for transfers between devices, local(): every = lax.all_gather(states, SEQ)  23.1 us
    dot_general x1, matrix products, local(): lax.dot_general(grad_proj, whole_w, contract, preferred_element_type=f32)  20.3 us
    dot_general x1, matrix products, local(): projected = jnp.dot(tokens, whole_w, preferred_element_type=f32)  20.1 us
    another operation x3, other arithmetic  14.5 us
    reduce_sum x1, other arithmetic, local(): jnp.sum(jnp.exp(-rates[r] * col) * grad_mix, axis=0)  9.15 us
    dot_general x2, matrix products, spectral_conv(): return jnp.dot(inv, prod, preferred_element_type=f32)  8.88 us
  transfers between devices with their start and end apart: 3, of which 3 were waited for; matrix products, arithmetic and copies ran while one was open for 7% of the time, Pallas kernels for 0%

profile of v2, /device:TPU:32, one launch (start us, length us, event | category | flops | bytes accessed | tf_op | source)
XLA Modules:
  0.0 318.0 jit_solution(13994923010235042850)
XLA Ops:
  7.2 0.0 copy-start.8
  7.2 0.0 copy-start.14
  7.2 0.0 all-gather.4.cloned.1.call-start
  7.2 2.3 copy.18
  9.6 0.0 all-gather.4.cloned.1.call-update
  9.6 0.0 all-gather.6.cloned.1.call-start
  9.6 0.0 copy-done.8
  9.6 1.0 copy.20
  10.7 0.0 copy-done.14
  10.7 105.1 %all-gather.4.cloned.1.call-done = bf16[8192,1536]{0,1:T(8,128)(2,1)} async-done(((bf16[256,1536]{0,1:T(8,128)(2,1)}), bf16[8192,1536]{0,1:T(8,128)(2,1)}) %all-gather.4.cloned.1.call-update) | async-done | bytes 25165840 | tf_op jit(solution)/shard_map/all_gather | solution.py:54
  115.8 20.1 %convolution_convert_fusion.1 = bf16[512,1536]{1,0:T(8,128)(2,1)} fusion(bf16[512,8192]{1,0:T(8,128)(2,1)} %param.6, bf16[8192,1536]{0,1:T(8,128)(2,1)} %all-gather.4.cloned.1.call-done), kind=kOutput, calls=%fused_computation.1 | convolution fusion | flops 12885688320 | bytes 35127296 | tf_op jit(solution)/shard_map/dot_general | solution.py:55
  136.0 1.7 copy.19
  137.7 0.0 copy-start.3
  137.7 9.1 %multiply_reduce_fusion = (f32[512]{0:T(512)S(1)}, f32[512]{0:T(512)S(1)}, f32[512]{0:T(512)S(1)}, f32[512]{0:T(512)S(1)}, f32[512]{0:T(512)S(1)}, /*index=5*/f3...) fusion(f32[512]{0:T(512)S(1)} %bitcast.220, ...), kind=kLoop, calls=%fused_computation.62 | loop fusion | flops 25935872 | bytes 5867520 | tf_op jit(solution)/shard_map/reduce_sum | solution.py:78
  146.9 0.0 copy-done.3
  146.9 0.1 stack.143
  146.9 0.1 stack.161
  147.0 0.6 pad_maximum_fusion.3
  147.6 0.0 all-gather.6.cloned.1.call-update
  147.7 0.2 reduce-scatter.2.cloned.1.call-start
  148.0 3.8 %fusion.110 = f32[512,512]{1,0:T(8,128)S(1)} fusion(), kind=kLoop, calls=%fused_computation.190 | loop fusion | flops 3670016 | bytes 1048576 | tf_op jit(solution)/shard_map/cos | solution.py:20
  151.8 0.0 copy-start.4
  151.8 4.1 %fusion.71 = bf16[512,512]{1,0:T(8,128)(2,1)S(1)} fusion(f32[512]{0:T(512)S(1)} %fusion.119, s32[512]{0:T(512)S(1)} %iota_subtract_fusion.1, pred[512]{0:T(512)(128)(4,1)S(1)} %iota_compare_fusion), kind=kLoop, calls=%fused_computation.151 | loop fusion | flops 3932160 | bytes 528896 | tf_op jit(solution)/shard_map/convert.10
  155.9 9.7 %multiply_convert_fusion.3 = (bf16[512,512]{1,0:T(8,128)(2,1)}, bf16[512,512]{1,0:T(8,128)(2,1)}, bf16[512,512]{1,0:T(8,128)(2,1)}, f32[512,512]{1,0:T(8,128)S(1...) fusion(f32[512]{0:T(512)S(1)} %get-tuple-element.142, s32[512]{0:T(512)S(1)} %iota_subtract_fusion.1, ...), kind=kLoop, calls=%fused_computation.58 | loop fusion | flops 10223616 | bytes 3678720 | tf_op jit(solution)/shard_map/convert.11
  165.7 0.0 copy-start.1
  165.7 0.0 copy-done.4
  165.7 0.0 copy-start.6
  165.7 0.7 fusion.11
  166.4 0.2 copy-done.1
  166.7 0.6 copy-done.6
  167.3 2.1 fusion.26
  169.3 0.0 copy-start.15
  169.3 23.1 %all-gather.6.cloned.1.call-done = f32[64,16,512]{2,1,0:T(8,128)} async-done(((f32[2,16,512]{2,1,0:T(8,128)}), f32[64,16,512]{2,1,0:T(8,128)}) %all-gather.6.cloned.1.call-update) | async-done | bytes 2097168 | tf_op jit(solution)/shard_map/all_gather | solution.py:81
  192.4 0.0 copy-start.2
  192.4 2.1 fusion.14
  194.6 0.0 copy-done.15
  194.7 0.0 copy-done.2
  194.7 0.0 copy-start
  194.8 6.9 %fusion = f32[1024,512]{1,0:T(8,128)S(1)} fusion(f32[512,512]{1,0:T(8,128)S(1)} %copy-done.2, f32[512,512]{1,0:T(8,128)S(1)} %fusion.110, f32[512]{0:T(512)S(1)} %bitcast.221, f32[512]{0:T(512)S(1)} %bitcast.241, f32[512]{0:T(512)S(1)} %bitcast.165, f32[512]{0:T(512)S(1)} %bitcast.242, f32[512]{0:T(512)S(1)} %bitcast.169, f32[512]{0:T(512)S(1)} %bitcast.243, ...), kind=kOutput, calls=%fused_computation.3 | convolution fusion | flops 3234070528 | bytes 4259840 | tf_op jit(solution)/shard_map/dot_general | solution.py:105
  201.7 0.0 copy-done
  201.8 0.0 copy-start.7
  201.8 0.0 copy-start.12
  201.8 0.0 copy-start.13
  201.8 0.0 copy-start.16
  201.8 0.7 subtract_convert_fusion.1
  202.5 0.5 copy-done.7
  203.0 0.1 copy-done.12
  203.1 0.2 copy-done.13
  203.3 0.0 copy-done.16
  203.3 0.0 copy-start.5
  203.3 0.0 copy-start.9
  203.3 0.0 copy-start.10
  203.3 0.0 copy-start.11
  203.3 3.6 %fusion.2 = f32[512,512]{0,1:T(8,128)S(1)} fusion(bf16[512,512]{1,0:T(8,128)(2,1)S(1)} %copy-done.13, bf16[512,512]{1,0:T(8,128)(2,1)S(1)} %copy-done.12, bf16[512,512]{1,0:T(8,128)(2,1)S(1)} %get-tuple-element.69, bf16[512,512]{1,0:T(8,128)(2,1)S(1)} %get-tuple-element.70, f32[512,512]{0,1:T(8,128)S(1)} %copy-done.7, f32[512]{0:T(512)S(1)} %bitcast.289, ...), kind=kOutput, calls=%fused_computation.13 | convolution fusion | flops 554172416 | bytes 4263936 | tf_op jit(solution)/shard_map/dot_general | solution.py:38
  206.9 0.0 copy-done.5
  206.9 0.0 copy-done.9
  206.9 0.0 copy-done.10
  206.9 0.0 copy-done.11
  206.9 5.3 %fusion.72 = (bf16[512,1,512]{0,2,1:T(8,128)(2,1)S(1)}, bf16[512,1,512]{0,2,1:T(8,128)(2,1)S(1)}, bf16[512,512]{0,1:T(8,128)(2,1)S(1)}, bf16[512,1,512]{0,2,1:T(8,128)(2,1)S(1)}) fusion(f32[512,512]{0,1:T(8,128)S(1)} %fusion.2, f32[512,3,512]{0,2,1:T(8,128)} %bitcast.153, bf16[512,512]{0,1:T(8,128)(2,1)S(1)} %copy-done.9, f32[512,512]{0,1:T(8,128)S(1)} %copy-done.5, ...), kind=kOutput, calls=%fused_computation.152 | convolution fusion | flops 556531712 | bytes 10031104 | tf_op jit(solution)/shard_map/dot_general | solution.py:38
  212.2 0.2 pad_maximum_fusion.2
  212.4 20.3 %convolution_convert_fusion = bf16[512,8192]{1,0:T(8,128)(2,1)} fusion(bf16[512,1536]{0,1:T(8,128)(2,1)S(1)} %bitcast.156, bf16[8192,1536]{0,1:T(8,128)(2,1)} %all-gather.4.cloned.1.call-done), kind=kOutput, calls=%fused_computation | convolution fusion | flops 12889096192 | bytes 35127296 | tf_op jit(solution)/shard_map/dot_general | solution.py:124
  232.7 0.0 reduce-scatter.2.cloned.1.call-update
  232.7 1.0 copy.22
  233.7 77.7 %reduce-scatter.2.cloned.1.call-done = bf16[512,2048]{1,0:T(8,128)(2,1)} async-done(((bf16[512,8192]{1,0:T(8,128)(2,1)}), bf16[512,2048]{1,0:T(8,128)(2,1)}) %reduce-scatter.2.cloned.1.call-update) | async-done | bytes 2097168 | tf_op jit(solution)/shard_map/reduce_scatter | solution.py:125
  (17 shorter events, 0.2 us)
Async XLA Ops:
  7.2 2.5 copy-start.8
  7.2 3.5 %copy-start.14 = (f32[16,512]{1,0:T(8,128)S(1)}, f32[16,512]{1,0:T(8,128)}, u32[]{:S(2)}) copy-start(f32[16,512]{1,0:T(8,128)} %param.9) | copy-start | bytes 98308
  7.2 108.6 %all-gather.4.cloned.1.call-start = ((), (), s32[]{:S(2)}) async-start(), calls=%async_computation.1 | async-start | bytes 25952256 | tf_op jit(solution)/shard_map/all_gather | solution.py:54
  9.6 182.9 %all-gather.6.cloned.1.call-start = ((), (), s32[]{:S(2)}) async-start(), calls=%async_computation.3 | async-start | bytes 2162688 | tf_op jit(solution)/shard_map/all_gather | solution.py:81
  137.7 9.2 %copy-start.3 = (f32[512,1536]{0,1:T(8,128)}, f32[512,1536]{0,1:T(8,128)S(1)}, u32[]{:S(2)}) copy-start(f32[512,1536]{0,1:T(8,128)S(1)} %copy.19) | copy-start | bytes 9437188
  147.7 163.8 %reduce-scatter.2.cloned.1.call-start = ((), (), s32[]{:S(2)}) async-start(), calls=%async_computation.2 | async-start | bytes 10485760 | tf_op jit(solution)/shard_map/reduce_scatter | solution.py:125
  151.8 13.9 %copy-start.4 = (f32[512,512]{0,1:T(8,128)S(1)}, f32[512,512]{0,1:T(8,128)}, u32[]{:S(2)}) copy-start(f32[512,512]{0,1:T(8,128)} %get-tuple-element.61) | copy-start | bytes 3145732
  165.7 1.0 copy-start.1
  165.7 1.6 copy-start.6
  169.3 25.3 %copy-start.15 = (f32[16,512]{1,0:T(8,128)S(1)}, f32[16,512]{1,0:T(8,128)}, u32[]{:S(2)}) copy-start(f32[16,512]{1,0:T(8,128)} %param.8) | copy-start | bytes 98308
  192.4 2.3 copy-start.2
  194.7 7.0 %copy-start = (f32[1024,512]{1,0:T(8,128)S(1)}, f32[1024,512]{1,0:T(8,128)}, u32[]{:S(2)}) copy-start(f32[1024,512]{1,0:T(8,128)} %fusion.26) | copy-start | bytes 6291460
  201.8 1.2 copy-start.7
  201.8 1.3 copy-start.12
  201.8 1.5 copy-start.13
  201.8 1.5 copy-start.16
  203.3 3.6 %copy-start.5 = (f32[512,512]{0,1:T(8,128)S(1)}, f32[512,512]{0,1:T(8,128)}, u32[]{:S(2)}) copy-start(f32[512,512]{0,1:T(8,128)} %get-tuple-element.61) | copy-start | bytes 3145732
  203.3 3.6 %copy-start.9 = (bf16[512,512]{0,1:T(8,128)(2,1)S(1)}, bf16[512,512]{0,1:T(8,128)(2,1)}, u32[]{:S(2)}) copy-start(bf16[512,512]{0,1:T(8,128)(2,1)} %copy.20) | copy-start | bytes 1572868
  203.3 3.6 %copy-start.10 = (bf16[512,512]{1,0:T(8,128)(2,1)S(1)}, bf16[512,512]{1,0:T(8,128)(2,1)}, u32[]{:S(2)}) copy-start(bf16[512,512]{1,0:T(8,128)(2,1)} %get-tuple-element.138) | copy-start | bytes 1572868
  203.3 3.6 %copy-start.11 = (bf16[512,512]{1,0:T(8,128)(2,1)S(1)}, bf16[512,512]{1,0:T(8,128)(2,1)}, u32[]{:S(2)}) copy-start(bf16[512,512]{1,0:T(8,128)(2,1)} %get-tuple-element.141) | copy-start | bytes 1572868
Sparse Core Ops, SparseCore 0:
  10.8 104.9 all-gather.3
  147.8 44.6 all-gather.5
  232.8 78.5 reduce-scatter.1

commit v3 on v2

--- a/solution.py
+++ b/solution.py
@@ -1,9 +1,14 @@
+import functools
 import math
 
 import jax
 import jax.numpy as jnp
 from jax import lax
+from jax.experimental import pallas as pl
+from jax.experimental.pallas import tpu as pltpu
 from jax.sharding import PartitionSpec as P
+
+MESH = pl.DeviceIdType.MESH
 
 f32 = jnp.float32
 bf16 = jnp.bfloat16
@@ -38,6 +43,99 @@
     return jnp.dot(inv, prod, preferred_element_type=f32)
 
 
+def ring_kernel(n, gp_ref, w_hbm, out_ref, wbuf, acc, snd, rcv, wsem, send_sem, recv_sem):
+    me = lax.axis_index("chan")
+    right = lax.rem(me + 1, n)
+    left = lax.rem(me + n - 1, n)
+    half = out_ref.shape[1] // 2
+    block = 2 * half
+    tile = min(256, half)
+
+    barrier = pltpu.get_barrier_semaphore()
+    for neighbour in (left, right):
+        pl.semaphore_signal(barrier, inc=1, device_id={"chan": neighbour}, device_id_type=MESH)
+    pl.semaphore_wait(barrier, 2)
+
+    def load(d, dest):
+        first = pl.multiple_of(dest * block + d * half, 8)
+        cp = pltpu.make_async_copy(w_hbm.at[pl.ds(first, half)], wbuf.at[d], wsem.at[d])
+        cp.start()
+        return cp
+
+    def product(d):
+        def body(j, carry):
+            rows = pl.ds(pl.multiple_of(j * tile, tile), tile)
+            acc[d, :, rows] = lax.dot_general(
+                gp_ref[...], wbuf[d, rows, :], (((1,), (1,)), ((), ())),
+                preferred_element_type=jnp.float32,
+            )
+            return carry
+
+        lax.fori_loop(0, half // tile, body, 0)
+
+    targets = (right, left)
+    copies = [None, None]
+    for step in range(n - 1):
+        dests = (lax.rem(me + 2 * n - 1 - step, n), lax.rem(me + 1 + step, n))
+        loads = [load(d, dests[d]) for d in (0, 1)]
+        for d in (0, 1):
+            loads[d].wait()
+            product(d)
+            if copies[d] is not None:
+                copies[d].wait_recv()
+                copies[d].wait_send()
+                snd[d] = (acc[d] + rcv[d, step - 1].astype(jnp.float32)).astype(snd.dtype)
+            else:
+                snd[d] = acc[d].astype(snd.dtype)
+            copies[d] = pltpu.make_async_remote_copy(
+                src_ref=snd.at[d],
+                dst_ref=rcv.at[d, step],
+                send_sem=send_sem.at[d],
+                recv_sem=recv_sem.at[d, step],
+                device_id={"chan": targets[d]},
+                device_id_type=MESH,
+            )
+            copies[d].start()
+    loads = [load(d, me) for d in (0, 1)]
+    for d in (0, 1):
+        loads[d].wait()
+        product(d)
+        copies[d].wait_recv()
+        copies[d].wait_send()
+        out_ref[:, pl.ds(d * half, half)] = (
+            acc[d] + rcv[d, n - 2].astype(jnp.float32)
+        ).astype(out_ref.dtype)
+
+
+def ring_reduce(grad_proj, whole_w, n):
+    rows, width = grad_proj.shape
+    block = whole_w.shape[0] // n
+    half = block // 2
+    return pl.pallas_call(
+        functools.partial(ring_kernel, n),
+        out_shape=jax.ShapeDtypeStruct((rows, block), jnp.bfloat16),
+        in_specs=[pl.BlockSpec(memory_space=pltpu.VMEM), pl.BlockSpec(memory_space=pl.ANY)],
+        out_specs=pl.BlockSpec(memory_space=pltpu.VMEM),
+        scratch_shapes=[
+            pltpu.VMEM((2, half, width), jnp.bfloat16),
+            pltpu.VMEM((2, rows, half), jnp.float32),
+            pltpu.VMEM((2, rows, half), jnp.bfloat16),
+            pltpu.VMEM((2, n - 1, rows, half), jnp.bfloat16),
+            pltpu.SemaphoreType.DMA((2,)),
+            pltpu.SemaphoreType.DMA((2,)),
+            pltpu.SemaphoreType.DMA((2, n - 1)),
+        ],
+        compiler_params=pltpu.CompilerParams(
+            collective_id=0, has_side_effects=True, vmem_limit_bytes=60 * 1024 * 1024
+        ),
+        cost_estimate=pl.CostEstimate(
+            flops=2 * rows * width * whole_w.shape[0],
+            bytes_accessed=2 * (whole_w.size + grad_proj.size + rows * block),
+            transcendentals=0,
+        ),
+    )(grad_proj, whole_w)
+
+
 def mode_sum(amp, rates, lag):
     total = amp[0] * jnp.exp(-rates[0] * lag)
     for r in range(1, rates.shape[0]):
@@ -120,9 +218,7 @@
 
     grad_proj = jnp.stack([grad_query, grad_conv * value_in, grad_conv * key_in], axis=1).astype(bf16)
     grad_proj = grad_proj.reshape(tok_rows, 3 * chan_count)
-    contract = (((1,), (1,)), ((), ()))
-    dx_terms = lax.dot_general(grad_proj, whole_w, contract, preferred_element_type=f32)
-    grad_tokens = lax.psum_scatter(dx_terms.astype(bf16), "chan", scatter_dimension=1, tiled=True)
+    grad_tokens = ring_reduce(grad_proj, whole_w, lax.axis_size("chan"))
     return (gated_output, grad_tokens)
 
 

time: 321 us -> 298 us (0.928)
  waiting for transfers between devices: 206 us -> 116 us
  Pallas kernels: 0 us -> 84.7 us
  matrix products: 59 us -> 38.6 us
  local copies, waits for them, and re-layouts: 8.01 us -> 13 us
    pallas_call x0 -> x1, Pallas kernels: none -> 84.7 us  [ring_reduce(): pl.pallas_call(functools.partial(ring_kernel, n), out_shape=jax.ShapeDtyp...]
    reduce_scatter x1 -> x0, waiting for transfers between devices: 77.7 us -> none  [local(): lax.psum_scatter(dx_terms.astype(bf16), 'chan', scatter_dimension=1, tile...]
    dot_general x1 -> x0, matrix products: 20.3 us -> none  [local(): lax.dot_general(grad_proj, whole_w, contract, preferred_element_type=f32)]
    all_gather x1, waiting for transfers between devices: 105 us -> 93.9 us  [local(): whole_w = lax.all_gather(flat_w, SEQ, axis=0, tiled=True)]
    unnamed x37 -> x38, local copies, waits for them, and re-layouts: 6.04 us -> 8.32 us
  transfers between devices with their start and end apart: 3 -> 2, of which waited for: 3 -> 2; matrix products, arithmetic and copies ran while one was open for 7% -> 7% of each run, Pallas kernels for 0% -> 0%
where the time goes in v3:
time: 298 us; the launch traced here: 297 us
  waiting for transfers between devices  116 us (39%)
  Pallas kernels  84.7 us (28%)
  matrix products  38.6 us (13%)
  other arithmetic  30.5 us (10%)
  between operations  14.4 us (5%)
  local copies, waits for them, and re-layouts  13 us (4%)
    all_gather x1, waiting for transfers between devices, local(): whole_w = lax.all_gather(flat_w, SEQ, axis=0, tiled=True)  93.9 us
    pallas_call x1, Pallas kernels, ring_reduce(): pl.pallas_call(functools.partial(ring_kernel, n), out_shape=jax.ShapeDtyp...  84.7 us
    all_gather x1, waiting for transfers between devices, local(): every = lax.all_gather(states, SEQ)  21.9 us
    dot_general x1, matrix products, local(): projected = jnp.dot(tokens, whole_w, preferred_element_type=f32)  20.1 us
    another operation x3, other arithmetic  14.5 us
    reduce_sum x1, other arithmetic, local(): jnp.sum(jnp.exp(-rates[r] * col) * grad_mix, axis=0)  9.15 us
    dot_general x2, matrix products, spectral_conv(): return jnp.dot(inv, prod, preferred_element_type=f32)  8.85 us
    unnamed x38, local copies, waits for them, and re-layouts  8.32 us
  transfers between devices with their start and end apart: 2, of which 2 were waited for; matrix products, arithmetic and copies ran while one was open for 7% of the time, Pallas kernels for 0%

profile of v3, /device:TPU:32, one launch (start us, length us, event | category | flops | bytes accessed | tf_op | source)
XLA Modules:
  0.0 297.1 jit_solution(13225050536831521599)
XLA Ops:
  7.2 0.0 copy-start.8
  7.2 0.0 all-gather.4.cloned.1.call-start
  7.2 1.5 copy.22
  8.7 0.0 copy-start.14
  8.7 1.2 copy.23
  9.8 0.0 all-gather.4.cloned.1.call-update
  9.9 0.0 all-gather.6.cloned.1.call-start
  9.9 0.0 copy-done.8
  9.9 1.0 copy.25
  10.9 0.0 copy-done.14
  11.0 93.9 %all-gather.4.cloned.1.call-done.w_hbm = bf16[8192,1536]{1,0:T(8,128)(2,1)} async-done(((bf16[256,1536]{1,0:T(8,128)(2,1)}), bf16[8192,1536]{1,0:T(8,128)(2,1)}) %all-gather.4.cloned.1.call-update) | async-done | bytes 25165840 | tf_op jit(solution)/shard_map/all_gather | solution.py:152
  104.9 20.1 %convolution_convert_fusion = bf16[512,1536]{1,0:T(8,128)(2,1)} fusion(bf16[512,8192]{1,0:T(8,128)(2,1)} %param.6, bf16[8192,1536]{1,0:T(8,128)(2,1)} %all-gather.4.cloned.1.call-done.w_hbm), kind=kOutput, calls=%fused_computation | convolution fusion | flops 12885688320 | bytes 35127296 | tf_op jit(solution)/shard_map/dot_general | solution.py:153
  124.9 1.7 copy.24
  126.7 0.0 copy-start.3
  126.7 9.1 %multiply_reduce_fusion = (f32[512]{0:T(512)S(1)}, f32[512]{0:T(512)S(1)}, f32[512]{0:T(512)S(1)}, f32[512]{0:T(512)S(1)}, f32[512]{0:T(512)S(1)}, /*index=5*/f3...) fusion(f32[512]{0:T(512)S(1)} %bitcast.218, ...), kind=kLoop, calls=%fused_computation.61 | loop fusion | flops 25935872 | bytes 5867520 | tf_op jit(solution)/shard_map/reduce_sum | solution.py:176
  135.8 0.0 copy-done.3
  135.8 0.1 stack.143
  135.9 0.1 stack.161
  136.0 0.6 pad_maximum_fusion.3
  136.6 0.0 all-gather.6.cloned.1.call-update
  136.8 3.8 %fusion.110 = f32[512,512]{1,0:T(8,128)S(1)} fusion(), kind=kLoop, calls=%fused_computation.189 | loop fusion | flops 3670016 | bytes 1048576 | tf_op jit(solution)/shard_map/cos | solution.py:25
  140.6 0.0 copy-start.4
  140.6 4.1 %fusion.71 = bf16[512,512]{1,0:T(8,128)(2,1)S(1)} fusion(f32[512]{0:T(512)S(1)} %fusion.119, s32[512]{0:T(512)S(1)} %iota_subtract_fusion.1, pred[512]{0:T(512)(128)(4,1)S(1)} %iota_compare_fusion), kind=kLoop, calls=%fused_computation.150 | loop fusion | flops 3932160 | bytes 528896 | tf_op jit(solution)/shard_map/convert.10
  144.7 9.7 %multiply_convert_fusion.3 = (bf16[512,512]{1,0:T(8,128)(2,1)}, bf16[512,512]{1,0:T(8,128)(2,1)}, bf16[512,512]{1,0:T(8,128)(2,1)}, f32[512,512]{1,0:T(8,128)S(1...) fusion(f32[512]{0:T(512)S(1)} %get-tuple-element.142, s32[512]{0:T(512)S(1)} %iota_subtract_fusion.1, ...), kind=kLoop, calls=%fused_computation.57 | loop fusion | flops 10223616 | bytes 3678720 | tf_op jit(solution)/shard_map/convert.11
  154.4 0.0 copy-start.1
  154.4 0.0 copy-done.4
  154.4 0.0 copy-start.6
  154.4 0.7 fusion.11
  155.2 0.2 copy-done.1
  155.4 0.6 copy-done.6
  156.0 2.1 fusion.26
  158.1 0.0 copy-start.15
  158.1 21.9 %all-gather.6.cloned.1.call-done = f32[64,16,512]{2,1,0:T(8,128)} async-done(((f32[2,16,512]{2,1,0:T(8,128)}), f32[64,16,512]{2,1,0:T(8,128)}) %all-gather.6.cloned.1.call-update) | async-done | bytes 2097168 | tf_op jit(solution)/shard_map/all_gather | solution.py:179
  179.9 0.0 copy-start.2
  180.0 2.1 fusion.14
  182.1 0.0 copy-done.15
  182.2 0.0 copy-done.2
  182.2 0.0 copy-start
  182.3 6.9 %fusion = f32[1024,512]{1,0:T(8,128)S(1)} fusion(f32[512,512]{1,0:T(8,128)S(1)} %copy-done.2, f32[512,512]{1,0:T(8,128)S(1)} %fusion.110, f32[512]{0:T(512)S(1)} %bitcast.219, f32[512]{0:T(512)S(1)} %bitcast.239, f32[512]{0:T(512)S(1)} %bitcast.163, f32[512]{0:T(512)S(1)} %bitcast.240, f32[512]{0:T(512)S(1)} %bitcast.167, f32[512]{0:T(512)S(1)} %bitcast.241, ...), kind=kOutput, calls=%fused_computation.2 | convolution fusion | flops 3234070528 | bytes 4259840 | tf_op jit(solution)/shard_map/dot_general | solution.py:203
  189.2 0.0 copy-done
  189.3 0.0 copy-start.7
  189.3 0.0 copy-start.12
  189.3 0.0 copy-start.13
  189.3 0.0 copy-start.16
  189.3 0.7 subtract_convert_fusion.1
  190.0 0.5 copy-done.7
  190.5 0.1 copy-done.12
  190.6 0.2 copy-done.13
  190.8 0.0 copy-done.16
  190.8 0.0 copy-start.5
  190.8 0.0 copy-start.9
  190.8 0.0 copy-start.10
  190.8 0.0 copy-start.11
  190.8 3.5 %fusion.2 = f32[512,512]{0,1:T(8,128)S(1)} fusion(bf16[512,512]{1,0:T(8,128)(2,1)S(1)} %copy-done.13, bf16[512,512]{1,0:T(8,128)(2,1)S(1)} %copy-done.12, bf16[512,512]{1,0:T(8,128)(2,1)S(1)} %get-tuple-element.69, bf16[512,512]{1,0:T(8,128)(2,1)S(1)} %get-tuple-element.70, f32[512,512]{0,1:T(8,128)S(1)} %copy-done.7, f32[512]{0:T(512)S(1)} %bitcast.287, ...), kind=kOutput, calls=%fused_computation.12 | convolution fusion | flops 554172416 | bytes 4263936 | tf_op jit(solution)/shard_map/dot_general | solution.py:43
  194.3 0.0 copy-done.5
  194.4 0.0 copy-done.9
  194.4 0.0 copy-done.10
  194.4 0.0 copy-done.11
  194.4 5.3 %fusion.72 = (bf16[512,1,512]{0,2,1:T(8,128)(2,1)S(1)}, bf16[512,1,512]{0,2,1:T(8,128)(2,1)S(1)}, bf16[512,512]{0,1:T(8,128)(2,1)S(1)}, bf16[512,1,512]{0,2,1:T(8,128)(2,1)S(1)}) fusion(f32[512,512]{0,1:T(8,128)S(1)} %fusion.2, f32[512,3,512]{0,2,1:T(8,128)} %bitcast.152, bf16[512,512]{0,1:T(8,128)(2,1)S(1)} %copy-done.9, f32[512,512]{0,1:T(8,128)S(1)} %copy-done.5, ...), kind=kOutput, calls=%fused_computation.151 | convolution fusion | flops 556531712 | bytes 10031104 | tf_op jit(solution)/shard_map/dot_general | solution.py:43
  199.7 0.2 pad_maximum_fusion.2
  199.9 1.6 copy.27.gp_ref
  201.5 84.7 %shard_map.77 = bf16[512,2048]{1,0:T(8,128)(2,1)} custom-call(bf16[512,1536]{1,0:T(8,128)(2,1)} %copy.27.gp_ref, bf16[8192,1536]{1,0:T(8,128)(2,1)} %all-gather.4.cloned.1.call-done.w_hbm), custom_call_target="tpu_custom_call" | custom-call | flops 12884901888 | bytes 28835840 | tf_op jit(solution)/shard_map/pallas_call | solution.py:114
  286.1 1.0 copy.28
  287.1 3.2 %copy.31 = bf16[512,2048]{1,0:T(8,128)(2,1)} copy(bf16[512,2048]{1,0:T(8,128)(2,1)} %shard_map.77) | data formatting | bytes 4194304
  (17 shorter events, 0.2 us)
Async XLA Ops:
  7.2 2.8 copy-start.8
  7.2 97.7 %all-gather.4.cloned.1.call-start = ((), (), s32[]{:S(2)}) async-start(), calls=%async_computation | async-start | bytes 25952256 | tf_op jit(solution)/shard_map/all_gather | solution.py:152
  8.7 2.3 copy-start.14
  9.9 170.1 %all-gather.6.cloned.1.call-start = ((), (), s32[]{:S(2)}) async-start(), calls=%async_computation.1 | async-start | bytes 2162688 | tf_op jit(solution)/shard_map/all_gather | solution.py:179
  126.7 9.2 %copy-start.3 = (f32[512,1536]{0,1:T(8,128)}, f32[512,1536]{0,1:T(8,128)S(1)}, u32[]{:S(2)}) copy-start(f32[512,1536]{0,1:T(8,128)S(1)} %copy.24) | copy-start | bytes 9437188
  140.6 13.9 %copy-start.4 = (f32[512,512]{0,1:T(8,128)S(1)}, f32[512,512]{0,1:T(8,128)}, u32[]{:S(2)}) copy-start(f32[512,512]{0,1:T(8,128)} %get-tuple-element.61) | copy-start | bytes 3145732
  154.4 1.0 copy-start.1
  154.4 1.6 copy-start.6
  158.1 24.0 %copy-start.15 = (f32[16,512]{1,0:T(8,128)S(1)}, f32[16,512]{1,0:T(8,128)}, u32[]{:S(2)}) copy-start(f32[16,512]{1,0:T(8,128)} %param.8) | copy-start | bytes 98308
  179.9 2.3 copy-start.2
  182.2 7.0 %copy-start = (f32[1024,512]{1,0:T(8,128)S(1)}, f32[1024,512]{1,0:T(8,128)}, u32[]{:S(2)}) copy-start(f32[1024,512]{1,0:T(8,128)} %fusion.26) | copy-start | bytes 6291460
  189.3 1.2 copy-start.7
  189.3 1.3 copy-start.12
  189.3 1.5 copy-start.13
  189.3 1.5 copy-start.16
  190.8 3.6 %copy-start.5 = (f32[512,512]{0,1:T(8,128)S(1)}, f32[512,512]{0,1:T(8,128)}, u32[]{:S(2)}) copy-start(f32[512,512]{0,1:T(8,128)} %get-tuple-element.61) | copy-start | bytes 3145732
  190.8 3.6 %copy-start.9 = (bf16[512,512]{0,1:T(8,128)(2,1)S(1)}, bf16[512,512]{0,1:T(8,128)(2,1)}, u32[]{:S(2)}) copy-start(bf16[512,512]{0,1:T(8,128)(2,1)} %copy.25) | copy-start | bytes 1572868
  190.8 3.6 %copy-start.10 = (bf16[512,512]{1,0:T(8,128)(2,1)S(1)}, bf16[512,512]{1,0:T(8,128)(2,1)}, u32[]{:S(2)}) copy-start(bf16[512,512]{1,0:T(8,128)(2,1)} %get-tuple-element.138) | copy-start | bytes 1572868
  190.8 3.6 %copy-start.11 = (bf16[512,512]{1,0:T(8,128)(2,1)S(1)}, bf16[512,512]{1,0:T(8,128)(2,1)}, u32[]{:S(2)}) copy-start(bf16[512,512]{1,0:T(8,128)(2,1)} %get-tuple-element.141) | copy-start | bytes 1572868
Sparse Core Ops, SparseCore 0:
  10.8 93.9 all-gather.3
  136.8 43.1 all-gather.5

commit v4 on v3

--- a/solution.py
+++ b/solution.py
@@ -41,6 +41,113 @@
     pi = xc * h_b + xs * h_a2
     prod = jnp.concatenate([pr, pi], axis=0).astype(bf16)
     return jnp.dot(inv, prod, preferred_element_type=f32)
+
+
+def gather_kernel(shard_ref, out_hbm, send_sem, recv_sem, local_sem):
+    rows = shard_ref.shape[0]
+    side = 4
+    x = lax.axis_index("x")
+    y = lax.axis_index("y")
+    core = lax.axis_index("core")
+    other = 1 - core
+    a0 = x * other + y * core
+    b0 = y * other + x * core
+
+    def coords(a, b):
+        a = lax.rem(a + 2 * side, side)
+        b = lax.rem(b + 2 * side, side)
+        return a * other + b * core, b * other + a * core
+
+    def slot(a, b, c):
+        xx, yy = coords(a, b)
+        return out_hbm.at[pl.ds(pl.multiple_of(((xx * side + yy) * 2 + c) * rows, rows), rows)]
+
+    def device(a, b, c):
+        xx, yy = coords(a, b)
+        return {"x": xx, "y": yy, "core": c}
+
+    peers = [device(a0 + 1, b0, core), device(a0 - 1, b0, core), device(a0, b0 + 1, core),
+             device(a0, b0 - 1, core), device(a0, b0, other)]
+    barrier = pltpu.get_barrier_semaphore()
+    for peer in peers:
+        pl.semaphore_signal(barrier, inc=1, device_id=peer, device_id_type=MESH)
+    pl.semaphore_wait(barrier, len(peers))
+
+    sent = []
+
+    def push(src, dst, target, index):
+        cp = pltpu.make_async_remote_copy(
+            src_ref=src, dst_ref=dst, send_sem=send_sem.at[index], recv_sem=recv_sem.at[index],
+            device_id=target, device_id_type=MESH,
+        )
+        cp.start()
+        sent.append(cp)
+        return cp
+
+    mine = slot(a0, b0, core)
+    own = pltpu.make_async_copy(shard_ref, mine, local_sem.at[0])
+    own.start()
+    partner = device(a0, b0, other)
+    up = push(shard_ref, mine, device(a0 + 1, b0, core), 0)
+    down = push(shard_ref, mine, device(a0 - 1, b0, core), 1)
+    own.wait()
+    push(mine, mine, partner, 15)
+    up.wait_recv()
+    fwd = push(slot(a0 - 1, b0, core), slot(a0 - 1, b0, core), device(a0 + 1, b0, core), 2)
+    push(slot(a0 - 1, b0, core), slot(a0 - 1, b0, core), partner, 16)
+    down.wait_recv()
+    push(slot(a0 + 1, b0, core), slot(a0 + 1, b0, core), partner, 17)
+    fwd.wait_recv()
+    push(slot(a0 + 2, b0, core), slot(a0 + 2, b0, core), partner, 18)
+    outs = []
+    for j in range(side):
+        src = slot(a0 + j, b0, core)
+        outs.append(push(src, src, device(a0, b0 + 1, core), 3 + j))
+    for j in range(side):
+        src = slot(a0 + j, b0, core)
+        outs.append(push(src, src, device(a0, b0 - 1, core), 7 + j))
+    later = []
+    for j in range(side):
+        outs[j].wait_recv()
+        src = slot(a0 + j, b0 - 1, core)
+        if j < 2:
+            later.append(push(src, src, device(a0, b0 + 1, core), 11 + j))
+        push(src, src, partner, 19 + j)
+    for j in range(side):
+        outs[side + j].wait_recv()
+        src = slot(a0 + j, b0 + 1, core)
+        if j >= 2:
+            later.append(push(src, src, device(a0, b0 - 1, core), 11 + j))
+        push(src, src, partner, 23 + j)
+    for j in range(side):
+        later[j].wait_recv()
+        src = slot(a0 + j, b0 + 2, core)
+        push(src, src, partner, 27 + j)
+    for cp in sent:
+        cp.wait_send()
+    for index in range(15, 31):
+        pltpu.make_async_remote_copy(
+            src_ref=mine, dst_ref=mine, send_sem=send_sem.at[index], recv_sem=recv_sem.at[index],
+            device_id=partner, device_id_type=MESH,
+        ).wait_recv()
+
+
+def gather_rows(shard):
+    rows, width = shard.shape
+    total = rows * lax.axis_size(SEQ)
+    return pl.pallas_call(
+        gather_kernel,
+        out_shape=jax.ShapeDtypeStruct((total, width), shard.dtype),
+        in_specs=[pl.BlockSpec(memory_space=pltpu.VMEM)],
+        out_specs=pl.BlockSpec(memory_space=pl.ANY),
+        scratch_shapes=[
+            pltpu.SemaphoreType.DMA((31,)),
+            pltpu.SemaphoreType.DMA((31,)),
+            pltpu.SemaphoreType.DMA((1,)),
+        ],
+        compiler_params=pltpu.CompilerParams(collective_id=1, has_side_effects=True),
+        cost_estimate=pl.CostEstimate(flops=0, bytes_accessed=2 * total * width * 2, transcendentals=0),
+    )(shard)
 
 
 def ring_kernel(n, gp_ref, w_hbm, out_ref, wbuf, acc, snd, rcv, wsem, send_sem, recv_sem):
@@ -149,7 +256,7 @@
     seq_count = lax.axis_size(SEQ)
     me = lax.axis_index(SEQ)
     flat_w = proj_weight.reshape(proj_weight.shape[0], 3 * chan_count)
-    whole_w = lax.all_gather(flat_w, SEQ, axis=0, tiled=True)
+    whole_w = gather_rows(flat_w)
     projected = jnp.dot(tokens, whole_w, preferred_element_type=f32)
     proj_vals = (
         lax.optimization_barrier(projected.astype(bf16))
@@ -222,14 +329,14 @@
     return (gated_output, grad_tokens)
 
 
-SEQ = ("xy", "core")
+SEQ = ("x", "y", "core")
 
 
 def solution(mesh):
-    cores = 2
+    side, cores = 4, 2
     split = jax.sharding.Mesh(
-        mesh.devices.reshape(mesh.shape["seq"] // cores, cores, mesh.shape["chan"]),
-        ("xy", "core", "chan"),
+        mesh.devices.reshape(side, mesh.shape["seq"] // (side * cores), cores, mesh.shape["chan"]),
+        ("x", "y", "core", "chan"),
     )
     placed = (
         P(SEQ, None),

time: 298 us -> 295 us (0.990)
  waiting for transfers between devices: 116 us -> 23.6 us
  Pallas kernels: 84.7 us -> 172 us
    all_gather x1 -> x0, waiting for transfers between devices: 93.9 us -> none  [local(): whole_w = lax.all_gather(flat_w, SEQ, axis=0, tiled=True)]
    pallas_call x0 -> x1, Pallas kernels: none -> 87.2 us  [gather_rows(): pl.pallas_call(gather_kernel, out_shape=jax.ShapeDtypeStruct((total, widt...]
    unnamed x38 -> x36, local copies, waits for them, and re-layouts: 8.32 us -> 9.74 us
  transfers between devices with their start and end apart: 2 -> 1, of which waited for: 2 -> 1; matrix products, arithmetic and copies ran while one was open for 7% -> 7% of each run, Pallas kernels for 0% -> 0%
where the time goes in v4:
time: 295 us; the launch traced here: 294 us
  Pallas kernels  172 us (58%)
  matrix products  38.7 us (13%)
  other arithmetic  31.4 us (11%)
  waiting for transfers between devices  23.6 us (8%)
  local copies, waits for them, and re-layouts  14.4 us (5%)
  between operations  14.4 us (5%)
    pallas_call x1, Pallas kernels, gather_rows(): pl.pallas_call(gather_kernel, out_shape=jax.ShapeDtypeStruct((total, widt...  87.2 us
    pallas_call x1, Pallas kernels, ring_reduce(): pl.pallas_call(functools.partial(ring_kernel, n), out_shape=jax.ShapeDtyp...  84.6 us
    all_gather x1, waiting for transfers between devices, local(): every = lax.all_gather(states, SEQ)  23.6 us
    dot_general x1, matrix products, local(): projected = jnp.dot(tokens, whole_w, preferred_element_type=f32)  20.1 us
    another operation x3, other arithmetic  14.4 us
    unnamed x36, local copies, waits for them, and re-layouts  9.74 us
    reduce_sum x1, other arithmetic, local(): jnp.sum(jnp.exp(-rates[r] * col) * grad_mix, axis=0)  8.91 us
    dot_general x2, matrix products, spectral_conv(): return jnp.dot(inv, prod, preferred_element_type=f32)  8.89 us
  transfers between devices with their start and end apart: 1, of which 1 were waited for; matrix products, arithmetic and copies ran while one was open for 7% of the time, Pallas kernels for 0%

profile of v4, /device:TPU:32, one launch (start us, length us, event | category | flops | bytes accessed | tf_op | source)
XLA Modules:
  0.0 294.4 jit_solution(12674513266078613535)
XLA Ops:
  7.2 0.0 all-gather.3.cloned.1.call-start
  7.2 1.2 slice_negate_fusion.15
  8.4 1.4 copy.22
  9.8 1.2 copy.23.shard_ref
  11.0 87.2 %shard_map.77.w_hbm = bf16[8192,1536]{1,0:T(8,128)(2,1)} custom-call(bf16[256,1536]{1,0:T(8,128)(2,1)} %copy.23.shard_ref), custom_call_target="tpu_custom_call" | custom-call | bytes 50331648 | tf_op jit(solution)/shard_map/pallas_call | solution.py:138
  98.2 20.1 %convolution_convert_fusion = bf16[512,1536]{1,0:T(8,128)(2,1)} fusion(bf16[512,8192]{1,0:T(8,128)(2,1)} %param.6, bf16[8192,1536]{1,0:T(8,128)(2,1)} %shard_map.77.w_hbm), kind=kOutput, calls=%fused_computation | convolution fusion | flops 12885688320 | bytes 35127296 | tf_op jit(solution)/shard_map/dot_general | solution.py:260
  118.3 1.7 copy.24
  120.0 0.0 copy-start.3
  120.0 2.4 copy.25
  122.4 0.0 copy-start.13
  122.5 8.9 %multiply_reduce_fusion = (f32[512]{0:T(512)S(1)}, f32[512]{0:T(512)S(1)}, f32[512]{0:T(512)S(1)}, f32[512]{0:T(512)S(1)}, f32[512]{0:T(512)S(1)}, /*index=5*/f3...) fusion(f32[512]{0:T(512)S(1)} %bitcast.218, ...), kind=kLoop, calls=%fused_computation.61 | loop fusion | flops 25935872 | bytes 5867520 | tf_op jit(solution)/shard_map/reduce_sum | solution.py:283
  131.4 0.0 copy-done.3
  131.4 0.1 stack.143
  131.5 0.1 stack.161
  131.5 0.6 pad_maximum_fusion.3
  132.2 0.0 all-gather.3.cloned.1.call-update
  132.3 3.8 %fusion.110 = f32[512,512]{1,0:T(8,128)S(1)} fusion(), kind=kLoop, calls=%fused_computation.189 | loop fusion | flops 3670016 | bytes 1048576 | tf_op jit(solution)/shard_map/cos | solution.py:25
  136.1 0.0 copy-done.13
  136.1 0.0 copy-start.4
  136.1 4.1 %fusion.71 = bf16[512,512]{1,0:T(8,128)(2,1)S(1)} fusion(f32[512]{0:T(512)S(1)} %fusion.119, s32[512]{0:T(512)S(1)} %iota_subtract_fusion.1, pred[512]{0:T(512)(128)(4,1)S(1)} %iota_compare_fusion), kind=kLoop, calls=%fused_computation.150 | loop fusion | flops 3932160 | bytes 528896 | tf_op jit(solution)/shard_map/convert.10
  140.2 9.7 %multiply_convert_fusion.3 = (bf16[512,512]{1,0:T(8,128)(2,1)}, bf16[512,512]{1,0:T(8,128)(2,1)}, bf16[512,512]{1,0:T(8,128)(2,1)}, f32[512,512]{1,0:T(8,128)S(1...) fusion(f32[512]{0:T(512)S(1)} %get-tuple-element.142, s32[512]{0:T(512)S(1)} %iota_subtract_fusion.1, ...), kind=kLoop, calls=%fused_computation.57 | loop fusion | flops 10223616 | bytes 3678720 | tf_op jit(solution)/shard_map/convert.11
  150.0 0.0 copy-start.1
  150.0 0.0 copy-done.4
  150.0 0.0 copy-start.6
  150.0 0.8 fusion.11
  150.8 0.2 copy-done.1
  151.0 0.6 copy-done.6
  151.6 2.1 fusion.26
  153.6 0.0 copy-start.14
  153.6 23.6 %all-gather.3.cloned.1.call-done = f32[64,16,512]{2,1,0:T(8,128)} async-done(((f32[2,16,512]{2,1,0:T(8,128)}), f32[64,16,512]{2,1,0:T(8,128)}) %all-gather.3.cloned.1.call-update) | async-done | bytes 2097168 | tf_op jit(solution)/shard_map/all_gather | solution.py:286
  177.2 0.0 copy-start.2
  177.2 2.1 fusion.14
  179.4 0.0 copy-done.14
  179.5 0.0 copy-done.2
  179.5 0.0 copy-start
  179.5 6.9 %fusion = f32[1024,512]{1,0:T(8,128)S(1)} fusion(f32[512,512]{1,0:T(8,128)S(1)} %copy-done.2, f32[512,512]{1,0:T(8,128)S(1)} %fusion.110, f32[512]{0:T(512)S(1)} %bitcast.219, f32[512]{0:T(512)S(1)} %bitcast.239, f32[512]{0:T(512)S(1)} %bitcast.163, f32[512]{0:T(512)S(1)} %bitcast.240, f32[512]{0:T(512)S(1)} %bitcast.167, f32[512]{0:T(512)S(1)} %bitcast.241, ...), kind=kOutput, calls=%fused_computation.2 | convolution fusion | flops 3234070528 | bytes 4259840 | tf_op jit(solution)/shard_map/dot_general | solution.py:310
  186.5 0.0 copy-done
  186.5 0.0 copy-start.7
  186.5 0.0 copy-start.11
  186.5 0.0 copy-start.12
  186.5 0.0 copy-start.15
  186.5 0.6 subtract_convert_fusion.1
  187.2 0.6 copy-done.7
  187.7 0.1 copy-done.11
  187.8 0.2 copy-done.12
  188.0 0.0 copy-done.15
  188.0 0.0 copy-start.5
  188.0 0.0 copy-start.8
  188.0 0.0 copy-start.9
  188.0 0.0 copy-start.10
  188.0 3.5 %fusion.2 = f32[512,512]{0,1:T(8,128)S(1)} fusion(bf16[512,512]{1,0:T(8,128)(2,1)S(1)} %copy-done.12, bf16[512,512]{1,0:T(8,128)(2,1)S(1)} %copy-done.11, bf16[512,512]{1,0:T(8,128)(2,1)S(1)} %get-tuple-element.69, bf16[512,512]{1,0:T(8,128)(2,1)S(1)} %get-tuple-element.70, f32[512,512]{0,1:T(8,128)S(1)} %copy-done.7, f32[512]{0:T(512)S(1)} %bitcast.287, ...), kind=kOutput, calls=%fused_computation.12 | convolution fusion | flops 554172416 | bytes 4263936 | tf_op jit(solution)/shard_map/dot_general | solution.py:43
  191.6 0.0 copy-done.5
  191.6 0.0 copy-done.8
  191.6 0.0 copy-done.9
  191.6 0.0 copy-done.10
  191.6 5.3 %fusion.72 = (bf16[512,1,512]{0,2,1:T(8,128)(2,1)S(1)}, bf16[512,1,512]{0,2,1:T(8,128)(2,1)S(1)}, bf16[512,512]{0,1:T(8,128)(2,1)S(1)}, bf16[512,1,512]{0,2,1:T(8,128)(2,1)S(1)}) fusion(f32[512,512]{0,1:T(8,128)S(1)} %fusion.2, f32[512,3,512]{0,2,1:T(8,128)} %bitcast.152, bf16[512,512]{0,1:T(8,128)(2,1)S(1)} %copy-done.8, f32[512,512]{0,1:T(8,128)S(1)} %copy-done.5, ...), kind=kOutput, calls=%fused_computation.151 | convolution fusion | flops 556531712 | bytes 10031104 | tf_op jit(solution)/shard_map/dot_general | solution.py:43
  197.0 0.2 pad_maximum_fusion.2
  197.2 1.6 copy.27.gp_ref
  198.7 84.6 %shard_map.78 = bf16[512,2048]{1,0:T(8,128)(2,1)} custom-call(bf16[512,1536]{1,0:T(8,128)(2,1)} %copy.27.gp_ref, bf16[8192,1536]{1,0:T(8,128)(2,1)} %shard_map.77.w_hbm), custom_call_target="tpu_custom_call" | custom-call | flops 12884901888 | bytes 28835840 | tf_op jit(solution)/shard_map/pallas_call | solution.py:221
  283.3 1.0 copy.28
  284.4 3.2 %copy.31 = bf16[512,2048]{1,0:T(8,128)(2,1)} copy(bf16[512,2048]{1,0:T(8,128)(2,1)} %shard_map.78) | data formatting | bytes 4194304
  (16 shorter events, 0.2 us)
Async XLA Ops:
  7.2 170.1 %all-gather.3.cloned.1.call-start = ((), (), s32[]{:S(2)}) async-start(), calls=%async_computation | async-start | bytes 2162688 | tf_op jit(solution)/shard_map/all_gather | solution.py:286
  120.0 11.4 %copy-start.3 = (f32[512,1536]{0,1:T(8,128)}, f32[512,1536]{0,1:T(8,128)S(1)}, u32[]{:S(2)}) copy-start(f32[512,1536]{0,1:T(8,128)S(1)} %copy.24) | copy-start | bytes 9437188
  122.4 13.6 %copy-start.13 = (f32[16,512]{1,0:T(8,128)S(1)}, f32[16,512]{1,0:T(8,128)}, u32[]{:S(2)}) copy-start(f32[16,512]{1,0:T(8,128)} %param.9) | copy-start | bytes 98308
  136.1 13.9 %copy-start.4 = (f32[512,512]{0,1:T(8,128)S(1)}, f32[512,512]{0,1:T(8,128)}, u32[]{:S(2)}) copy-start(f32[512,512]{0,1:T(8,128)} %get-tuple-element.61) | copy-start | bytes 3145732
  150.0 1.0 copy-start.1
  150.0 1.6 copy-start.6
  153.6 25.7 %copy-start.14 = (f32[16,512]{1,0:T(8,128)S(1)}, f32[16,512]{1,0:T(8,128)}, u32[]{:S(2)}) copy-start(f32[16,512]{1,0:T(8,128)} %param.8) | copy-start | bytes 98308
  177.2 2.3 copy-start.2
  179.5 7.0 %copy-start = (f32[1024,512]{1,0:T(8,128)S(1)}, f32[1024,512]{1,0:T(8,128)}, u32[]{:S(2)}) copy-start(f32[1024,512]{1,0:T(8,128)} %fusion.26) | copy-start | bytes 6291460
  186.5 1.2 copy-start.7
  186.5 1.3 copy-start.11
  186.5 1.5 copy-start.12
  186.5 1.5 copy-start.15
  188.0 3.6 %copy-start.5 = (f32[512,512]{0,1:T(8,128)S(1)}, f32[512,512]{0,1:T(8,128)}, u32[]{:S(2)}) copy-start(f32[512,512]{0,1:T(8,128)} %get-tuple-element.61) | copy-start | bytes 3145732
  188.0 3.6 %copy-start.8 = (bf16[512,512]{0,1:T(8,128)(2,1)S(1)}, bf16[512,512]{0,1:T(8,128)(2,1)}, u32[]{:S(2)}) copy-start(bf16[512,512]{0,1:T(8,128)(2,1)} %copy.25) | copy-start | bytes 1572868
  188.0 3.6 %copy-start.9 = (bf16[512,512]{1,0:T(8,128)(2,1)S(1)}, bf16[512,512]{1,0:T(8,128)(2,1)}, u32[]{:S(2)}) copy-start(bf16[512,512]{1,0:T(8,128)(2,1)} %get-tuple-element.138) | copy-start | bytes 1572868
  188.0 3.6 %copy-start.10 = (bf16[512,512]{1,0:T(8,128)(2,1)S(1)}, bf16[512,512]{1,0:T(8,128)(2,1)}, u32[]{:S(2)}) copy-start(bf16[512,512]{1,0:T(8,128)(2,1)} %get-tuple-element.141) | copy-start | bytes 1572868
Sparse Core Ops, SparseCore 0:
  132.3 44.8 all-gather.2

commit v5 on v4

--- a/solution.py
+++ b/solution.py
@@ -132,7 +132,7 @@
         ).wait_recv()
 
 
-def gather_rows(shard):
+def gather_rows(shard, collective):
     rows, width = shard.shape
     total = rows * lax.axis_size(SEQ)
     return pl.pallas_call(
@@ -145,7 +145,7 @@
             pltpu.SemaphoreType.DMA((31,)),
             pltpu.SemaphoreType.DMA((1,)),
         ],
-        compiler_params=pltpu.CompilerParams(collective_id=1, has_side_effects=True),
+        compiler_params=pltpu.CompilerParams(collective_id=collective, has_side_effects=True),
         cost_estimate=pl.CostEstimate(flops=0, bytes_accessed=2 * total * width * 2, transcendentals=0),
     )(shard)
 
@@ -256,7 +256,7 @@
     seq_count = lax.axis_size(SEQ)
     me = lax.axis_index(SEQ)
     flat_w = proj_weight.reshape(proj_weight.shape[0], 3 * chan_count)
-    whole_w = gather_rows(flat_w)
+    whole_w = gather_rows(flat_w, 1)
     projected = jnp.dot(tokens, whole_w, preferred_element_type=f32)
     proj_vals = (
         lax.optimization_barrier(projected.astype(bf16))
@@ -283,7 +283,7 @@
         [jnp.sum(jnp.exp(-rates[r] * col) * grad_mix, axis=0) for r in range(modes)]
     )
     states = jnp.stack([end_fwd, end_bwd])
-    every = lax.all_gather(states, SEQ)
+    every = gather_rows(states.reshape(2 * modes, chan_count), 2).reshape(seq_count, 2, modes, chan_count)
 
     others = jnp.arange(seq_count, dtype=jnp.int32)
     gap_f = me - 1 - others

time: 295 us -> 285 us (0.966); the launches traced: 294 us -> 279 us
  Pallas kernels: 172 us -> 197 us
  waiting for transfers between devices: 23.6 us -> 0 us
  between operations: 14.4 us -> 1.19 us
    pallas_call x1 -> x2, Pallas kernels: 87.2 us -> 111 us  [gather_rows(): pl.pallas_call(gather_kernel, out_shape=jax.ShapeDtypeStruct((total, widt...]
    all_gather x1 -> x0, waiting for transfers between devices: 23.6 us -> none  [local(): every = lax.all_gather(states, SEQ)]
    unnamed x36 -> x22, local copies, waits for them, and re-layouts: 9.74 us -> 9 us
  transfers between devices with their start and end apart: 1 -> 0, of which waited for: 1 -> 0; matrix products, arithmetic and copies ran while one was open for 7% -> 0% of each run, Pallas kernels for 0% -> 0%
where the time goes in v5:
time: 285 us; the launch traced here: 279 us
  Pallas kernels  197 us (69%)
  matrix products  36.4 us (13%)
  other arithmetic  31.3 us (11%)
  local copies, waits for them, and re-layouts  13.7 us (5%)
    pallas_call x2, Pallas kernels, gather_rows(): pl.pallas_call(gather_kernel, out_shape=jax.ShapeDtypeStruct((total, widt...  111 us
    pallas_call x1, Pallas kernels, ring_reduce(): pl.pallas_call(functools.partial(ring_kernel, n), out_shape=jax.ShapeDtyp...  85.6 us
    dot_general x1, matrix products, local(): projected = jnp.dot(tokens, whole_w, preferred_element_type=f32)  20.1 us
    another operation x3, other arithmetic  13.8 us
    reduce_sum x1, other arithmetic, local(): jnp.sum(jnp.exp(-rates[r] * col) * grad_mix, axis=0)  9.36 us
    unnamed x22, local copies, waits for them, and re-layouts  9 us
    dot_general x2, matrix products, spectral_conv(): return jnp.dot(inv, prod, preferred_element_type=f32)  7.87 us
    dot_general x1, matrix products, local(): spec = jnp.dot(fwd, taps, precision=lax.Precision.HIGHEST)  6.92 us

profile of v5, /device:TPU:32, one launch (start us, length us, event | category | flops | bytes accessed | tf_op | source)
XLA Modules:
  0.0 279.5 jit_solution(15170575586863002948)
XLA Ops:
  0.6 1.2 slice_negate_fusion.15
  1.8 1.4 copy.16
  3.2 1.2 copy.17.shard_ref
  4.4 87.2 %shard_map.77.w_hbm = bf16[8192,1536]{1,0:T(8,128)(2,1)} custom-call(bf16[256,1536]{1,0:T(8,128)(2,1)} %copy.17.shard_ref), custom_call_target="tpu_custom_call" | custom-call | bytes 50331648 | tf_op jit(solution)/shard_map/pallas_call | solution.py:138
  91.6 20.1 %convolution_convert_fusion = bf16[512,1536]{1,0:T(8,128)(2,1)} fusion(bf16[512,8192]{1,0:T(8,128)(2,1)} %param.6, bf16[8192,1536]{1,0:T(8,128)(2,1)} %shard_map.77.w_hbm), kind=kOutput, calls=%fused_computation | convolution fusion | flops 12885688320 | bytes 35127296 | tf_op jit(solution)/shard_map/dot_general | solution.py:260
  111.7 1.7 copy.18
  113.4 2.0 copy.19
  115.5 9.4 %multiply_reduce_fusion = (f32[512]{0:T(512)S(1)}, f32[512]{0:T(512)S(1)}, f32[512]{0:T(512)S(1)}, f32[512]{0:T(512)S(1)}, f32[512]{0:T(512)S(1)}, /*index=5*/f3...) fusion(f32[512]{0:T(512)S(1)} %bitcast.220, ...), kind=kLoop, calls=%fused_computation.61 | loop fusion | flops 25935872 | bytes 5867520 | tf_op jit(solution)/shard_map/reduce_sum | solution.py:283
  124.8 0.0 copy-start.6
  124.9 0.1 stack.143
  124.9 0.1 stack.161
  125.0 0.6 pad_maximum_fusion.3
  125.6 0.0 copy-start.7
  125.6 24.1 %shard_map.78 = f32[1024,512]{1,0:T(8,128)} custom-call(f32[32,512]{1,0:T(8,128)} %bitcast.157), custom_call_target="tpu_custom_call" | custom-call | bytes 2097152 | tf_op jit(solution)/shard_map/pallas_call | solution.py:138
  149.8 0.0 copy-done.6
  149.8 2.1 fusion.14
  151.9 0.0 copy-done.7
  152.1 8.9 %multiply_convert_fusion.3 = (bf16[512,512]{1,0:T(8,128)(2,1)S(1)}, bf16[512,512]{1,0:T(8,128)(2,1)S(1)}, bf16[512,512]{1,0:T(8,128)(2,1)S(1)}, f32[512,512]{1,0...) fusion(f32[512]{0:T(512)S(1)} %get-tuple-element.140, s32[512]{0:T(512)S(1)} %iota_subtract_fusion.1, ...), kind=kLoop, calls=%fused_computation.57 | loop fusion | flops 10223616 | bytes 3678720 | tf_op jit(solution)/shard_map/convert.11
  160.9 4.0 %fusion.110 = f32[512,512]{1,0:T(8,128)S(1)} fusion(), kind=kLoop, calls=%fused_computation.189 | loop fusion | flops 3670016 | bytes 1048576 | tf_op jit(solution)/shard_map/cos | solution.py:25
  164.9 0.0 copy-start.2
  164.9 6.9 %fusion = f32[1024,512]{1,0:T(8,128)S(1)} fusion(f32[512,512]{1,0:T(8,128)S(1)} %get-tuple-element.137, f32[512,512]{1,0:T(8,128)S(1)} %fusion.110, f32[512]{0:T(512)S(1)} %bitcast.221, f32[512]{0:T(512)S(1)} %bitcast.273, f32[512]{0:T(512)S(1)} %bitcast.165, f32[512]{0:T(512)S(1)} %bitcast.274, f32[512]{0:T(512)S(1)} %bitcast.169, f32[512]{0:T(512)S(1)} %bitcast.275, ...), kind=kOutput, calls=%fused_computation.2 | convolution fusion | flops 3234070528 | bytes 4259840 | tf_op jit(solution)/shard_map/dot_general | solution.py:310
  171.8 0.0 copy-start
  171.8 0.0 copy-done.2
  171.9 0.0 copy-start.3
  171.9 0.7 fusion.11
  172.6 0.5 copy-done
  173.2 4.3 %fusion.71 = bf16[512,512]{1,0:T(8,128)(2,1)S(1)} fusion(f32[512]{0:T(512)S(1)} %fusion.119, s32[512]{0:T(512)S(1)} %iota_subtract_fusion.1, pred[512]{0:T(512)(128)(4,1)S(1)} %iota_compare_fusion), kind=kLoop, calls=%fused_computation.150 | loop fusion | flops 3932160 | bytes 528896 | tf_op jit(solution)/shard_map/convert.10
  177.4 0.0 copy-done.3
  177.5 0.0 copy-start.1
  177.5 0.0 slice-start
  177.5 0.8 fusion.26
  178.2 0.8 copy-done.1
  179.1 0.0 slice-done
  179.1 0.0 copy-start.8
  179.1 0.6 subtract_convert_fusion.1
  179.8 0.0 copy-done.8
  179.8 0.0 copy-start.4
  179.8 3.3 %fusion.2 = f32[512,512]{0,1:T(8,128)S(1)} fusion(bf16[512,512]{1,0:T(8,128)(2,1)S(1)} %get-tuple-element.135, bf16[512,512]{1,0:T(8,128)(2,1)S(1)} %get-tuple-element.134, bf16[512,512]{1,0:T(8,128)(2,1)S(1)} %get-tuple-element.67, bf16[512,512]{1,0:T(8,128)(2,1)S(1)} %get-tuple-element.68, f32[512,512]{0,1:T(8,128)S(1)} %copy-done.3, ...), kind=kOutput, calls=%fused_computation.12 | convolution fusion | flops 554172416 | bytes 4263936 | tf_op jit(solution)/shard_map/dot_general | solution.py:43
  183.1 0.0 copy-done.4
  183.2 4.5 %fusion.72 = (bf16[512,1,512]{0,2,1:T(8,128)(2,1)S(1)}, bf16[512,1,512]{0,2,1:T(8,128)(2,1)S(1)}, bf16[512,512]{0,1:T(8,128)(2,1)}, bf16[512,1,512]{0,2,1:T(8,128)(2,1)S(1)}) fusion(f32[512,512]{0,1:T(8,128)S(1)} %fusion.2, f32[512,3,512]{0,2,1:T(8,128)S(1)} %bitcast.154, bf16[512,512]{0,1:T(8,128)(2,1)S(1)} %copy-done.4, f32[512,512]{0,1:T(8,128)S(1)} %copy-done.2, ...), kind=kOutput, calls=%fused_computation.151 | convolution fusion | flops 556531712 | bytes 10031104 | tf_op jit(solution)/shard_map/dot_general | solution.py:43
  187.7 0.2 pad_maximum_fusion.2
  187.9 1.6 copy.21.gp_ref
  189.4 0.0 copy-start.5
  189.4 85.6 %shard_map.79 = bf16[512,2048]{1,0:T(8,128)(2,1)} custom-call(bf16[512,1536]{1,0:T(8,128)(2,1)} %copy.21.gp_ref, bf16[8192,1536]{1,0:T(8,128)(2,1)} %shard_map.77.w_hbm), custom_call_target="tpu_custom_call" | custom-call | flops 12884901888 | bytes 28835840 | tf_op jit(solution)/shard_map/pallas_call | solution.py:221
  275.1 0.0 copy-done.5
  275.1 1.0 copy.22
  276.1 3.2 %copy.25 = bf16[512,2048]{1,0:T(8,128)(2,1)} copy(bf16[512,2048]{1,0:T(8,128)(2,1)} %shard_map.79) | data formatting | bytes 4194304
  (15 shorter events, 0.2 us)
Async XLA Ops:
  124.8 24.9 %copy-start.6 = (f32[16,512]{1,0:T(8,128)S(1)}, f32[16,512]{1,0:T(8,128)}, u32[]{:S(2)}) copy-start(f32[16,512]{1,0:T(8,128)} %param.9) | copy-start | bytes 98308
  125.6 26.2 %copy-start.7 = (f32[16,512]{1,0:T(8,128)S(1)}, f32[16,512]{1,0:T(8,128)}, u32[]{:S(2)}) copy-start(f32[16,512]{1,0:T(8,128)} %param.8) | copy-start | bytes 98308
  164.9 7.0 %copy-start.2 = (f32[512,512]{0,1:T(8,128)S(1)}, f32[512,512]{0,1:T(8,128)}, u32[]{:S(2)}) copy-start(f32[512,512]{0,1:T(8,128)} %get-tuple-element.59) | copy-start | bytes 3145732
  171.8 1.3 copy-start
  171.9 5.6 %copy-start.3 = (f32[512,512]{0,1:T(8,128)S(1)}, f32[512,512]{0,1:T(8,128)}, u32[]{:S(2)}) copy-start(f32[512,512]{0,1:T(8,128)} %get-tuple-element.58) | copy-start | bytes 3145732
  177.5 1.6 copy-start.1
  177.5 1.6 slice-start
  179.1 0.7 copy-start.8
  179.8 3.4 %copy-start.4 = (bf16[512,512]{0,1:T(8,128)(2,1)S(1)}, bf16[512,512]{0,1:T(8,128)(2,1)}, u32[]{:S(2)}) copy-start(bf16[512,512]{0,1:T(8,128)(2,1)} %copy.19) | copy-start | bytes 1572868
  189.4 85.7 %copy-start.5 = (bf16[512,512]{0,1:T(8,128)(2,1)S(1)}, bf16[512,512]{0,1:T(8,128)(2,1)}, u32[]{:S(2)}) copy-start(bf16[512,512]{0,1:T(8,128)(2,1)} %get-tuple-element.66) | copy-start | bytes 1572868

commit v6 on v5

--- a/solution.py
+++ b/solution.py
@@ -16,19 +16,36 @@
 
 def dft_tables(block_len, flip=False):
     n_len = 2 * block_len
-    k = jnp.arange(block_len, dtype=jnp.int32)[:, None]
-    n = jnp.arange(block_len, dtype=jnp.int32)[None, :]
+    low = 32
+    high = block_len // low
+    n = jnp.arange(block_len, dtype=jnp.int32)
     if flip:
         n = block_len - 1 - n
-    phase = (k * n) % n_len
-    angle = (2.0 * math.pi / n_len) * phase.astype(f32)
-    cos_rows = jnp.cos(angle)
-    sin_rows = jnp.sin(angle)
+
+    def trig(mult):
+        phase = (mult[:, None] * n[None, :]) % n_len
+        angle = (2.0 * math.pi / n_len) * phase.astype(f32)
+        return jnp.cos(angle), jnp.sin(angle)
+
+    ca, sa = trig(jnp.arange(high, dtype=jnp.int32) * low)
+    cb, sb = trig(jnp.arange(low, dtype=jnp.int32))
     nyquist = jnp.where(n % 2 == 0, 1.0, -1.0).astype(f32)
-    sin_rows = jnp.where(k == 0, nyquist, sin_rows)
+    first = (jnp.arange(block_len) == 0)[:, None]
+    weight = jnp.where(jnp.arange(block_len) == 0, 1.0, 2.0).astype(f32) / n_len
+
+    cos_rows = (ca[:, None, :] * cb[None] - sa[:, None, :] * sb[None]).reshape(block_len, block_len)
+    sin_rows = (sa[:, None, :] * cb[None] + ca[:, None, :] * sb[None]).reshape(block_len, block_len)
+    sin_rows = jnp.where(first, nyquist[None, :], sin_rows)
     fwd = jnp.concatenate([cos_rows, sin_rows], axis=0)
-    weight = jnp.where(k == 0, 1.0, 2.0).astype(f32) / n_len
-    inv = (jnp.concatenate([cos_rows * weight, sin_rows * weight], axis=0)).T
+
+    cos_t = (ca.T[:, :, None] * cb.T[:, None, :] - sa.T[:, :, None] * sb.T[:, None, :]).reshape(
+        block_len, block_len
+    )
+    sin_t = (sa.T[:, :, None] * cb.T[:, None, :] + ca.T[:, :, None] * sb.T[:, None, :]).reshape(
+        block_len, block_len
+    )
+    sin_t = jnp.where(first.T, nyquist[:, None], sin_t)
+    inv = jnp.concatenate([cos_t * weight[None, :], sin_t * weight[None, :]], axis=1)
     return fwd, inv
 
 

time: 285 us -> 268 us (0.940); the launches traced: 279 us -> 267 us
  other arithmetic: 31.3 us -> 17.9 us
    another operation x3, other arithmetic: 13.8 us -> 1.17 us
where the time goes in v6:
time: 268 us; the launch traced here: 267 us
  Pallas kernels  197 us (74%)
  matrix products  36.3 us (14%)
  other arithmetic  17.9 us (7%)
  local copies, waits for them, and re-layouts  15.1 us (6%)
    pallas_call x2, Pallas kernels, gather_rows(): pl.pallas_call(gather_kernel, out_shape=jax.ShapeDtypeStruct((total, widt...  111 us
    pallas_call x1, Pallas kernels, ring_reduce(): pl.pallas_call(functools.partial(ring_kernel, n), out_shape=jax.ShapeDtyp...  85.6 us
    dot_general x1, matrix products, local(): projected = jnp.dot(tokens, whole_w, preferred_element_type=f32)  20.1 us
    unnamed x22, local copies, waits for them, and re-layouts  10.2 us
    reduce_sum x1, other arithmetic, local(): jnp.sum(jnp.exp(-rates[r] * col) * grad_mix, axis=0)  8.92 us
    dot_general x2, matrix products, spectral_conv(): return jnp.dot(inv, prod, preferred_element_type=f32)  7.82 us
    dot_general x1, matrix products, local(): spec = jnp.dot(fwd, taps, precision=lax.Precision.HIGHEST)  6.93 us

profile of v6, /device:TPU:32, one launch (start us, length us, event | category | flops | bytes accessed | tf_op | source)
XLA Modules:
  0.0 267.2 jit_solution(2766184887709983490)
XLA Ops:
  0.6 1.2 slice_negate_fusion.15
  1.8 1.4 copy.16
  3.2 1.2 copy.17.shard_ref
  4.4 87.2 %shard_map.77.w_hbm = bf16[8192,1536]{1,0:T(8,128)(2,1)} custom-call(bf16[256,1536]{1,0:T(8,128)(2,1)} %copy.17.shard_ref), custom_call_target="tpu_custom_call" | custom-call | bytes 50331648 | tf_op jit(solution)/shard_map/pallas_call | solution.py:155
  91.6 20.1 %convolution_convert_fusion = bf16[512,1536]{1,0:T(8,128)(2,1)} fusion(bf16[512,8192]{1,0:T(8,128)(2,1)} %param.6, bf16[8192,1536]{1,0:T(8,128)(2,1)} %shard_map.77.w_hbm), kind=kOutput, calls=%fused_computation | convolution fusion | flops 12885688320 | bytes 35127296 | tf_op jit(solution)/shard_map/dot_general | solution.py:277
  111.7 1.7 copy.18
  113.4 2.0 copy.19
  115.5 8.9 %multiply_reduce_fusion = (f32[512]{0:T(512)S(1)}, f32[512]{0:T(512)S(1)}, f32[512]{0:T(512)S(1)}, f32[512]{0:T(512)S(1)}, f32[512]{0:T(512)S(1)}, /*index=5*/f3...) fusion(f32[512]{0:T(512)S(1)} %bitcast.251, ...), kind=kLoop, calls=%fused_computation.61 | loop fusion | flops 25935872 | bytes 5867520 | tf_op jit(solution)/shard_map/reduce_sum | solution.py:300
  124.4 0.0 copy-start.6
  124.4 0.1 stack.143
  124.5 0.1 stack.161
  124.6 0.6 pad_maximum_fusion.3
  125.2 0.0 copy-start.7
  125.2 24.1 %shard_map.78 = f32[1024,512]{1,0:T(8,128)} custom-call(f32[32,512]{1,0:T(8,128)} %bitcast.188), custom_call_target="tpu_custom_call" | custom-call | bytes 2097152 | tf_op jit(solution)/shard_map/pallas_call | solution.py:155
  149.3 0.0 copy-done.6
  149.4 2.1 fusion.8
  151.4 0.0 copy-done.7
  151.6 0.3 fusion.156
  151.9 0.3 fusion.142
  152.2 0.3 fusion.139
  152.5 0.3 fusion.140
  152.7 0.5 multiply_subtract_fusion.1
  153.2 0.1 bitcast_select_fusion.2
  153.4 0.0 copy-start.2
  153.4 6.9 %fusion = f32[1024,512]{1,0:T(8,128)S(1)} fusion(f32[512,512]{1,0:T(8,128)S(1)} %bitcast_select_fusion.2, f32[512,512]{1,0:T(8,128)S(1)} %bitcast.181, f32[512]{0:T(512)S(1)} %bitcast.252, f32[512]{0:T(512)S(1)} %bitcast.288, f32[512]{0:T(512)S(1)} %bitcast.196, f32[512]{0:T(512)S(1)} %bitcast.289, f32[512]{0:T(512)S(1)} %bitcast.200, f32[512]{0:T(512)S(1)} %bitcast.290, ...), kind=kOutput, calls=%fused_computation.2 | convolution fusion | flops 3234070528 | bytes 4259840 | tf_op jit(solution)/shard_map/dot_general | solution.py:327
  160.3 0.0 copy-start
  160.3 0.0 copy-done.2
  160.3 0.8 fusion.5
  161.1 0.5 copy-done
  161.6 0.0 copy-start.3
  161.6 0.1 multiply_add_fusion
  161.8 0.1 fusion.27
  161.9 0.9 copy-done.3
  162.9 0.0 copy-start.1
  162.9 0.0 slice-start
  162.9 0.7 fusion.20
  163.6 0.8 copy-done.1
  164.5 0.0 slice-done
  164.5 0.6 subtract_convert_fusion.2
  165.1 0.2 fusion.178
  165.4 0.3 fusion.160
  165.7 0.3 fusion.148
  166.0 0.3 fusion.145
  166.2 0.3 fusion.146
  166.5 0.6 multiply_subtract_fusion
  167.1 0.0 copy-start.8
  167.1 0.4 fusion.29
  167.6 0.3 copy-done.8
  167.8 0.0 copy-start.4
  167.8 3.3 %fusion.2 = f32[512,512]{0,1:T(8,128)S(1)} fusion(bf16[512,512]{0,1:T(8,128)(2,1)S(1)} %get-tuple-element.142, bf16[512,512]{0,1:T(8,128)(2,1)S(1)} %get-tuple-element.148, bf16[512,512]{1,0:T(8,128)(2,1)S(1)} %get-tuple-element.67, bf16[512,512]{1,0:T(8,128)(2,1)S(1)} %get-tuple-element.68, f32[512,512]{0,1:T(8,128)S(1)} %copy-done.3, ...), kind=kOutput, calls=%fused_computation.6 | convolution fusion | flops 554172416 | bytes 4263936 | tf_op jit(solution)/shard_map/dot_general | solution.py:60
  171.1 0.0 copy-done.4
  171.2 4.5 %fusion.66 = (bf16[512,1,512]{0,2,1:T(8,128)(2,1)S(1)}, bf16[512,1,512]{0,2,1:T(8,128)(2,1)S(1)}, bf16[512,512]{0,1:T(8,128)(2,1)}, bf16[512,1,512]{0,2,1:T(8,128)(2,1)S(1)}) fusion(f32[512,512]{0,1:T(8,128)S(1)} %fusion.2, f32[512,3,512]{0,2,1:T(8,128)S(1)} %bitcast.184, bf16[512,512]{0,1:T(8,128)(2,1)S(1)} %copy-done.4, f32[512,512]{0,1:T(8,128)S(1)} %copy-done.2, ...), kind=kOutput, calls=%fused_computation.147 | convolution fusion | flops 556531712 | bytes 10031104 | tf_op jit(solution)/shard_map/dot_general | solution.py:60
  175.7 0.2 pad_maximum_fusion.2
  175.8 1.6 copy.21.gp_ref
  177.4 0.0 copy-start.5
  177.4 85.6 %shard_map.79 = bf16[512,2048]{1,0:T(8,128)(2,1)} custom-call(bf16[512,1536]{1,0:T(8,128)(2,1)} %copy.21.gp_ref, bf16[8192,1536]{1,0:T(8,128)(2,1)} %shard_map.77.w_hbm), custom_call_target="tpu_custom_call" | custom-call | flops 12884901888 | bytes 28835840 | tf_op jit(solution)/shard_map/pallas_call | solution.py:238
  263.0 0.0 copy-done.5
  263.0 1.0 copy.22
  264.0 3.2 %copy.25 = bf16[512,2048]{1,0:T(8,128)(2,1)} copy(bf16[512,2048]{1,0:T(8,128)(2,1)} %shard_map.79) | data formatting | bytes 4194304
  (15 shorter events, 0.2 us)
Async XLA Ops:
  124.4 24.9 %copy-start.6 = (f32[16,512]{1,0:T(8,128)S(1)}, f32[16,512]{1,0:T(8,128)}, u32[]{:S(2)}) copy-start(f32[16,512]{1,0:T(8,128)} %param.9) | copy-start | bytes 98308
  125.2 26.2 %copy-start.7 = (f32[16,512]{1,0:T(8,128)S(1)}, f32[16,512]{1,0:T(8,128)}, u32[]{:S(2)}) copy-start(f32[16,512]{1,0:T(8,128)} %param.8) | copy-start | bytes 98308
  153.4 7.0 %copy-start.2 = (f32[512,512]{0,1:T(8,128)S(1)}, f32[512,512]{0,1:T(8,128)}, u32[]{:S(2)}) copy-start(f32[512,512]{0,1:T(8,128)} %get-tuple-element.59) | copy-start | bytes 3145732
  160.3 1.3 copy-start
  161.6 1.2 copy-start.3
  162.9 1.6 copy-start.1
  162.9 1.6 slice-start
  167.1 0.7 copy-start.8
  167.8 3.3 %copy-start.4 = (bf16[512,512]{0,1:T(8,128)(2,1)S(1)}, bf16[512,512]{0,1:T(8,128)(2,1)}, u32[]{:S(2)}) copy-start(bf16[512,512]{0,1:T(8,128)(2,1)} %copy.19) | copy-start | bytes 1572868
  177.4 85.6 %copy-start.5 = (bf16[512,512]{0,1:T(8,128)(2,1)S(1)}, bf16[512,512]{0,1:T(8,128)(2,1)}, u32[]{:S(2)}) copy-start(bf16[512,512]{0,1:T(8,128)(2,1)} %get-tuple-element.66) | copy-start | bytes 1572868

commit v7 on v6

--- a/solution.py
+++ b/solution.py
@@ -167,6 +167,63 @@
     )(shard)
 
 
+def state_kernel(st_ref, out_ref, send_sem, recv_sem):
+    count = out_ref.shape[0]
+    side = 4
+    me = (lax.axis_index("x") * side + lax.axis_index("y")) * 2 + lax.axis_index("core")
+
+    def device(j):
+        return {"x": j // (2 * side), "y": (j // 2) % side, "core": j % 2}
+
+    barrier = pltpu.get_barrier_semaphore()
+
+    def greet(o, carry):
+        pl.semaphore_signal(barrier, inc=1, device_id=device(lax.rem(me + o, count)), device_id_type=MESH)
+        return carry
+
+    lax.fori_loop(1, count, greet, 0)
+    pl.semaphore_wait(barrier, count - 1)
+
+    def copy(o):
+        j = lax.rem(me + o, count)
+        return pltpu.make_async_remote_copy(
+            src_ref=st_ref.at[(me + o) // count],
+            dst_ref=out_ref.at[me],
+            send_sem=send_sem.at[o - 1],
+            recv_sem=recv_sem.at[o - 1],
+            device_id=device(j),
+            device_id_type=MESH,
+        )
+
+    def start(o, carry):
+        copy(o).start()
+        return carry
+
+    lax.fori_loop(1, count, start, 0)
+    out_ref[me] = jnp.zeros(out_ref.shape[1:], out_ref.dtype)
+
+    def finish(o, carry):
+        cp = copy(o)
+        cp.wait_send()
+        cp.wait_recv()
+        return carry
+
+    lax.fori_loop(1, count, finish, 0)
+
+
+def exchange_states(states):
+    count = lax.axis_size(SEQ)
+    return pl.pallas_call(
+        state_kernel,
+        out_shape=jax.ShapeDtypeStruct((count,) + states.shape[1:], states.dtype),
+        in_specs=[pl.BlockSpec(memory_space=pltpu.VMEM)],
+        out_specs=pl.BlockSpec(memory_space=pltpu.VMEM),
+        scratch_shapes=[pltpu.SemaphoreType.DMA((count - 1,)), pltpu.SemaphoreType.DMA((count - 1,))],
+        compiler_params=pltpu.CompilerParams(collective_id=2, has_side_effects=True),
+        cost_estimate=pl.CostEstimate(flops=0, bytes_accessed=8 * states[0].size * count, transcendentals=0),
+    )(states)
+
+
 def ring_kernel(n, gp_ref, w_hbm, out_ref, wbuf, acc, snd, rcv, wsem, send_sem, recv_sem):
     me = lax.axis_index("chan")
     right = lax.rem(me + 1, n)
@@ -300,7 +357,7 @@
         [jnp.sum(jnp.exp(-rates[r] * col) * grad_mix, axis=0) for r in range(modes)]
     )
     states = jnp.stack([end_fwd, end_bwd])
-    every = gather_rows(states.reshape(2 * modes, chan_count), 2).reshape(seq_count, 2, modes, chan_count)
+    every = exchange_states(states)
 
     others = jnp.arange(seq_count, dtype=jnp.int32)
     gap_f = me - 1 - others
@@ -316,8 +373,8 @@
         jnp.exp(-span * jnp.maximum(gap_b, 0).astype(f32)[:, None, None]),
         0.0,
     )
-    into_f = jnp.sum(w_f * every[:, 0], axis=0) * mode_gain
-    into_b = jnp.sum(w_b * every[:, 1], axis=0) * mode_gain
+    into_f = jnp.sum(w_f * every, axis=0) * mode_gain
+    into_b = jnp.sum(w_b * every, axis=0) * mode_gain
 
     taps = mode_sum(mode_gain, rates, col)
     fwd, inv = dft_tables(tok_rows)

time: 268 us -> 266 us (level); the launches traced: 267 us -> 262 us
  Pallas kernels: 197 us -> 192 us
    pallas_call x2 -> x1, Pallas kernels: 111 us -> 87.2 us  [gather_rows(): pl.pallas_call(gather_kernel, out_shape=jax.ShapeDtypeStruct((total, widt...]
    pallas_call x0 -> x1, Pallas kernels: none -> 21.6 us  [exchange_states(): pl.pallas_call(state_kernel, out_shape=jax.ShapeDtypeStruct((count,) + st...]
where the time goes in v7:
time: 266 us; the launch traced here: 262 us
  Pallas kernels  192 us (72%)
  matrix products  36.3 us (14%)
  other arithmetic  17.6 us (7%)
  local copies, waits for them, and re-layouts  14.9 us (6%)
    pallas_call x1, Pallas kernels, gather_rows(): pl.pallas_call(gather_kernel, out_shape=jax.ShapeDtypeStruct((total, widt...  87.2 us
    pallas_call x1, Pallas kernels, ring_reduce(): pl.pallas_call(functools.partial(ring_kernel, n), out_shape=jax.ShapeDtyp...  83.4 us
    pallas_call x1, Pallas kernels, exchange_states(): pl.pallas_call(state_kernel, out_shape=jax.ShapeDtypeStruct((count,) + st...  21.6 us
    dot_general x1, matrix products, local(): projected = jnp.dot(tokens, whole_w, preferred_element_type=f32)  20.1 us
    unnamed x22, local copies, waits for them, and re-layouts  10.2 us
    reduce_sum x1, other arithmetic, local(): jnp.sum(jnp.exp(-rates[r] * col) * grad_mix, axis=0)  8.93 us
    dot_general x2, matrix products, spectral_conv(): return jnp.dot(inv, prod, preferred_element_type=f32)  7.81 us
    dot_general x1, matrix products, local(): spec = jnp.dot(fwd, taps, precision=lax.Precision.HIGHEST)  6.93 us

profile of v7, /device:TPU:32, one launch (start us, length us, event | category | flops | bytes accessed | tf_op | source)
XLA Modules:
  0.0 262.1 jit_solution(13388645204634838500)
XLA Ops:
  0.6 1.1 slice_negate_fusion.15
  1.7 1.4 copy.15
  3.1 1.2 copy.16.shard_ref
  4.3 87.2 %shard_map.77.w_hbm = bf16[8192,1536]{1,0:T(8,128)(2,1)} custom-call(bf16[256,1536]{1,0:T(8,128)(2,1)} %copy.16.shard_ref), custom_call_target="tpu_custom_call" | custom-call | bytes 50331648 | tf_op jit(solution)/shard_map/pallas_call | solution.py:155
  91.5 20.1 %convolution_convert_fusion = bf16[512,1536]{1,0:T(8,128)(2,1)} fusion(bf16[512,8192]{1,0:T(8,128)(2,1)} %param.6, bf16[8192,1536]{1,0:T(8,128)(2,1)} %shard_map.77.w_hbm), kind=kOutput, calls=%fused_computation | convolution fusion | flops 12885688320 | bytes 35127296 | tf_op jit(solution)/shard_map/dot_general | solution.py:334
  111.6 1.7 copy.17
  113.3 2.0 copy.18
  115.3 0.0 copy-start.6
  115.4 8.9 %multiply_reduce_fusion.2 = (f32[512]{0:T(512)S(1)}, f32[512]{0:T(512)S(1)}, f32[512]{0:T(512)S(1)}, f32[512]{0:T(512)S(1)}, f32[512]{0:T(512)S(1)}, /*index=5*/...) fusion(f32[512]{0:T(512)S(1)} %bitcast.233, ...), kind=kLoop, calls=%fused_computation.57 | loop fusion | flops 25935872 | bytes 5867520 | tf_op jit(solution)/shard_map/reduce_sum | solution.py:357
  124.3 0.0 copy-start.7
  124.3 0.1 stack.143
  124.4 0.1 stack.161
  124.5 0.6 pad_maximum_fusion.3.st_ref
  125.1 21.6 %shard_map.78 = f32[32,16,512]{2,1,0:T(8,128)} custom-call(f32[2,16,512]{2,1,0:T(8,128)} %pad_maximum_fusion.3.st_ref), custom_call_target="tpu_custom_call" | custom-call | bytes 2097152 | tf_op jit(solution)/shard_map/pallas_call | solution.py:216
  146.8 0.0 copy-done.6
  146.8 1.7 multiply_reduce_fusion
  148.5 0.0 copy-done.7
  148.7 0.3 fusion.152
  149.0 0.3 fusion.138
  149.3 0.3 fusion.135
  149.6 0.3 fusion.136
  149.8 0.5 multiply_subtract_fusion.1
  150.3 0.1 bitcast_select_fusion.2
  150.5 0.0 copy-start.2
  150.5 6.9 %fusion = f32[1024,512]{1,0:T(8,128)S(1)} fusion(f32[512,512]{1,0:T(8,128)S(1)} %bitcast_select_fusion.2, f32[512,512]{1,0:T(8,128)S(1)} %bitcast.164, f32[512]{0:T(512)S(1)} %bitcast.234, f32[512]{0:T(512)S(1)} %bitcast.270, f32[512]{0:T(512)S(1)} %bitcast.178, f32[512]{0:T(512)S(1)} %bitcast.271, f32[512]{0:T(512)S(1)} %bitcast.182, f32[512]{0:T(512)S(1)} %bitcast.272, ...), kind=kOutput, calls=%fused_computation.2 | convolution fusion | flops 3234070528 | bytes 4259840 | tf_op jit(solution)/shard_map/dot_general | solution.py:384
  157.4 0.0 copy-start
  157.4 0.0 copy-done.2
  157.4 0.8 fusion.5
  158.2 0.5 copy-done
  158.7 0.0 copy-start.3
  158.7 0.1 multiply_add_fusion
  158.9 0.1 fusion.23
  159.0 0.9 copy-done.3
  160.0 0.0 copy-start.1
  160.0 0.0 slice-start
  160.0 0.7 fusion.16
  160.7 0.8 copy-done.1
  161.6 0.0 slice-done
  161.6 0.6 subtract_convert_fusion.2
  162.2 0.3 fusion.156
  162.6 0.3 fusion.144
  162.9 0.5 fusion.141
  163.3 0.3 fusion.142
  163.6 0.6 multiply_subtract_fusion
  164.2 0.0 copy-start.8
  164.2 0.4 fusion.25
  164.7 0.3 copy-done.8
  164.9 0.0 copy-start.4
  164.9 3.3 %fusion.2 = f32[512,512]{0,1:T(8,128)S(1)} fusion(bf16[512,512]{0,1:T(8,128)(2,1)S(1)} %get-tuple-element.142, bf16[512,512]{0,1:T(8,128)(2,1)S(1)} %get-tuple-element.148, bf16[512,512]{1,0:T(8,128)(2,1)S(1)} %get-tuple-element.67, bf16[512,512]{1,0:T(8,128)(2,1)S(1)} %get-tuple-element.68, f32[512,512]{0,1:T(8,128)S(1)} %copy-done.3, ...), kind=kOutput, calls=%fused_computation.6 | convolution fusion | flops 554172416 | bytes 4263936 | tf_op jit(solution)/shard_map/dot_general | solution.py:60
  168.2 0.0 copy-done.4
  168.3 4.5 %fusion.62 = (bf16[512,1,512]{0,2,1:T(8,128)(2,1)S(1)}, bf16[512,1,512]{0,2,1:T(8,128)(2,1)S(1)}, bf16[512,512]{0,1:T(8,128)(2,1)}, bf16[512,1,512]{0,2,1:T(8,128)(2,1)S(1)}) fusion(f32[512,512]{0,1:T(8,128)S(1)} %fusion.2, f32[512,3,512]{0,2,1:T(8,128)S(1)} %bitcast.167, bf16[512,512]{0,1:T(8,128)(2,1)S(1)} %copy-done.4, f32[512,512]{0,1:T(8,128)S(1)} %copy-done.2, ...), kind=kOutput, calls=%fused_computation.143 | convolution fusion | flops 556531712 | bytes 10031104 | tf_op jit(solution)/shard_map/dot_general | solution.py:60
  172.8 0.2 pad_maximum_fusion.2
  172.9 1.6 copy.19.gp_ref
  174.5 0.0 copy-start.5
  174.5 83.4 %shard_map.79 = bf16[512,2048]{1,0:T(8,128)(2,1)} custom-call(bf16[512,1536]{1,0:T(8,128)(2,1)} %copy.19.gp_ref, bf16[8192,1536]{1,0:T(8,128)(2,1)} %shard_map.77.w_hbm), custom_call_target="tpu_custom_call" | custom-call | flops 12884901888 | bytes 28835840 | tf_op jit(solution)/shard_map/pallas_call | solution.py:295
  257.9 0.0 copy-done.5
  257.9 1.0 copy.20
  258.9 3.2 %copy.22 = bf16[512,2048]{1,0:T(8,128)(2,1)} copy(bf16[512,2048]{1,0:T(8,128)(2,1)} %shard_map.79) | data formatting | bytes 4194304
  (16 shorter events, 0.2 us)
Async XLA Ops:
  115.3 31.4 %copy-start.6 = (f32[16,512]{1,0:T(8,128)S(1)}, f32[16,512]{1,0:T(8,128)}, u32[]{:S(2)}) copy-start(f32[16,512]{1,0:T(8,128)} %param.9) | copy-start | bytes 98308
  124.3 24.2 %copy-start.7 = (f32[16,512]{1,0:T(8,128)S(1)}, f32[16,512]{1,0:T(8,128)}, u32[]{:S(2)}) copy-start(f32[16,512]{1,0:T(8,128)} %param.8) | copy-start | bytes 98308
  150.5 7.0 %copy-start.2 = (f32[512,512]{0,1:T(8,128)S(1)}, f32[512,512]{0,1:T(8,128)}, u32[]{:S(2)}) copy-start(f32[512,512]{0,1:T(8,128)} %get-tuple-element.59) | copy-start | bytes 3145732
  157.4 1.3 copy-start
  158.7 1.2 copy-start.3
  160.0 1.6 copy-start.1
  160.0 1.6 slice-start
  164.2 0.7 copy-start.8
  164.9 3.3 %copy-start.4 = (bf16[512,512]{0,1:T(8,128)(2,1)S(1)}, bf16[512,512]{0,1:T(8,128)(2,1)}, u32[]{:S(2)}) copy-start(bf16[512,512]{0,1:T(8,128)(2,1)} %copy.18) | copy-start | bytes 1572868
  174.5 83.4 %copy-start.5 = (bf16[512,512]{0,1:T(8,128)(2,1)S(1)}, bf16[512,512]{0,1:T(8,128)(2,1)}, u32[]{:S(2)}) copy-start(bf16[512,512]{0,1:T(8,128)(2,1)} %get-tuple-element.66) | copy-start | bytes 1572868

commit v8 on v7

--- a/solution.py
+++ b/solution.py
@@ -75,22 +75,23 @@
         b = lax.rem(b + 2 * side, side)
         return a * other + b * core, b * other + a * core
 
-    def slot(a, b, c):
+    def slot(a, b):
         xx, yy = coords(a, b)
-        return out_hbm.at[pl.ds(pl.multiple_of(((xx * side + yy) * 2 + c) * rows, rows), rows)]
+        return out_hbm.at[pl.ds(pl.multiple_of(((xx * side + yy) * 2 + core) * rows, rows), rows)]
 
     def device(a, b, c):
         xx, yy = coords(a, b)
         return {"x": xx, "y": yy, "core": c}
 
+    partner = device(a0, b0, other)
     peers = [device(a0 + 1, b0, core), device(a0 - 1, b0, core), device(a0, b0 + 1, core),
-             device(a0, b0 - 1, core), device(a0, b0, other)]
+             device(a0, b0 - 1, core), partner]
     barrier = pltpu.get_barrier_semaphore()
     for peer in peers:
         pl.semaphore_signal(barrier, inc=1, device_id=peer, device_id_type=MESH)
     pl.semaphore_wait(barrier, len(peers))
 
-    sent = []
+    sent = {}
 
     def push(src, dst, target, index):
         cp = pltpu.make_async_remote_copy(
@@ -98,55 +99,55 @@
             device_id=target, device_id_type=MESH,
         )
         cp.start()
-        sent.append(cp)
+        sent[index] = cp
         return cp
 
-    mine = slot(a0, b0, core)
+    def along_b(j):
+        src = slot(a0 + j, b0)
+        push(src, src, device(a0, b0 + 1, core), 3 + j)
+        push(src, src, device(a0, b0 - 1, core), 7 + j)
+
+    mine = slot(a0, b0)
     own = pltpu.make_async_copy(shard_ref, mine, local_sem.at[0])
     own.start()
-    partner = device(a0, b0, other)
     up = push(shard_ref, mine, device(a0 + 1, b0, core), 0)
     down = push(shard_ref, mine, device(a0 - 1, b0, core), 1)
     own.wait()
+    along_b(0)
     push(mine, mine, partner, 15)
     up.wait_recv()
-    fwd = push(slot(a0 - 1, b0, core), slot(a0 - 1, b0, core), device(a0 + 1, b0, core), 2)
-    push(slot(a0 - 1, b0, core), slot(a0 - 1, b0, core), partner, 16)
+    fwd = push(slot(a0 - 1, b0), slot(a0 - 1, b0), device(a0 + 1, b0, core), 2)
+    along_b(3)
+    push(slot(a0 - 1, b0), slot(a0 - 1, b0), partner, 16)
     down.wait_recv()
-    push(slot(a0 + 1, b0, core), slot(a0 + 1, b0, core), partner, 17)
+    along_b(1)
+    push(slot(a0 + 1, b0), slot(a0 + 1, b0), partner, 17)
     fwd.wait_recv()
-    push(slot(a0 + 2, b0, core), slot(a0 + 2, b0, core), partner, 18)
-    outs = []
-    for j in range(side):
-        src = slot(a0 + j, b0, core)
-        outs.append(push(src, src, device(a0, b0 + 1, core), 3 + j))
-    for j in range(side):
-        src = slot(a0 + j, b0, core)
-        outs.append(push(src, src, device(a0, b0 - 1, core), 7 + j))
-    later = []
-    for j in range(side):
-        outs[j].wait_recv()
-        src = slot(a0 + j, b0 - 1, core)
+    along_b(2)
+    push(slot(a0 + 2, b0), slot(a0 + 2, b0), partner, 18)
+    later = {}
+    for j in (0, 3, 1, 2):
+        sent[3 + j].wait_recv()
+        src = slot(a0 + j, b0 - 1)
         if j < 2:
-            later.append(push(src, src, device(a0, b0 + 1, core), 11 + j))
+            later[j] = push(src, src, device(a0, b0 + 1, core), 11 + j)
         push(src, src, partner, 19 + j)
-    for j in range(side):
-        outs[side + j].wait_recv()
-        src = slot(a0 + j, b0 + 1, core)
+        sent[7 + j].wait_recv()
+        src = slot(a0 + j, b0 + 1)
         if j >= 2:
-            later.append(push(src, src, device(a0, b0 - 1, core), 11 + j))
+            later[j] = push(src, src, device(a0, b0 - 1, core), 11 + j)
         push(src, src, partner, 23 + j)
-    for j in range(side):
+    for j in (0, 3, 1, 2):
         later[j].wait_recv()
-        src = slot(a0 + j, b0 + 2, core)
+        src = slot(a0 + j, b0 + 2)
         push(src, src, partner, 27 + j)
-    for cp in sent:
-        cp.wait_send()
     for index in range(15, 31):
         pltpu.make_async_remote_copy(
             src_ref=mine, dst_ref=mine, send_sem=send_sem.at[index], recv_sem=recv_sem.at[index],
             device_id=partner, device_id_type=MESH,
         ).wait_recv()
+    for index in sorted(sent):
+        sent[index].wait_send()
 
 
 def gather_rows(shard, collective):
@@ -163,7 +164,7 @@
             pltpu.SemaphoreType.DMA((1,)),
         ],
         compiler_params=pltpu.CompilerParams(collective_id=collective, has_side_effects=True),
-        cost_estimate=pl.CostEstimate(flops=0, bytes_accessed=2 * total * width * 2, transcendentals=0),
+        cost_estimate=pl.CostEstimate(flops=0, bytes_accessed=4 * total * width, transcendentals=0),
     )(shard)
 
 

time: 266 us -> 257 us (0.966)
  Pallas kernels: 192 us -> 186 us
    pallas_call x1, Pallas kernels: 87.2 us -> 79.6 us  [gather_rows(): pl.pallas_call(gather_kernel, out_shape=jax.ShapeDtypeStruct((total, widt...]
where the time goes in v8:
time: 257 us; the launch traced here: 256 us
  Pallas kernels  186 us (72%)
  matrix products  36.3 us (14%)
  other arithmetic  17.6 us (7%)
  local copies, waits for them, and re-layouts  14.9 us (6%)
    pallas_call x1, Pallas kernels, ring_reduce(): pl.pallas_call(functools.partial(ring_kernel, n), out_shape=jax.ShapeDtyp...  86 us
    pallas_call x1, Pallas kernels, gather_rows(): pl.pallas_call(gather_kernel, out_shape=jax.ShapeDtypeStruct((total, widt...  79.6 us
    pallas_call x1, Pallas kernels, exchange_states(): pl.pallas_call(state_kernel, out_shape=jax.ShapeDtypeStruct((count,) + st...  20.2 us
    dot_general x1, matrix products, local(): projected = jnp.dot(tokens, whole_w, preferred_element_type=f32)  20.1 us
    unnamed x22, local copies, waits for them, and re-layouts  10.2 us
    reduce_sum x1, other arithmetic, local(): jnp.sum(jnp.exp(-rates[r] * col) * grad_mix, axis=0)  8.93 us
    dot_general x2, matrix products, spectral_conv(): return jnp.dot(inv, prod, preferred_element_type=f32)  7.81 us
    dot_general x1, matrix products, local(): spec = jnp.dot(fwd, taps, precision=lax.Precision.HIGHEST)  6.93 us

profile of v8, /device:TPU:32, one launch (start us, length us, event | category | flops | bytes accessed | tf_op | source)
XLA Modules:
  0.0 255.6 jit_solution(3074527795361344426)
XLA Ops:
  0.6 1.1 slice_negate_fusion.15
  1.7 1.4 copy.15
  3.1 1.2 copy.16.shard_ref
  4.3 79.6 %shard_map.77.w_hbm = bf16[8192,1536]{1,0:T(8,128)(2,1)} custom-call(bf16[256,1536]{1,0:T(8,128)(2,1)} %copy.16.shard_ref), custom_call_target="tpu_custom_call" | custom-call | bytes 50331648 | tf_op jit(solution)/shard_map/pallas_call | solution.py:156
  83.8 20.1 %convolution_convert_fusion = bf16[512,1536]{1,0:T(8,128)(2,1)} fusion(bf16[512,8192]{1,0:T(8,128)(2,1)} %param.6, bf16[8192,1536]{1,0:T(8,128)(2,1)} %shard_map.77.w_hbm), kind=kOutput, calls=%fused_computation | convolution fusion | flops 12885688320 | bytes 35127296 | tf_op jit(solution)/shard_map/dot_general | solution.py:335
  103.9 1.7 copy.17
  105.7 2.0 copy.18
  107.7 0.0 copy-start.6
  107.7 8.9 %multiply_reduce_fusion.2 = (f32[512]{0:T(512)S(1)}, f32[512]{0:T(512)S(1)}, f32[512]{0:T(512)S(1)}, f32[512]{0:T(512)S(1)}, f32[512]{0:T(512)S(1)}, /*index=5*/...) fusion(f32[512]{0:T(512)S(1)} %bitcast.233, ...), kind=kLoop, calls=%fused_computation.57 | loop fusion | flops 25935872 | bytes 5867520 | tf_op jit(solution)/shard_map/reduce_sum | solution.py:358
  116.6 0.0 copy-start.7
  116.7 0.1 stack.143
  116.7 0.1 stack.161
  116.8 0.6 pad_maximum_fusion.3.st_ref
  117.5 20.2 %shard_map.78 = f32[32,16,512]{2,1,0:T(8,128)} custom-call(f32[2,16,512]{2,1,0:T(8,128)} %pad_maximum_fusion.3.st_ref), custom_call_target="tpu_custom_call" | custom-call | bytes 2097152 | tf_op jit(solution)/shard_map/pallas_call | solution.py:217
  137.7 0.0 copy-done.6
  137.7 1.7 multiply_reduce_fusion
  139.4 0.0 copy-done.7
  139.6 0.3 fusion.152
  139.9 0.3 fusion.138
  140.2 0.3 fusion.135
  140.5 0.3 fusion.136
  140.7 0.5 multiply_subtract_fusion.1
  141.2 0.1 bitcast_select_fusion.2
  141.4 0.0 copy-start.2
  141.4 6.9 %fusion = f32[1024,512]{1,0:T(8,128)S(1)} fusion(f32[512,512]{1,0:T(8,128)S(1)} %bitcast_select_fusion.2, f32[512,512]{1,0:T(8,128)S(1)} %bitcast.164, f32[512]{0:T(512)S(1)} %bitcast.234, f32[512]{0:T(512)S(1)} %bitcast.270, f32[512]{0:T(512)S(1)} %bitcast.178, f32[512]{0:T(512)S(1)} %bitcast.271, f32[512]{0:T(512)S(1)} %bitcast.182, f32[512]{0:T(512)S(1)} %bitcast.272, ...), kind=kOutput, calls=%fused_computation.2 | convolution fusion | flops 3234070528 | bytes 4259840 | tf_op jit(solution)/shard_map/dot_general | solution.py:385
  148.3 0.0 copy-start
  148.3 0.0 copy-done.2
  148.3 0.8 fusion.5
  149.1 0.5 copy-done
  149.6 0.0 copy-start.3
  149.6 0.1 multiply_add_fusion
  149.8 0.1 fusion.23
  149.9 0.9 copy-done.3
  150.9 0.0 copy-start.1
  150.9 0.0 slice-start
  150.9 0.7 fusion.16
  151.6 0.8 copy-done.1
  152.5 0.0 slice-done
  152.5 0.6 subtract_convert_fusion.2
  153.1 0.3 fusion.156
  153.5 0.3 fusion.144
  153.8 0.5 fusion.141
  154.3 0.3 fusion.142
  154.5 0.6 multiply_subtract_fusion
  155.1 0.0 copy-start.8
  155.1 0.4 fusion.25
  155.6 0.3 copy-done.8
  155.8 0.0 copy-start.4
  155.8 3.3 %fusion.2 = f32[512,512]{0,1:T(8,128)S(1)} fusion(bf16[512,512]{0,1:T(8,128)(2,1)S(1)} %get-tuple-element.142, bf16[512,512]{0,1:T(8,128)(2,1)S(1)} %get-tuple-element.148, bf16[512,512]{1,0:T(8,128)(2,1)S(1)} %get-tuple-element.67, bf16[512,512]{1,0:T(8,128)(2,1)S(1)} %get-tuple-element.68, f32[512,512]{0,1:T(8,128)S(1)} %copy-done.3, ...), kind=kOutput, calls=%fused_computation.6 | convolution fusion | flops 554172416 | bytes 4263936 | tf_op jit(solution)/shard_map/dot_general | solution.py:60
  159.2 0.0 copy-done.4
  159.2 4.5 %fusion.62 = (bf16[512,1,512]{0,2,1:T(8,128)(2,1)S(1)}, bf16[512,1,512]{0,2,1:T(8,128)(2,1)S(1)}, bf16[512,512]{0,1:T(8,128)(2,1)}, bf16[512,1,512]{0,2,1:T(8,128)(2,1)S(1)}) fusion(f32[512,512]{0,1:T(8,128)S(1)} %fusion.2, f32[512,3,512]{0,2,1:T(8,128)S(1)} %bitcast.167, bf16[512,512]{0,1:T(8,128)(2,1)S(1)} %copy-done.4, f32[512,512]{0,1:T(8,128)S(1)} %copy-done.2, ...), kind=kOutput, calls=%fused_computation.143 | convolution fusion | flops 556531712 | bytes 10031104 | tf_op jit(solution)/shard_map/dot_general | solution.py:60
  163.7 0.2 pad_maximum_fusion.2
  163.8 1.6 copy.19.gp_ref
  165.4 0.0 copy-start.5
  165.4 86.0 %shard_map.79 = bf16[512,2048]{1,0:T(8,128)(2,1)} custom-call(bf16[512,1536]{1,0:T(8,128)(2,1)} %copy.19.gp_ref, bf16[8192,1536]{1,0:T(8,128)(2,1)} %shard_map.77.w_hbm), custom_call_target="tpu_custom_call" | custom-call | flops 12884901888 | bytes 28835840 | tf_op jit(solution)/shard_map/pallas_call | solution.py:296
  251.5 0.0 copy-done.5
  251.5 1.0 copy.20
  252.5 3.2 %copy.22 = bf16[512,2048]{1,0:T(8,128)(2,1)} copy(bf16[512,2048]{1,0:T(8,128)(2,1)} %shard_map.79) | data formatting | bytes 4194304
  (16 shorter events, 0.2 us)
Async XLA Ops:
  107.7 30.0 %copy-start.6 = (f32[16,512]{1,0:T(8,128)S(1)}, f32[16,512]{1,0:T(8,128)}, u32[]{:S(2)}) copy-start(f32[16,512]{1,0:T(8,128)} %param.9) | copy-start | bytes 98308
  116.6 22.8 %copy-start.7 = (f32[16,512]{1,0:T(8,128)S(1)}, f32[16,512]{1,0:T(8,128)}, u32[]{:S(2)}) copy-start(f32[16,512]{1,0:T(8,128)} %param.8) | copy-start | bytes 98308
  141.4 7.0 %copy-start.2 = (f32[512,512]{0,1:T(8,128)S(1)}, f32[512,512]{0,1:T(8,128)}, u32[]{:S(2)}) copy-start(f32[512,512]{0,1:T(8,128)} %get-tuple-element.59) | copy-start | bytes 3145732
  148.3 1.3 copy-start
  149.6 1.2 copy-start.3
  150.9 1.6 copy-start.1
  150.9 1.6 slice-start
  155.1 0.7 copy-start.8
  155.8 3.3 %copy-start.4 = (bf16[512,512]{0,1:T(8,128)(2,1)S(1)}, bf16[512,512]{0,1:T(8,128)(2,1)}, u32[]{:S(2)}) copy-start(bf16[512,512]{0,1:T(8,128)(2,1)} %copy.18) | copy-start | bytes 1572868
  165.4 86.0 %copy-start.5 = (bf16[512,512]{0,1:T(8,128)(2,1)S(1)}, bf16[512,512]{0,1:T(8,128)(2,1)}, u32[]{:S(2)}) copy-start(bf16[512,512]{0,1:T(8,128)(2,1)} %get-tuple-element.66) | copy-start | bytes 1572868

commit v9 on v8

--- a/solution.py
+++ b/solution.py
@@ -318,11 +318,31 @@
     )(grad_proj, whole_w)
 
 
-def mode_sum(amp, rates, lag):
-    total = amp[0] * jnp.exp(-rates[0] * lag)
-    for r in range(1, rates.shape[0]):
-        total = total + amp[r] * jnp.exp(-rates[r] * lag)
-    return total
+def split_powers(rates, first, step, count_hi, low):
+    hi = jnp.arange(count_hi, dtype=f32)[:, None, None]
+    lo = jnp.arange(low, dtype=f32)[:, None, None]
+    shift = 0.0 if step > 0 else -step * low * (count_hi - 1)
+    return (
+        jnp.exp(-rates[None] * (step * low * hi + shift)),
+        jnp.exp(-rates[None] * (first - shift + step * lo)),
+    )
+
+
+def mode_sum(amp, rates, first, step, length):
+    low = 32
+    e_hi, e_lo = split_powers(rates, first, step, length // low, low)
+    scaled = amp[None] * e_hi
+    total = jnp.sum(scaled[:, None] * e_lo[None], axis=2)
+    return total.reshape(length, amp.shape[1])
+
+
+def mode_states(signal, rates, first, step):
+    low = 32
+    length = signal.shape[0]
+    e_hi, e_lo = split_powers(rates, first, step, length // low, low)
+    pieces = signal.reshape(length // low, low, 1, signal.shape[1])
+    inner = jnp.sum(pieces * e_lo[None], axis=1)
+    return jnp.sum(inner * e_hi, axis=0)
 
 
 def local(tokens, proj_weight, residues, decay_rates, skip_gain, grad_out):
@@ -350,13 +370,8 @@
     mode_gain = residues * jnp.sqrt(-jnp.expm1(-2.0 * rates))
     steps = jnp.arange(tok_rows, dtype=f32)
 
-    col = steps[:, None]
-    end_fwd = jnp.stack(
-        [jnp.sum(jnp.exp(-rates[r] * (tok_rows - 1 - col)) * mixed_in, axis=0) for r in range(modes)]
-    )
-    end_bwd = jnp.stack(
-        [jnp.sum(jnp.exp(-rates[r] * col) * grad_mix, axis=0) for r in range(modes)]
-    )
+    end_fwd = mode_states(mixed_in, rates, float(tok_rows - 1), -1.0)
+    end_bwd = mode_states(grad_mix, rates, 0.0, 1.0)
     states = jnp.stack([end_fwd, end_bwd])
     every = exchange_states(states)
 
@@ -377,7 +392,7 @@
     into_f = jnp.sum(w_f * every, axis=0) * mode_gain
     into_b = jnp.sum(w_b * every, axis=0) * mode_gain
 
-    taps = mode_sum(mode_gain, rates, col)
+    taps = mode_sum(mode_gain, rates, 0.0, 1.0, tok_rows)
     fwd, inv = dft_tables(tok_rows)
     fwd_b = fwd.astype(bf16)
     inv_b = inv.astype(bf16)
@@ -389,13 +404,13 @@
     h_b = jnp.where(row0, 0.0, spec[tok_rows:])
 
     local_f = spectral_conv(mixed_in, fwd_b, inv_b, h_a, h_a2, h_b)
-    carry_f = mode_sum(into_f, rates, col + 1.0)
+    carry_f = mode_sum(into_f, rates, 1.0, 1.0, tok_rows)
     filtered = local_f + carry_f + skip_gain[None, :] * mixed_in
     gated_output = (query_in * filtered).astype(bf16)
     grad_query = grad_gate * filtered
 
     local_b = spectral_conv(grad_mix, fwd_r.astype(bf16), inv_r.astype(bf16), h_a, h_a2, h_b)
-    carry_b = mode_sum(into_b, rates, tok_rows - col)
+    carry_b = mode_sum(into_b, rates, float(tok_rows), -1.0, tok_rows)
     grad_conv = local_b + carry_b + skip_gain[None, :] * grad_mix
 
     grad_proj = jnp.stack([grad_query, grad_conv * value_in, grad_conv * key_in], axis=1).astype(bf16)

time: 257 us -> 301 us (1.17)
  the two profiles are of different devices: /device:TPU:32 before, /device:TPU:48 now
where the time goes in v9:
time: 301 us; the launch traced here: 295 us
  Pallas kernels  187 us (62%)
  other arithmetic  50.9 us (17%)
  matrix products  31.1 us (10%)
  local copies, waits for them, and re-layouts  25 us (8%)
    pallas_call x1, Pallas kernels, ring_reduce(): pl.pallas_call(functools.partial(ring_kernel, n), out_shape=jax.ShapeDtyp...  86.3 us
    pallas_call x1, Pallas kernels, gather_rows(): pl.pallas_call(gather_kernel, out_shape=jax.ShapeDtypeStruct((total, widt...  77.9 us
    pallas_call x1, Pallas kernels, exchange_states(): pl.pallas_call(state_kernel, out_shape=jax.ShapeDtypeStruct((count,) + st...  23 us
    dot_general x1, matrix products, local(): projected = jnp.dot(tokens, whole_w, preferred_element_type=f32)  20.1 us
    reduce_sum x2, other arithmetic, mode_sum(): total = jnp.sum(scaled[:, None] * e_lo[None], axis=2)  18.7 us
    reduce_sum x1, other arithmetic, mode_states(): inner = jnp.sum(pieces * e_lo[None], axis=1)  12.9 us
    unnamed x40, local copies, waits for them, and re-layouts  9.82 us
    dot_general x2, matrix products, spectral_conv(): return jnp.dot(inv, prod, preferred_element_type=f32)  6.07 us

profile of v9, /device:TPU:48, one launch (start us, length us, event | category | flops | bytes accessed | tf_op | source)
XLA Modules:
  0.0 295.3 jit_solution(16924288794986256134)
XLA Ops:
  0.7 0.3 fusion.93
  1.0 0.3 fusion.79
  1.3 0.3 fusion.76
  1.5 0.3 fusion.77
  1.8 0.0 copy-start.15
  1.8 0.0 copy-start.16
  1.8 1.7 multiply_subtract_fusion.1
  3.5 1.1 bitcast_select_fusion.2
  4.6 0.9 fusion.38
  5.6 0.0 copy-start.11
  5.6 2.3 multiply_exponential_fusion
  8.0 0.3 copy.27
  8.2 1.2 copy.28.shard_ref
  9.4 77.9 %shard_map.77.w_hbm = bf16[8192,1536]{1,0:T(8,128)(2,1)} custom-call(bf16[256,1536]{1,0:T(8,128)(2,1)} %copy.28.shard_ref), custom_call_target="tpu_custom_call" | custom-call | bytes 50331648 | tf_op jit(solution)/shard_map/pallas_call | solution.py:156
  87.3 20.1 %convolution_convert_fusion = bf16[512,1536]{1,0:T(8,128)(2,1)} fusion(bf16[512,8192]{1,0:T(8,128)(2,1)} %param.6, bf16[8192,1536]{1,0:T(8,128)(2,1)} %shard_map.77.w_hbm), kind=kOutput, calls=%fused_computation.5 | convolution fusion | flops 12885688320 | bytes 35127296 | tf_op jit(solution)/shard_map/dot_general | solution.py:355
  107.4 2.1 copy.29
  109.5 2.1 copy.31
  111.5 2.3 convert_multiply_fusion.1
  113.8 2.5 copy.32
  116.3 8.2 %multiply_reduce_fusion.4 = (f32[16,32,512]{2,1,0:T(8,128)S(1)}, f32[16,16,512]{2,1,0:T(8,128)}) fusion(f32[32,16,512]{2,1,0:T(8,128)} %get-tuple-element.37, f32[16,16,512]{2,1,0:T(8,128)} %fusion.38, f32[16,32,512]{2,1,0:T(8,128)} %bitcast.94), kind=kLoop, calls=%fused_computation.4 | loop fusion | flops 16384000 | bytes 4194304 | tf_op jit(solution)/shard_map/reduce_sum | solution.py:335
  124.5 3.4 %fusion = f32[1024,512]{1,0:T(8,128)S(1)} fusion(f32[512,512]{1,0:T(8,128)S(1)} %bitcast.92, f32[512,512]{1,0:T(8,128)S(1)} %copy-done.1, f32[512,512]{1,0:T(8,128)S(1)} %bitcast.86), kind=kOutput, calls=%fused_computation.7 | convolution fusion | flops 3221749760 | bytes 5242880 | tf_op jit(solution)/shard_map/dot_general | solution.py:400
  127.9 0.0 copy-start.4
  128.0 0.8 fusion.5
  128.7 0.5 copy-done.4
  129.3 0.1 multiply_add_fusion
  129.4 0.1 fusion.23
  129.6 0.9 copy-done.2
  130.5 0.1 copy-done.8
  130.6 0.7 fusion.16
  131.4 0.8 copy-done.5
  132.2 0.0 slice-done
  132.2 2.0 subtract_convert_fusion.2
  134.2 1.2 slice_multiply_fusion
  135.4 2.6 copy.30
  138.0 12.9 %multiply_reduce_fusion.3 = f32[16,16,512]{2,1,0:T(8,128)S(1)} fusion(f32[32,16,512]{2,1,0:T(8,128)} %get-tuple-element.35, f32[16,32,512]{2,1,0:T(8,128)} %bitcast.93), kind=kLoop, calls=%fused_computation.3 | loop fusion | flops 8257536 | bytes 2621440 | tf_op jit(solution)/shard_map/reduce_sum | solution.py:344
  150.9 0.2 multiply_reduce_fusion.8
  151.2 0.6 pad_maximum_fusion.3.st_ref
  151.8 23.0 %shard_map.78 = f32[32,16,512]{2,1,0:T(8,128)} custom-call(f32[2,16,512]{2,1,0:T(8,128)} %pad_maximum_fusion.3.st_ref), custom_call_target="tpu_custom_call" | custom-call | bytes 2097152 | tf_op jit(solution)/shard_map/pallas_call | solution.py:217
  174.9 1.9 multiply_reduce_fusion.5
  176.8 0.2 fusion.36
  177.0 10.6 %multiply_reduce_fusion = (f32[16,32,512]{2,1,0:T(8,128)}, f32[16,32,512]{2,1,0:T(8,128)}) fusion(f32[32,16,512]{2,1,0:T(8,128)S(1)} %copy-done.6, f32[16,16,512]{2,1,0:T(8,128)S(1)} %get-tuple-element.30, f32[32,16,512]{2,1,0:T(8,128)S(1)} %copy-done.7, f32[16,16,512]{2,1,0:T(8,128)S(1)} %get-tuple-element.31), kind=kLoop, calls=%fused_computation | loop fusion | flops 16252928 | bytes 5242880 | tf_op jit(solution)/shard_map/reduce_sum | solution.py:335
  187.6 2.5 copy.34
  190.2 0.3 fusion.97
  190.5 0.3 fusion.85
  190.8 0.3 fusion.82
  191.0 0.3 fusion.83
  191.3 0.6 multiply_subtract_fusion
  191.9 0.0 copy-start.3
  191.9 0.0 copy-start.10
  191.9 0.0 copy-start.12
  191.9 0.0 copy-start.13
  192.0 0.0 copy-start.17
  192.0 1.4 fusion.25
  193.3 0.5 copy-done.10
  193.8 0.1 copy-done.12
  194.0 0.2 copy-done.13
  194.1 1.9 fusion.2
  196.1 2.6 copy.33
  198.7 4.1 %fusion.33 = (bf16[512,1,512]{0,2,1:T(8,128)(2,1)S(1)}, bf16[512,1,512]{0,2,1:T(8,128)(2,1)S(1)}, bf16[512,512]{0,1:T(8,128)(2,1)}, bf16[512,1,512]{0,2,1:T(8,128)(2,1)S(1)}) fusion(f32[512,512]{0,1:T(8,128)} %fusion.2, f32[512,3,512]{0,2,1:T(8,128)S(1)} %bitcast.85, bf16[512,512]{0,1:T(8,128)(2,1)} %copy.31, f32[512]{0:T(512)S(1)} %copy-done.17, ...), kind=kOutput, calls=%fused_computation.75 | convolution fusion | flops 544473088 | bytes 9963520 | tf_op jit(solution)/shard_map/dot_general | solution.py:60
  202.8 0.2 pad_maximum_fusion.2
  203.0 1.6 copy.35.gp_ref
  204.6 86.3 %shard_map.79 = bf16[512,2048]{1,0:T(8,128)(2,1)} custom-call(bf16[512,1536]{1,0:T(8,128)(2,1)} %copy.35.gp_ref, bf16[8192,1536]{1,0:T(8,128)(2,1)} %shard_map.77.w_hbm), custom_call_target="tpu_custom_call" | custom-call | flops 12884901888 | bytes 28835840 | tf_op jit(solution)/shard_map/pallas_call | solution.py:296
  290.9 1.0 copy.36
  291.9 3.2 %copy.38 = bf16[512,2048]{1,0:T(8,128)(2,1)} copy(bf16[512,2048]{1,0:T(8,128)(2,1)} %shard_map.79) | data formatting | bytes 4194304
  (37 shorter events, 0.2 us)
Async XLA Ops:
  1.8 2.8 copy-start.15
  1.8 2.8 copy-start.16
  5.6 2.4 copy-start.11
  116.3 8.2 %copy-start = (f32[16,32,512]{2,1,0:T(8,128)S(1)}, f32[16,32,512]{2,1,0:T(8,128)}, u32[]{:S(2)}) copy-start(f32[16,32,512]{2,1,0:T(8,128)} %get-tuple-element.26) | copy-start | bytes 3145732
  116.3 8.2 %copy-start.1 = (f32[512,512]{1,0:T(8,128)S(1)}, f32[512,512]{1,0:T(8,128)}, u32[]{:S(2)}) copy-start(f32[512,512]{1,0:T(8,128)} %bitcast_select_fusion.2) | copy-start | bytes 3145732
  127.9 1.3 copy-start.4
  129.3 1.2 copy-start.2
  129.3 1.4 copy-start.8
  130.6 1.6 copy-start.5
  130.6 1.6 slice-start
  138.0 12.9 %copy-start.9 = (f32[16,16,512]{2,1,0:T(8,128)S(1)}, f32[16,16,512]{2,1,0:T(8,128)}, u32[]{:S(2)}) copy-start(f32[16,16,512]{2,1,0:T(8,128)} %get-tuple-element.11) | copy-start | bytes 1572868
  174.8 2.2 copy-start.6
  174.8 2.2 copy-start.7
  191.9 1.4 copy-start.3
  191.9 1.9 copy-start.10
  191.9 2.0 copy-start.12
  191.9 2.2 copy-start.13
  192.0 2.2 copy-start.17
  204.6 86.3 %copy-start.14 = (bf16[512,512]{0,1:T(8,128)(2,1)S(1)}, bf16[512,512]{0,1:T(8,128)(2,1)}, u32[]{:S(2)}) copy-start(bf16[512,512]{0,1:T(8,128)(2,1)} %get-tuple-element.20) | copy-start | bytes 1572868

commit v10 on v8

--- a/solution.py
+++ b/solution.py
@@ -47,17 +47,6 @@
     sin_t = jnp.where(first.T, nyquist[:, None], sin_t)
     inv = jnp.concatenate([cos_t * weight[None, :], sin_t * weight[None, :]], axis=1)
     return fwd, inv
-
-
-def spectral_conv(signal, fwd, inv, h_a, h_a2, h_b):
-    block_len = signal.shape[0]
-    spec = jnp.dot(fwd, signal.astype(bf16), preferred_element_type=f32)
-    xc = spec[:block_len]
-    xs = spec[block_len:]
-    pr = xc * h_a - xs * h_b
-    pi = xc * h_b + xs * h_a2
-    prod = jnp.concatenate([pr, pi], axis=0).astype(bf16)
-    return jnp.dot(inv, prod, preferred_element_type=f32)
 
 
 def gather_kernel(shard_ref, out_hbm, send_sem, recv_sem, local_sem):
@@ -168,7 +157,29 @@
     )(shard)
 
 
-def state_kernel(st_ref, out_ref, send_sem, recv_sem):
+def local_conv(sig_ref, fwd_ref, inv_ref, ha_ref, ha2_ref, hb_ref, out_ref):
+    block_len = sig_ref.shape[0]
+    lanes = 128
+
+    def body(j, carry):
+        cols = pl.ds(pl.multiple_of(j * lanes, lanes), lanes)
+        sig = sig_ref[:, cols].astype(jnp.bfloat16)
+        xc = jnp.dot(fwd_ref[:block_len, :], sig, preferred_element_type=jnp.float32)
+        xs = jnp.dot(fwd_ref[block_len:, :], sig, preferred_element_type=jnp.float32)
+        ha = ha_ref[:, cols]
+        hb = hb_ref[:, cols]
+        pr = (xc * ha - xs * hb).astype(jnp.bfloat16)
+        pi = (xc * hb + xs * ha2_ref[:, cols]).astype(jnp.bfloat16)
+        out_ref[:, cols] = jnp.dot(
+            inv_ref[:, :block_len], pr, preferred_element_type=jnp.float32
+        ) + jnp.dot(inv_ref[:, block_len:], pi, preferred_element_type=jnp.float32)
+        return carry
+
+    lax.fori_loop(0, sig_ref.shape[1] // lanes, body, 0)
+
+
+def state_kernel(st_ref, mix_ref, gm_ref, fwd_ref, inv_ref, fwdr_ref, invr_ref, ha_ref, ha2_ref,
+                 hb_ref, out_ref, loc_f_ref, loc_b_ref, send_sem, recv_sem):
     count = out_ref.shape[0]
     side = 4
     me = (lax.axis_index("x") * side + lax.axis_index("y")) * 2 + lax.axis_index("core")
@@ -183,6 +194,7 @@
         return carry
 
     lax.fori_loop(1, count, greet, 0)
+    local_conv(mix_ref, fwd_ref, inv_ref, ha_ref, ha2_ref, hb_ref, loc_f_ref)
     pl.semaphore_wait(barrier, count - 1)
 
     def copy(o):
@@ -202,6 +214,7 @@
 
     lax.fori_loop(1, count, start, 0)
     out_ref[me] = jnp.zeros(out_ref.shape[1:], out_ref.dtype)
+    local_conv(gm_ref, fwdr_ref, invr_ref, ha_ref, ha2_ref, hb_ref, loc_b_ref)
 
     def finish(o, carry):
         cp = copy(o)
@@ -212,17 +225,26 @@
     lax.fori_loop(1, count, finish, 0)
 
 
-def exchange_states(states):
+def exchange_states(states, mixed_in, grad_mix, tables, spectra):
     count = lax.axis_size(SEQ)
+    vmem = pl.BlockSpec(memory_space=pltpu.VMEM)
+    block = jax.ShapeDtypeStruct(mixed_in.shape, jnp.float32)
+    rows, chans = mixed_in.shape
     return pl.pallas_call(
         state_kernel,
-        out_shape=jax.ShapeDtypeStruct((count,) + states.shape[1:], states.dtype),
-        in_specs=[pl.BlockSpec(memory_space=pltpu.VMEM)],
-        out_specs=pl.BlockSpec(memory_space=pltpu.VMEM),
+        out_shape=(jax.ShapeDtypeStruct((count,) + states.shape[1:], states.dtype), block, block),
+        in_specs=[vmem] * 10,
+        out_specs=(vmem, vmem, vmem),
         scratch_shapes=[pltpu.SemaphoreType.DMA((count - 1,)), pltpu.SemaphoreType.DMA((count - 1,))],
-        compiler_params=pltpu.CompilerParams(collective_id=2, has_side_effects=True),
-        cost_estimate=pl.CostEstimate(flops=0, bytes_accessed=8 * states[0].size * count, transcendentals=0),
-    )(states)
+        compiler_params=pltpu.CompilerParams(
+            collective_id=2, has_side_effects=True, vmem_limit_bytes=60 * 1024 * 1024
+        ),
+        cost_estimate=pl.CostEstimate(
+            flops=2 * 4 * 2 * rows * rows * chans,
+            bytes_accessed=8 * states[0].size * count + 4 * 8 * rows * chans,
+            transcendentals=0,
+        ),
+    )(states, mixed_in, grad_mix, *tables, *spectra)
 
 
 def ring_kernel(n, gp_ref, w_hbm, out_ref, wbuf, acc, snd, rcv, wsem, send_sem, recv_sem):
@@ -358,7 +380,16 @@
         [jnp.sum(jnp.exp(-rates[r] * col) * grad_mix, axis=0) for r in range(modes)]
     )
     states = jnp.stack([end_fwd, end_bwd])
-    every = exchange_states(states)
+    fwd, inv = dft_tables(tok_rows)
+    fwd_r, inv_r = dft_tables(tok_rows, flip=True)
+    taps = mode_sum(mode_gain, rates, col)
+    spec = jnp.dot(fwd, taps, precision=lax.Precision.HIGHEST)
+    row0 = (jnp.arange(tok_rows) == 0)[:, None]
+    h_a = spec[:tok_rows]
+    h_a2 = jnp.where(row0, spec[tok_rows:tok_rows + 1], h_a)
+    h_b = jnp.where(row0, 0.0, spec[tok_rows:])
+    tables = [t.astype(bf16) for t in (fwd, inv, fwd_r, inv_r)]
+    every, local_f, local_b = exchange_states(states, mixed_in, grad_mix, tables, (h_a, h_a2, h_b))
 
     others = jnp.arange(seq_count, dtype=jnp.int32)
     gap_f = me - 1 - others
@@ -377,24 +408,11 @@
     into_f = jnp.sum(w_f * every, axis=0) * mode_gain
     into_b = jnp.sum(w_b * every, axis=0) * mode_gain
 
-    taps = mode_sum(mode_gain, rates, col)
-    fwd, inv = dft_tables(tok_rows)
-    fwd_b = fwd.astype(bf16)
-    inv_b = inv.astype(bf16)
-    fwd_r, inv_r = dft_tables(tok_rows, flip=True)
-    spec = jnp.dot(fwd, taps, precision=lax.Precision.HIGHEST)
-    row0 = (jnp.arange(tok_rows) == 0)[:, None]
-    h_a = spec[:tok_rows]
-    h_a2 = jnp.where(row0, spec[tok_rows:tok_rows + 1], h_a)
-    h_b = jnp.where(row0, 0.0, spec[tok_rows:])
-
-    local_f = spectral_conv(mixed_in, fwd_b, inv_b, h_a, h_a2, h_b)
     carry_f = mode_sum(into_f, rates, col + 1.0)
     filtered = local_f + carry_f + skip_gain[None, :] * mixed_in
     gated_output = (query_in * filtered).astype(bf16)
     grad_query = grad_gate * filtered
 
-    local_b = spectral_conv(grad_mix, fwd_r.astype(bf16), inv_r.astype(bf16), h_a, h_a2, h_b)
     carry_b = mode_sum(into_b, rates, tok_rows - col)
     grad_conv = local_b + carry_b + skip_gain[None, :] * grad_mix
 

time: 257 us -> 282 us (1.097); the launches traced: 256 us -> 277 us
  other arithmetic: 17.6 us -> 35.8 us
  local copies, waits for them, and re-layouts: 14.9 us -> 26.1 us
  matrix products: 36.3 us -> 26.4 us
    dot_general x4 -> x0, matrix products: 9.3 us -> none  [the longest x2 7.81 us: spectral_conv(): return jnp.dot(inv, prod, preferred_element_type=f32)]
    another operation x1 -> x4, other arithmetic: 0.17 us -> 8.67 us  [local(): jnp.stack([grad_query, grad_conv * value_in, grad_conv * key_in], axis=1)]
    pallas_call x1, Pallas kernels: 20.2 us -> 26.1 us  [exchange_states(): pl.pallas_call(state_kernel, out_shape=(jax.ShapeDtypeStruct((count,) + s...]
    add x0 -> x2, local copies, waits for them, and re-layouts: none -> 5.08 us  [dft_tables(): sa.T[:, :, None] * cb.T[:, None, :] + ca.T[:, :, None] * sb.T[:, None, :]]
    sub x0 -> x2, local copies, waits for them, and re-layouts: none -> 4.15 us  [dft_tables(): ca.T[:, :, None] * cb.T[:, None, :] - sa.T[:, :, None] * sb.T[:, None, :]]
    pallas_call x1, Pallas kernels: 86 us -> 82 us  [ring_reduce(): pl.pallas_call(functools.partial(ring_kernel, n), out_shape=jax.ShapeDtyp...]
    concatenate x0 -> x3, other arithmetic: none -> 3.36 us  [the longest x2 2.32 us: dft_tables(): jnp.concatenate([cos_t * weight[None, :], sin_t * weight[None, :]], axis=1)]
    unnamed x22 -> x47, local copies, waits for them, and re-layouts: 10.2 us -> 8.14 us
where the time goes in v10:
time: 282 us; the launch traced here: 277 us
  Pallas kernels  188 us (67%)
  other arithmetic  35.8 us (13%)
  matrix products  26.4 us (9%)
  local copies, waits for them, and re-layouts  26.1 us (9%)
    pallas_call x1, Pallas kernels, ring_reduce(): pl.pallas_call(functools.partial(ring_kernel, n), out_shape=jax.ShapeDtyp...  82 us
    pallas_call x1, Pallas kernels, gather_rows(): pl.pallas_call(gather_kernel, out_shape=jax.ShapeDtypeStruct((total, widt...  79.6 us
    pallas_call x1, Pallas kernels, exchange_states(): pl.pallas_call(state_kernel, out_shape=(jax.ShapeDtypeStruct((count,) + s...  26.1 us
    dot_general x1, matrix products, local(): projected = jnp.dot(tokens, whole_w, preferred_element_type=f32)  20.1 us
    reduce_sum x1, other arithmetic, local(): jnp.sum(jnp.exp(-rates[r] * col) * grad_mix, axis=0)  8.9 us
    another operation x4, other arithmetic, local(): jnp.stack([grad_query, grad_conv * value_in, grad_conv * key_in], axis=1)  8.67 us
    unnamed x47, local copies, waits for them, and re-layouts  8.14 us
    dot_general x1, matrix products, local(): spec = jnp.dot(fwd, taps, precision=lax.Precision.HIGHEST)  6.35 us

profile of v10, /device:TPU:32, one launch (start us, length us, event | category | flops | bytes accessed | tf_op | source)
XLA Modules:
  0.0 277.1 jit_solution(6392528123339006361)
XLA Ops:
  0.6 0.3 fusion.130
  1.0 0.3 fusion.118
  1.3 0.3 fusion.115
  1.5 0.3 fusion.116
  1.8 1.3 multiply_subtract_fusion.2
  3.0 0.3 fusion.126
  3.4 0.3 fusion.112
  3.7 0.3 fusion.109
  3.9 0.3 fusion.110
  4.2 2.3 multiply_subtract_fusion
  6.5 1.6 copy.16
  8.1 2.5 copy.17
  10.6 2.6 copy.18
  13.2 2.5 copy.19
  15.8 0.0 copy-start.16
  15.8 0.0 copy-start.17
  15.8 2.5 multiply_convert_fusion
  18.2 0.0 copy-start.2
  18.2 0.0 copy-done.16
  18.3 0.0 copy-done.17
  18.4 0.0 copy-done
  18.4 6.3 %fusion = f32[1024,512]{1,0:T(8,128)S(1)} fusion(f32[512,512]{1,0:T(8,128)S(1)} %get-tuple-element.146, f32[512,512]{1,0:T(8,128)S(1)} %bitcast.146, f32[512]{0:T(512)S(1)} %bitcast.286, f32[512]{0:T(512)S(1)} %bitcast.287, f32[512]{0:T(512)S(1)} %bitcast.288, f32[512]{0:T(512)S(1)} %bitcast.289, f32[512]{0:T(512)S(1)} %bitcast.290, f32[512]{0:T(512)S(1)} %bitcast.291, ...), kind=kOutput, calls=%fused_computation.2 | convolution fusion | flops 3234070528 | bytes 4259840 | tf_op jit(solution)/shard_map/dot_general | solution.py:386
  24.8 0.0 copy-done.2
  24.8 1.8 slice_select_fusion
  26.5 1.2 pad_maximum_fusion.5.invr_ref
  27.7 1.1 pad_maximum_fusion.3.inv_ref
  28.9 0.0 copy-done.15
  28.9 0.3 copy.10
  29.1 1.3 copy.11.shard_ref
  30.5 79.6 %shard_map.77.w_hbm = bf16[8192,1536]{1,0:T(8,128)(2,1)} custom-call(bf16[256,1536]{1,0:T(8,128)(2,1)} %copy.11.shard_ref), custom_call_target="tpu_custom_call" | custom-call | bytes 50331648 | tf_op jit(solution)/shard_map/pallas_call | solution.py:145
  110.1 20.1 %convolution_convert_fusion = bf16[512,1536]{1,0:T(8,128)(2,1)} fusion(bf16[512,8192]{1,0:T(8,128)(2,1)} %param.6, bf16[8192,1536]{1,0:T(8,128)(2,1)} %shard_map.77.w_hbm), kind=kOutput, calls=%fused_computation | convolution fusion | flops 12885688320 | bytes 35127296 | tf_op jit(solution)/shard_map/dot_general | solution.py:357
  130.1 1.7 copy.12
  131.9 1.8 fusion.142
  133.6 1.7 copy.22
  135.3 0.0 copy-start.4
  135.3 0.0 copy-done.8
  135.4 1.3 copy.23
  136.7 1.3 copy.24
  138.0 8.9 %multiply_reduce_fusion.2 = (f32[512]{0:T(512)S(1)}, f32[512]{0:T(512)S(1)}, f32[512]{0:T(512)S(1)}, f32[512]{0:T(512)S(1)}, f32[512]{0:T(512)S(1)}, /*index=5*/...) fusion(f32[512]{0:T(512)S(1)} %bitcast.162, ...), kind=kLoop, calls=%fused_computation.69 | loop fusion | flops 25935872 | bytes 5867520 | tf_op jit(solution)/shard_map/reduce_sum | solution.py:380
  146.9 1.5 stack.143
  148.4 0.1 stack.161
  148.4 0.6 pad_maximum_fusion.6.st_ref
  149.1 0.0 copy-done.1
  149.1 1.2 fusion.1.fwd_ref
  150.2 0.1 multiply_add_fusion.3
  150.4 0.1 fusion.3
  150.5 1.0 pad_maximum_fusion.4.fwdr_ref
  151.6 26.1 %shard_map.78 = (f32[32,16,512]{2,1,0:T(8,128)}, f32[512,512]{1,0:T(8,128)}, f32[512,512]{1,0:T(8,128)}) custom-call(f32[2,16,512]{2,1,0:T(8,128)} %pad_maximum_fusion.6.st_ref, f32[512,512]{1,0:T(8,128)} %get-tuple-element.63.mix_ref, f32[512,512]{1,0:T(8,128)} %get-tuple-element.62.gm_ref, bf16[1024,512]{1,0:T(8,128)(2,1)} %fusion.1.fwd_ref, ...), custom_call_target="tpu_custom_call" | custom-call | flops 2147483648 | bytes 10485760 | tf_op jit(solution)/shard_map/pallas_call | solution.py:233
  177.7 1.7 multiply_reduce_fusion
  179.5 4.3 %fusion.39 = (bf16[512,1,512]{2,0,1:T(8,128)(2,1)S(1)}, f32[512,512]{1,0:T(8,128)S(1)}) fusion(f32[512,1,512]{2,0,1:T(8,128)S(1)} %copy-done.13, f32[512,512]{1,0:T(8,128)S(1)} %copy-done.12, f32[512]{0:T(512)S(1)} %copy-done.20, f32[512,512]{1,0:T(8,128)} %get-tuple-element.7, f32[512]{0:T(512)S(1)} %bitcast.163, f32[512]{0:T(512)S(1)} %bitcast.270, ...), kind=kLoop, calls=%fused_computation.118 | loop fusion | flops 13631488 | bytes 4788224 | tf_op jit(solution)/shard_map/stack | solution.py:419
  183.8 0.0 copy-start.19
  183.8 0.0 copy-done.6
  183.9 0.3 fusion.38
  184.2 0.9 copy-done.11
  185.0 0.3 copy-done.18
  185.4 0.2 copy-done.19
  185.5 3.9 %fusion.40 = (bf16[512,1,512]{2,0,1:T(8,128)(2,1)S(1)}, f32[512,512]{1,0:T(8,128)}) fusion(bf16[512,512]{1,0:T(8,128)(2,1)S(1)} %copy-done.19, f32[512,512]{1,0:T(8,128)S(1)} %copy-done.11, f32[512]{0:T(512)S(1)} %copy-done.20, f32[512,512]{1,0:T(8,128)S(1)} %copy-done.18, f32[512]{0:T(512)S(1)} %bitcast.164, f32[512]{0:T(512)S(1)} %bitcast.222, ...), kind=kLoop, calls=%fused_computation.119 | loop fusion | flops 13893632 | bytes 4263936 | tf_op jit(solution)/shard_map/stack | solution.py:419
  189.5 0.2 pad_maximum_fusion.2
  189.6 0.7 copy.20
  190.3 1.6 copy.21.gp_ref
  191.9 82.0 %shard_map.79 = bf16[512,2048]{1,0:T(8,128)(2,1)} custom-call(bf16[512,1536]{1,0:T(8,128)(2,1)} %copy.21.gp_ref, bf16[8192,1536]{1,0:T(8,128)(2,1)} %shard_map.77.w_hbm), custom_call_target="tpu_custom_call" | custom-call | flops 12884901888 | bytes 28835840 | tf_op jit(solution)/shard_map/pallas_call | solution.py:318
  274.0 0.9 fusion.6
  274.9 0.8 copy-done.9
  275.7 1.3 copy.26
  (42 shorter events, 0.3 us)
Async XLA Ops:
  3.0 15.3 %copy-start = (f32[16,32,512]{2,1,0:T(8,128)}, f32[16,32,512]{2,1,0:T(8,128)S(1)}, u32[]{:S(2)}) copy-start(f32[16,32,512]{2,1,0:T(8,128)S(1)} %get-tuple-element.74) | copy-start | bytes 3145732
  15.8 2.5 copy-start.16
  15.8 2.5 copy-start.17
  18.2 6.5 %copy-start.2 = (f32[512,512]{1,0:T(8,128)}, f32[512,512]{1,0:T(8,128)S(1)}, u32[]{:S(2)}) copy-start(f32[512,512]{1,0:T(8,128)S(1)} %get-tuple-element.146) | copy-start | bytes 3145732
  26.5 2.3 copy-start.15
  133.6 1.7 copy-start.8
  133.6 3.0 %copy-start.7 = (f32[512,1,512]{0,2,1:T(8,128)S(1)}, f32[512,1,512]{0,2,1:T(8,128)}, u32[]{:S(2)}) copy-start(f32[512,1,512]{0,2,1:T(8,128)} %get-tuple-element.66) | copy-start | bytes 3145732
  135.3 2.6 copy-start.4
  138.0 11.1 %copy-start.1 = (f32[16,32,512]{2,1,0:T(8,128)S(1)}, f32[16,32,512]{2,1,0:T(8,128)}, u32[]{:S(2)}) copy-start(f32[16,32,512]{2,1,0:T(8,128)} %copy-done) | copy-start | bytes 3145732
  138.0 11.1 %copy-start.3 = (f32[512,512]{1,0:T(8,128)S(1)}, f32[512,512]{1,0:T(8,128)}, u32[]{:S(2)}) copy-start(f32[512,512]{1,0:T(8,128)} %copy-done.2) | copy-start | bytes 3145732
  149.1 1.4 copy-start.10
  151.5 27.9 %copy-start.12 = (f32[512,512]{1,0:T(8,128)S(1)}, f32[512,512]{1,0:T(8,128)}, u32[]{:S(2)}) copy-start(f32[512,512]{1,0:T(8,128)} %get-tuple-element.62.gm_ref) | copy-start | bytes 3145732
  151.6 27.9 %copy-start.13 = (f32[512,1,512]{2,0,1:T(8,128)S(1)}, f32[512,1,512]{2,0,1:T(8,128)}, u32[]{:S(2)}) copy-start(f32[512,1,512]{2,0,1:T(8,128)} %copy.24) | copy-start | bytes 3145732
  151.6 27.9 %copy-start.20 = (f32[512]{0:T(512)S(1)}, f32[512]{0:T(512)}, u32[]{:S(2)}) copy-start(f32[512]{0:T(512)} %param.10) | copy-start | bytes 6148
  179.5 4.3 %copy-start.6 = (f32[512,1,512]{2,0,1:T(8,128)S(1)}, f32[512,1,512]{2,0,1:T(8,128)}, u32[]{:S(2)}) copy-start(f32[512,1,512]{2,0,1:T(8,128)} %copy.23) | copy-start | bytes 3145732
  183.8 1.2 copy-start.11
  183.8 1.5 copy-start.18
  183.8 1.7 copy-start.19
  191.9 82.0 %copy-start.5 = (f32[512,1,512]{2,0,1:T(8,128)S(1)}, f32[512,1,512]{2,0,1:T(8,128)}, u32[]{:S(2)}) copy-start(f32[512,1,512]{2,0,1:T(8,128)} %copy-done.4) | copy-start | bytes 3145732
  191.9 82.1 %copy-start.14 = (f32[512,512]{1,0:T(8,128)S(1)}, f32[512,512]{1,0:T(8,128)}, u32[]{:S(2)}) copy-start(f32[512,512]{1,0:T(8,128)} %get-tuple-element.59) | copy-start | bytes 3145732
  274.0 1.8 copy-start.9

commit v11 on v8

--- a/solution.py
+++ b/solution.py
@@ -284,9 +284,7 @@
         product(d)
         copies[d].wait_recv()
         copies[d].wait_send()
-        out_ref[:, pl.ds(d * half, half)] = (
-            acc[d] + rcv[d, n - 2].astype(jnp.float32)
-        ).astype(out_ref.dtype)
+        out_ref[:, pl.ds(d * half, half)] = acc[d] + rcv[d, n - 2].astype(jnp.float32)
 
 
 def ring_reduce(grad_proj, whole_w, n):
@@ -295,7 +293,7 @@
     half = block // 2
     return pl.pallas_call(
         functools.partial(ring_kernel, n),
-        out_shape=jax.ShapeDtypeStruct((rows, block), jnp.bfloat16),
+        out_shape=jax.ShapeDtypeStruct((rows, block), jnp.float32),
         in_specs=[pl.BlockSpec(memory_space=pltpu.VMEM), pl.BlockSpec(memory_space=pl.ANY)],
         out_specs=pl.BlockSpec(memory_space=pltpu.VMEM),
         scratch_shapes=[
@@ -400,7 +398,7 @@
 
     grad_proj = jnp.stack([grad_query, grad_conv * value_in, grad_conv * key_in], axis=1).astype(bf16)
     grad_proj = grad_proj.reshape(tok_rows, 3 * chan_count)
-    grad_tokens = ring_reduce(grad_proj, whole_w, lax.axis_size("chan"))
+    grad_tokens = ring_reduce(grad_proj, whole_w, lax.axis_size("chan")).astype(bf16)
     return (gated_output, grad_tokens)
 
 

time: 257 us -> 259 us (level)
  other arithmetic: 17.6 us -> 21.6 us
  local copies, waits for them, and re-layouts: 14.9 us -> 11.8 us
    convert_element_type x0 -> x1, other arithmetic: none -> 3.88 us  [local(): ring_reduce(grad_proj, whole_w, lax.axis_size('chan')).astype(bf16)]
    unnamed x22 -> x21, local copies, waits for them, and re-layouts: 10.2 us -> 7.06 us
where the time goes in v11:
time: 259 us; the launch traced here: 257 us
  Pallas kernels  186 us (72%)
  matrix products  36.3 us (14%)
  other arithmetic  21.6 us (8%)
  local copies, waits for them, and re-layouts  11.8 us (5%)
    pallas_call x1, Pallas kernels, ring_reduce(): pl.pallas_call(functools.partial(ring_kernel, n), out_shape=jax.ShapeDtyp...  86.5 us
    pallas_call x1, Pallas kernels, gather_rows(): pl.pallas_call(gather_kernel, out_shape=jax.ShapeDtypeStruct((total, widt...  79.6 us
    pallas_call x1, Pallas kernels, exchange_states(): pl.pallas_call(state_kernel, out_shape=jax.ShapeDtypeStruct((count,) + st...  20.2 us
    dot_general x1, matrix products, local(): projected = jnp.dot(tokens, whole_w, preferred_element_type=f32)  20.1 us
    reduce_sum x1, other arithmetic, local(): jnp.sum(jnp.exp(-rates[r] * col) * grad_mix, axis=0)  8.93 us
    dot_general x2, matrix products, spectral_conv(): return jnp.dot(inv, prod, preferred_element_type=f32)  7.82 us
    unnamed x21, local copies, waits for them, and re-layouts  7.06 us
    dot_general x1, matrix products, local(): spec = jnp.dot(fwd, taps, precision=lax.Precision.HIGHEST)  6.93 us

profile of v11, /device:TPU:32, one launch (start us, length us, event | category | flops | bytes accessed | tf_op | source)
XLA Modules:
  0.0 256.9 jit_solution(15057131115269303512)
XLA Ops:
  0.6 1.2 slice_negate_fusion.15
  1.8 1.4 copy.15
  3.2 1.2 copy.16.shard_ref
  4.4 79.6 %shard_map.77.w_hbm = bf16[8192,1536]{1,0:T(8,128)(2,1)} custom-call(bf16[256,1536]{1,0:T(8,128)(2,1)} %copy.16.shard_ref), custom_call_target="tpu_custom_call" | custom-call | bytes 50331648 | tf_op jit(solution)/shard_map/pallas_call | solution.py:156
  84.0 20.1 %convolution_convert_fusion = bf16[512,1536]{1,0:T(8,128)(2,1)} fusion(bf16[512,8192]{1,0:T(8,128)(2,1)} %param.6, bf16[8192,1536]{1,0:T(8,128)(2,1)} %shard_map.77.w_hbm), kind=kOutput, calls=%fused_computation | convolution fusion | flops 12885688320 | bytes 35127296 | tf_op jit(solution)/shard_map/dot_general | solution.py:333
  104.0 1.7 copy.17
  105.8 2.0 copy.18
  107.8 0.0 copy-start.6
  107.8 8.9 %multiply_reduce_fusion.2 = (f32[512]{0:T(512)S(1)}, f32[512]{0:T(512)S(1)}, f32[512]{0:T(512)S(1)}, f32[512]{0:T(512)S(1)}, f32[512]{0:T(512)S(1)}, /*index=5*/...) fusion(f32[512]{0:T(512)S(1)} %bitcast.233, ...), kind=kLoop, calls=%fused_computation.57 | loop fusion | flops 25935872 | bytes 5867520 | tf_op jit(solution)/shard_map/reduce_sum | solution.py:356
  116.8 0.0 copy-start.7
  116.8 0.1 stack.143
  116.9 0.1 stack.161
  116.9 0.6 pad_maximum_fusion.3.st_ref
  117.6 20.2 %shard_map.78 = f32[32,16,512]{2,1,0:T(8,128)} custom-call(f32[2,16,512]{2,1,0:T(8,128)} %pad_maximum_fusion.3.st_ref), custom_call_target="tpu_custom_call" | custom-call | bytes 2097152 | tf_op jit(solution)/shard_map/pallas_call | solution.py:217
  137.8 0.0 copy-done.6
  137.8 1.7 multiply_reduce_fusion
  139.6 0.0 copy-done.7
  139.7 0.3 fusion.152
  140.1 0.3 fusion.138
  140.3 0.3 fusion.135
  140.6 0.3 fusion.136
  140.9 0.5 multiply_subtract_fusion.1
  141.4 0.1 bitcast_select_fusion.2
  141.5 0.0 copy-start.2
  141.5 6.9 %fusion = f32[1024,512]{1,0:T(8,128)S(1)} fusion(f32[512,512]{1,0:T(8,128)S(1)} %bitcast_select_fusion.2, f32[512,512]{1,0:T(8,128)S(1)} %bitcast.164, f32[512]{0:T(512)S(1)} %bitcast.234, f32[512]{0:T(512)S(1)} %bitcast.270, f32[512]{0:T(512)S(1)} %bitcast.178, f32[512]{0:T(512)S(1)} %bitcast.271, f32[512]{0:T(512)S(1)} %bitcast.182, f32[512]{0:T(512)S(1)} %bitcast.272, ...), kind=kOutput, calls=%fused_computation.2 | convolution fusion | flops 3234070528 | bytes 4259840 | tf_op jit(solution)/shard_map/dot_general | solution.py:383
  148.4 0.0 copy-start
  148.5 0.0 copy-done.2
  148.5 0.8 fusion.5
  149.2 0.5 copy-done
  149.8 0.0 copy-start.3
  149.8 0.1 multiply_add_fusion
  149.9 0.1 fusion.23
  150.1 0.9 copy-done.3
  151.0 0.0 copy-start.1
  151.0 0.0 slice-start
  151.0 0.7 fusion.16
  151.7 0.8 copy-done.1
  152.6 0.0 slice-done
  152.6 0.6 subtract_convert_fusion.2
  153.3 0.3 fusion.156
  153.6 0.3 fusion.144
  153.9 0.5 fusion.141
  154.4 0.3 fusion.142
  154.6 0.6 multiply_subtract_fusion
  155.3 0.0 copy-start.8
  155.3 0.4 fusion.25
  155.7 0.3 copy-done.8
  155.9 0.0 copy-start.4
  155.9 3.3 %fusion.2 = f32[512,512]{0,1:T(8,128)S(1)} fusion(bf16[512,512]{0,1:T(8,128)(2,1)S(1)} %get-tuple-element.142, bf16[512,512]{0,1:T(8,128)(2,1)S(1)} %get-tuple-element.148, bf16[512,512]{1,0:T(8,128)(2,1)S(1)} %get-tuple-element.67, bf16[512,512]{1,0:T(8,128)(2,1)S(1)} %get-tuple-element.68, f32[512,512]{0,1:T(8,128)S(1)} %copy-done.3, ...), kind=kOutput, calls=%fused_computation.6 | convolution fusion | flops 554172416 | bytes 4263936 | tf_op jit(solution)/shard_map/dot_general | solution.py:60
  159.3 0.0 copy-done.4
  159.3 4.5 %fusion.62 = (bf16[512,1,512]{0,2,1:T(8,128)(2,1)S(1)}, bf16[512,1,512]{0,2,1:T(8,128)(2,1)S(1)}, bf16[512,512]{0,1:T(8,128)(2,1)}, bf16[512,1,512]{0,2,1:T(8,128)(2,1)S(1)}) fusion(f32[512,512]{0,1:T(8,128)S(1)} %fusion.2, f32[512,3,512]{0,2,1:T(8,128)S(1)} %bitcast.167, bf16[512,512]{0,1:T(8,128)(2,1)S(1)} %copy-done.4, f32[512,512]{0,1:T(8,128)S(1)} %copy-done.2, ...), kind=kOutput, calls=%fused_computation.143 | convolution fusion | flops 556531712 | bytes 10031104 | tf_op jit(solution)/shard_map/dot_general | solution.py:60
  163.8 0.2 pad_maximum_fusion.2
  164.0 1.6 copy.19.gp_ref
  165.5 86.5 %shard_map.79 = f32[512,2048]{1,0:T(8,128)} custom-call(bf16[512,1536]{1,0:T(8,128)(2,1)} %copy.19.gp_ref, bf16[8192,1536]{1,0:T(8,128)(2,1)} %shard_map.77.w_hbm), custom_call_target="tpu_custom_call" | custom-call | flops 12884901888 | bytes 28835840 | tf_op jit(solution)/shard_map/pallas_call | solution.py:294
  252.0 0.0 copy-start.5
  252.0 3.9 %convert_element_type.163 = bf16[512,2048]{1,0:T(8,128)(2,1)} convert(f32[512,2048]{1,0:T(8,128)} %shard_map.79) | non-fusion elementwise | flops 1048576 | bytes 6291456 | tf_op jit(solution)/shard_map/convert_element_type | solution.py:401
  255.9 0.0 copy-done.5
  255.9 1.0 copy.20
  (16 shorter events, 0.2 us)
Async XLA Ops:
  107.8 30.0 %copy-start.6 = (f32[16,512]{1,0:T(8,128)S(1)}, f32[16,512]{1,0:T(8,128)}, u32[]{:S(2)}) copy-start(f32[16,512]{1,0:T(8,128)} %param.9) | copy-start | bytes 98308
  116.8 22.8 %copy-start.7 = (f32[16,512]{1,0:T(8,128)S(1)}, f32[16,512]{1,0:T(8,128)}, u32[]{:S(2)}) copy-start(f32[16,512]{1,0:T(8,128)} %param.8) | copy-start | bytes 98308
  141.5 7.0 %copy-start.2 = (f32[512,512]{0,1:T(8,128)S(1)}, f32[512,512]{0,1:T(8,128)}, u32[]{:S(2)}) copy-start(f32[512,512]{0,1:T(8,128)} %get-tuple-element.59) | copy-start | bytes 3145732
  148.4 1.3 copy-start
  149.8 1.2 copy-start.3
  151.0 1.6 copy-start.1
  151.0 1.6 slice-start
  155.3 0.7 copy-start.8
  155.9 3.3 %copy-start.4 = (bf16[512,512]{0,1:T(8,128)(2,1)S(1)}, bf16[512,512]{0,1:T(8,128)(2,1)}, u32[]{:S(2)}) copy-start(bf16[512,512]{0,1:T(8,128)(2,1)} %copy.18) | copy-start | bytes 1572868
  252.0 3.9 %copy-start.5 = (bf16[512,512]{0,1:T(8,128)(2,1)S(1)}, bf16[512,512]{0,1:T(8,128)(2,1)}, u32[]{:S(2)}) copy-start(bf16[512,512]{0,1:T(8,128)(2,1)} %get-tuple-element.66) | copy-start | bytes 1572868

commit v12 on v8

--- a/solution.py
+++ b/solution.py
@@ -236,7 +236,6 @@
     barrier = pltpu.get_barrier_semaphore()
     for neighbour in (left, right):
         pl.semaphore_signal(barrier, inc=1, device_id={"chan": neighbour}, device_id_type=MESH)
-    pl.semaphore_wait(barrier, 2)
 
     def load(d, dest):
         first = pl.multiple_of(dest * block + d * half, 8)
@@ -260,9 +259,15 @@
     for step in range(n - 1):
         dests = (lax.rem(me + 2 * n - 1 - step, n), lax.rem(me + 1 + step, n))
         loads = [load(d, dests[d]) for d in (0, 1)]
+        if step == 0:
+            for d in (0, 1):
+                loads[d].wait()
+                product(d)
+            pl.semaphore_wait(barrier, 2)
         for d in (0, 1):
-            loads[d].wait()
-            product(d)
+            if step > 0:
+                loads[d].wait()
+                product(d)
             if copies[d] is not None:
                 copies[d].wait_recv()
                 copies[d].wait_send()

time: 257 us -> 260 us (1.012)
  no operation moved by 1% of the time
where the time goes in v12:
time: 260 us; the launch traced here: 257 us
  Pallas kernels  187 us (72%)
  matrix products  36.3 us (14%)
  other arithmetic  17.6 us (7%)
  local copies, waits for them, and re-layouts  14.9 us (6%)
    pallas_call x1, Pallas kernels, ring_reduce(): pl.pallas_call(functools.partial(ring_kernel, n), out_shape=jax.ShapeDtyp...  87 us
    pallas_call x1, Pallas kernels, gather_rows(): pl.pallas_call(gather_kernel, out_shape=jax.ShapeDtypeStruct((total, widt...  79.6 us
    pallas_call x1, Pallas kernels, exchange_states(): pl.pallas_call(state_kernel, out_shape=jax.ShapeDtypeStruct((count,) + st...  20.2 us
    dot_general x1, matrix products, local(): projected = jnp.dot(tokens, whole_w, preferred_element_type=f32)  20.1 us
    unnamed x22, local copies, waits for them, and re-layouts  10.2 us
    reduce_sum x1, other arithmetic, local(): jnp.sum(jnp.exp(-rates[r] * col) * grad_mix, axis=0)  8.93 us
    dot_general x2, matrix products, spectral_conv(): return jnp.dot(inv, prod, preferred_element_type=f32)  7.81 us
    dot_general x1, matrix products, local(): spec = jnp.dot(fwd, taps, precision=lax.Precision.HIGHEST)  6.93 us

profile of v12, /device:TPU:32, one launch (start us, length us, event | category | flops | bytes accessed | tf_op | source)
XLA Modules:
  0.0 256.6 jit_solution(842051574640556497)
XLA Ops:
  0.6 1.1 slice_negate_fusion.15
  1.7 1.4 copy.15
  3.1 1.2 copy.16.shard_ref
  4.3 79.6 %shard_map.77.w_hbm = bf16[8192,1536]{1,0:T(8,128)(2,1)} custom-call(bf16[256,1536]{1,0:T(8,128)(2,1)} %copy.16.shard_ref), custom_call_target="tpu_custom_call" | custom-call | bytes 50331648 | tf_op jit(solution)/shard_map/pallas_call | solution.py:156
  83.8 20.1 %convolution_convert_fusion = bf16[512,1536]{1,0:T(8,128)(2,1)} fusion(bf16[512,8192]{1,0:T(8,128)(2,1)} %param.6, bf16[8192,1536]{1,0:T(8,128)(2,1)} %shard_map.77.w_hbm), kind=kOutput, calls=%fused_computation | convolution fusion | flops 12885688320 | bytes 35127296 | tf_op jit(solution)/shard_map/dot_general | solution.py:340
  103.9 1.7 copy.17
  105.7 2.0 copy.18
  107.7 0.0 copy-start.6
  107.7 8.9 %multiply_reduce_fusion.2 = (f32[512]{0:T(512)S(1)}, f32[512]{0:T(512)S(1)}, f32[512]{0:T(512)S(1)}, f32[512]{0:T(512)S(1)}, f32[512]{0:T(512)S(1)}, /*index=5*/...) fusion(f32[512]{0:T(512)S(1)} %bitcast.233, ...), kind=kLoop, calls=%fused_computation.57 | loop fusion | flops 25935872 | bytes 5867520 | tf_op jit(solution)/shard_map/reduce_sum | solution.py:363
  116.6 0.0 copy-start.7
  116.7 0.1 stack.143
  116.7 0.1 stack.161
  116.8 0.6 pad_maximum_fusion.3.st_ref
  117.5 20.2 %shard_map.78 = f32[32,16,512]{2,1,0:T(8,128)} custom-call(f32[2,16,512]{2,1,0:T(8,128)} %pad_maximum_fusion.3.st_ref), custom_call_target="tpu_custom_call" | custom-call | bytes 2097152 | tf_op jit(solution)/shard_map/pallas_call | solution.py:217
  137.7 0.0 copy-done.6
  137.7 1.7 multiply_reduce_fusion
  139.4 0.0 copy-done.7
  139.6 0.3 fusion.152
  139.9 0.3 fusion.138
  140.2 0.3 fusion.135
  140.5 0.3 fusion.136
  140.7 0.5 multiply_subtract_fusion.1
  141.2 0.1 bitcast_select_fusion.2
  141.4 0.0 copy-start.2
  141.4 6.9 %fusion = f32[1024,512]{1,0:T(8,128)S(1)} fusion(f32[512,512]{1,0:T(8,128)S(1)} %bitcast_select_fusion.2, f32[512,512]{1,0:T(8,128)S(1)} %bitcast.164, f32[512]{0:T(512)S(1)} %bitcast.234, f32[512]{0:T(512)S(1)} %bitcast.270, f32[512]{0:T(512)S(1)} %bitcast.178, f32[512]{0:T(512)S(1)} %bitcast.271, f32[512]{0:T(512)S(1)} %bitcast.182, f32[512]{0:T(512)S(1)} %bitcast.272, ...), kind=kOutput, calls=%fused_computation.2 | convolution fusion | flops 3234070528 | bytes 4259840 | tf_op jit(solution)/shard_map/dot_general | solution.py:390
  148.3 0.0 copy-start
  148.3 0.0 copy-done.2
  148.3 0.8 fusion.5
  149.1 0.5 copy-done
  149.6 0.0 copy-start.3
  149.6 0.1 multiply_add_fusion
  149.8 0.1 fusion.23
  149.9 0.9 copy-done.3
  150.9 0.0 copy-start.1
  150.9 0.0 slice-start
  150.9 0.7 fusion.16
  151.6 0.8 copy-done.1
  152.5 0.0 slice-done
  152.5 0.6 subtract_convert_fusion.2
  153.1 0.3 fusion.156
  153.5 0.3 fusion.144
  153.8 0.5 fusion.141
  154.3 0.3 fusion.142
  154.5 0.6 multiply_subtract_fusion
  155.1 0.0 copy-start.8
  155.1 0.4 fusion.25
  155.6 0.3 copy-done.8
  155.8 0.0 copy-start.4
  155.8 3.3 %fusion.2 = f32[512,512]{0,1:T(8,128)S(1)} fusion(bf16[512,512]{0,1:T(8,128)(2,1)S(1)} %get-tuple-element.142, bf16[512,512]{0,1:T(8,128)(2,1)S(1)} %get-tuple-element.148, bf16[512,512]{1,0:T(8,128)(2,1)S(1)} %get-tuple-element.67, bf16[512,512]{1,0:T(8,128)(2,1)S(1)} %get-tuple-element.68, f32[512,512]{0,1:T(8,128)S(1)} %copy-done.3, ...), kind=kOutput, calls=%fused_computation.6 | convolution fusion | flops 554172416 | bytes 4263936 | tf_op jit(solution)/shard_map/dot_general | solution.py:60
  159.2 0.0 copy-done.4
  159.2 4.5 %fusion.62 = (bf16[512,1,512]{0,2,1:T(8,128)(2,1)S(1)}, bf16[512,1,512]{0,2,1:T(8,128)(2,1)S(1)}, bf16[512,512]{0,1:T(8,128)(2,1)}, bf16[512,1,512]{0,2,1:T(8,128)(2,1)S(1)}) fusion(f32[512,512]{0,1:T(8,128)S(1)} %fusion.2, f32[512,3,512]{0,2,1:T(8,128)S(1)} %bitcast.167, bf16[512,512]{0,1:T(8,128)(2,1)S(1)} %copy-done.4, f32[512,512]{0,1:T(8,128)S(1)} %copy-done.2, ...), kind=kOutput, calls=%fused_computation.143 | convolution fusion | flops 556531712 | bytes 10031104 | tf_op jit(solution)/shard_map/dot_general | solution.py:60
  163.7 0.2 pad_maximum_fusion.2
  163.8 1.6 copy.19.gp_ref
  165.4 0.0 copy-start.5
  165.4 87.0 %shard_map.79 = bf16[512,2048]{1,0:T(8,128)(2,1)} custom-call(bf16[512,1536]{1,0:T(8,128)(2,1)} %copy.19.gp_ref, bf16[8192,1536]{1,0:T(8,128)(2,1)} %shard_map.77.w_hbm), custom_call_target="tpu_custom_call" | custom-call | flops 12884901888 | bytes 28835840 | tf_op jit(solution)/shard_map/pallas_call | solution.py:301
  252.5 0.0 copy-done.5
  252.5 1.0 copy.20
  253.5 3.2 %copy.22 = bf16[512,2048]{1,0:T(8,128)(2,1)} copy(bf16[512,2048]{1,0:T(8,128)(2,1)} %shard_map.79) | data formatting | bytes 4194304
  (16 shorter events, 0.2 us)
Async XLA Ops:
  107.7 30.0 %copy-start.6 = (f32[16,512]{1,0:T(8,128)S(1)}, f32[16,512]{1,0:T(8,128)}, u32[]{:S(2)}) copy-start(f32[16,512]{1,0:T(8,128)} %param.9) | copy-start | bytes 98308
  116.6 22.8 %copy-start.7 = (f32[16,512]{1,0:T(8,128)S(1)}, f32[16,512]{1,0:T(8,128)}, u32[]{:S(2)}) copy-start(f32[16,512]{1,0:T(8,128)} %param.8) | copy-start | bytes 98308
  141.4 7.0 %copy-start.2 = (f32[512,512]{0,1:T(8,128)S(1)}, f32[512,512]{0,1:T(8,128)}, u32[]{:S(2)}) copy-start(f32[512,512]{0,1:T(8,128)} %get-tuple-element.59) | copy-start | bytes 3145732
  148.3 1.3 copy-start
  149.6 1.2 copy-start.3
  150.9 1.6 copy-start.1
  150.9 1.6 slice-start
  155.1 0.7 copy-start.8
  155.8 3.3 %copy-start.4 = (bf16[512,512]{0,1:T(8,128)(2,1)S(1)}, bf16[512,512]{0,1:T(8,128)(2,1)}, u32[]{:S(2)}) copy-start(bf16[512,512]{0,1:T(8,128)(2,1)} %copy.18) | copy-start | bytes 1572868
  165.4 87.0 %copy-start.5 = (bf16[512,512]{0,1:T(8,128)(2,1)S(1)}, bf16[512,512]{0,1:T(8,128)(2,1)}, u32[]{:S(2)}) copy-start(bf16[512,512]{0,1:T(8,128)(2,1)} %get-tuple-element.66) | copy-start | bytes 1572868

commit v13 on v8

--- a/solution.py
+++ b/solution.py
@@ -358,7 +358,7 @@
         [jnp.sum(jnp.exp(-rates[r] * col) * grad_mix, axis=0) for r in range(modes)]
     )
     states = jnp.stack([end_fwd, end_bwd])
-    every = exchange_states(states)
+    every = exchange_states(states.astype(bf16)).astype(f32)
 
     others = jnp.arange(seq_count, dtype=jnp.int32)
     gap_f = me - 1 - others

time: 257 us -> 248 us (0.965)
  Pallas kernels: 186 us -> 178 us
    pallas_call x1, Pallas kernels: 20.2 us -> 13 us  [exchange_states(): pl.pallas_call(state_kernel, out_shape=jax.ShapeDtypeStruct((count,) + st...]
where the time goes in v13:
time: 248 us
  Pallas kernels  178 us (72%)
  matrix products  36.3 us (15%)
  other arithmetic  17.5 us (7%)
  local copies, waits for them, and re-layouts  15.1 us (6%)
    pallas_call x1, Pallas kernels, ring_reduce(): pl.pallas_call(functools.partial(ring_kernel, n), out_shape=jax.ShapeDtyp...  85.2 us
    pallas_call x1, Pallas kernels, gather_rows(): pl.pallas_call(gather_kernel, out_shape=jax.ShapeDtypeStruct((total, widt...  79.6 us
    dot_general x1, matrix products, local(): projected = jnp.dot(tokens, whole_w, preferred_element_type=f32)  20.1 us
    pallas_call x1, Pallas kernels, exchange_states(): pl.pallas_call(state_kernel, out_shape=jax.ShapeDtypeStruct((count,) + st...  13 us
    unnamed x22, local copies, waits for them, and re-layouts  10.2 us
    reduce_sum x1, other arithmetic, local(): jnp.sum(jnp.exp(-rates[r] * col) * grad_mix, axis=0)  8.97 us
    dot_general x2, matrix products, spectral_conv(): return jnp.dot(inv, prod, preferred_element_type=f32)  7.81 us
    dot_general x1, matrix products, local(): spec = jnp.dot(fwd, taps, precision=lax.Precision.HIGHEST)  6.93 us

profile of v13, /device:TPU:32, one launch (start us, length us, event | category | flops | bytes accessed | tf_op | source)
XLA Modules:
  0.0 247.9 jit_solution(13629862261389481823)
XLA Ops:
  0.6 1.1 slice_negate_fusion.15
  1.7 1.4 copy.15
  3.1 1.2 copy.16.shard_ref
  4.3 79.6 %shard_map.77.w_hbm = bf16[8192,1536]{1,0:T(8,128)(2,1)} custom-call(bf16[256,1536]{1,0:T(8,128)(2,1)} %copy.16.shard_ref), custom_call_target="tpu_custom_call" | custom-call | bytes 50331648 | tf_op jit(solution)/shard_map/pallas_call | solution.py:156
  83.8 20.1 %convolution_convert_fusion = bf16[512,1536]{1,0:T(8,128)(2,1)} fusion(bf16[512,8192]{1,0:T(8,128)(2,1)} %param.6, bf16[8192,1536]{1,0:T(8,128)(2,1)} %shard_map.77.w_hbm), kind=kOutput, calls=%fused_computation | convolution fusion | flops 12885688320 | bytes 35127296 | tf_op jit(solution)/shard_map/dot_general | solution.py:335
  103.9 1.7 copy.17
  105.7 2.0 copy.18
  107.7 0.0 copy-start.6
  107.7 0.0 copy-start.7
  107.7 9.0 %multiply_reduce_fusion = (bf16[512]{0:T(512)(128)(2,1)S(1)}, bf16[512]{0:T(512)(128)(2,1)S(1)}, bf16[512]{0:T(512)(128)(2,1)S(1)}, bf16[512]{0:T(512)(128)(2,1)...) fusion(f32[512]{0:T(512)S(1)} %bitcast.201, ...), kind=kLoop, calls=%fused_computation.59 | loop fusion | flops 25935872 | bytes 5834752 | tf_op jit(solution)/shard_map/reduce_sum | solution.py:358
  116.9 0.1 stack.180
  117.1 0.1 stack.198
  117.2 0.6 pad_maximum_fusion.3.st_ref
  117.8 13.0 %shard_map.78 = bf16[32,16,512]{2,1,0:T(8,128)(2,1)} custom-call(bf16[2,16,512]{2,1,0:T(8,128)(2,1)} %pad_maximum_fusion.3.st_ref), custom_call_target="tpu_custom_call" | custom-call | bytes 2097152 | tf_op jit(solution)/shard_map/pallas_call | solution.py:217
  130.8 0.0 copy-done.6
  130.9 1.6 fusion.6
  132.5 0.0 copy-done.7
  132.6 0.3 fusion.154
  133.0 0.3 fusion.140
  133.3 0.3 fusion.137
  133.5 0.3 fusion.138
  133.8 0.5 multiply_subtract_fusion.1
  134.3 0.1 bitcast_select_fusion.2
  134.4 0.0 copy-start.2
  134.4 6.9 %fusion = f32[1024,512]{1,0:T(8,128)S(1)} fusion(f32[512,512]{1,0:T(8,128)S(1)} %bitcast_select_fusion.2, f32[512,512]{1,0:T(8,128)S(1)} %bitcast.132, f32[512]{0:T(512)S(1)} %bitcast.202, f32[512]{0:T(512)S(1)} %bitcast.238, f32[512]{0:T(512)S(1)} %bitcast.146, f32[512]{0:T(512)S(1)} %bitcast.239, f32[512]{0:T(512)S(1)} %bitcast.150, f32[512]{0:T(512)S(1)} %bitcast.240, ...), kind=kOutput, calls=%fused_computation.2 | convolution fusion | flops 3234070528 | bytes 4259840 | tf_op jit(solution)/shard_map/dot_general | solution.py:385
  141.4 0.0 copy-start
  141.4 0.0 copy-done.2
  141.4 0.8 fusion.7
  142.2 0.5 copy-done
  142.7 0.0 copy-start.3
  142.7 0.1 multiply_add_fusion
  142.8 0.1 fusion.25
  143.0 0.9 copy-done.3
  143.9 0.0 copy-start.1
  143.9 0.0 slice-start
  143.9 0.7 fusion.18
  144.7 0.8 copy-done.1
  145.5 0.0 slice-done
  145.5 0.6 subtract_convert_fusion.2
  146.2 0.3 fusion.158
  146.5 0.5 fusion.146
  147.0 0.3 fusion.143
  147.3 0.3 fusion.144
  147.6 0.6 multiply_subtract_fusion
  148.2 0.0 copy-start.8
  148.2 0.4 fusion.27
  148.6 0.3 copy-done.8
  148.9 0.0 copy-start.4
  148.9 3.3 %fusion.2 = f32[512,512]{0,1:T(8,128)S(1)} fusion(bf16[512,512]{0,1:T(8,128)(2,1)S(1)} %get-tuple-element.142, bf16[512,512]{0,1:T(8,128)(2,1)S(1)} %get-tuple-element.148, bf16[512,512]{1,0:T(8,128)(2,1)S(1)} %get-tuple-element.67, bf16[512,512]{1,0:T(8,128)(2,1)S(1)} %get-tuple-element.68, f32[512,512]{0,1:T(8,128)S(1)} %copy-done.3, ...), kind=kOutput, calls=%fused_computation.6 | convolution fusion | flops 554172416 | bytes 4263936 | tf_op jit(solution)/shard_map/dot_general | solution.py:60
  152.2 0.0 copy-done.4
  152.2 4.5 %fusion.64 = (bf16[512,1,512]{0,2,1:T(8,128)(2,1)S(1)}, bf16[512,1,512]{0,2,1:T(8,128)(2,1)S(1)}, bf16[512,512]{0,1:T(8,128)(2,1)}, bf16[512,1,512]{0,2,1:T(8,128)(2,1)S(1)}) fusion(f32[512,512]{0,1:T(8,128)S(1)} %fusion.2, f32[512,3,512]{0,2,1:T(8,128)S(1)} %bitcast.135, bf16[512,512]{0,1:T(8,128)(2,1)S(1)} %copy-done.4, f32[512,512]{0,1:T(8,128)S(1)} %copy-done.2, ...), kind=kOutput, calls=%fused_computation.145 | convolution fusion | flops 556531712 | bytes 10031104 | tf_op jit(solution)/shard_map/dot_general | solution.py:60
  156.7 0.2 pad_maximum_fusion.2
  156.9 1.6 copy.19.gp_ref
  158.5 0.0 copy-start.5
  158.5 85.2 %shard_map.79 = bf16[512,2048]{1,0:T(8,128)(2,1)} custom-call(bf16[512,1536]{1,0:T(8,128)(2,1)} %copy.19.gp_ref, bf16[8192,1536]{1,0:T(8,128)(2,1)} %shard_map.77.w_hbm), custom_call_target="tpu_custom_call" | custom-call | flops 12884901888 | bytes 28835840 | tf_op jit(solution)/shard_map/pallas_call | solution.py:296
  243.7 0.0 copy-done.5
  243.7 1.0 copy.20
  244.7 3.2 %copy.22 = bf16[512,2048]{1,0:T(8,128)(2,1)} copy(bf16[512,2048]{1,0:T(8,128)(2,1)} %shard_map.79) | data formatting | bytes 4194304
  (48 shorter events, 0.4 us)
Async XLA Ops:
  107.7 23.1 %copy-start.6 = (f32[16,512]{1,0:T(8,128)S(1)}, f32[16,512]{1,0:T(8,128)}, u32[]{:S(2)}) copy-start(f32[16,512]{1,0:T(8,128)} %param.9) | copy-start | bytes 98308
  107.7 24.8 %copy-start.7 = (f32[16,512]{1,0:T(8,128)S(1)}, f32[16,512]{1,0:T(8,128)}, u32[]{:S(2)}) copy-start(f32[16,512]{1,0:T(8,128)} %param.8) | copy-start | bytes 98308
  134.4 7.0 %copy-start.2 = (f32[512,512]{0,1:T(8,128)S(1)}, f32[512,512]{0,1:T(8,128)}, u32[]{:S(2)}) copy-start(f32[512,512]{0,1:T(8,128)} %get-tuple-element.59) | copy-start | bytes 3145732
  141.4 1.3 copy-start
  142.7 1.2 copy-start.3
  143.9 1.6 copy-start.1
  143.9 1.6 slice-start
  148.2 0.7 copy-start.8
  148.9 3.3 %copy-start.4 = (bf16[512,512]{0,1:T(8,128)(2,1)S(1)}, bf16[512,512]{0,1:T(8,128)(2,1)}, u32[]{:S(2)}) copy-start(bf16[512,512]{0,1:T(8,128)(2,1)} %copy.18) | copy-start | bytes 1572868
  158.5 85.2 %copy-start.5 = (bf16[512,512]{0,1:T(8,128)(2,1)S(1)}, bf16[512,512]{0,1:T(8,128)(2,1)}, u32[]{:S(2)}) copy-start(bf16[512,512]{0,1:T(8,128)(2,1)} %get-tuple-element.66) | copy-start | bytes 1572868

commit v14 on v13

--- a/solution.py
+++ b/solution.py
@@ -168,31 +168,42 @@
     )(shard)
 
 
-def state_kernel(st_ref, out_ref, send_sem, recv_sem):
-    count = out_ref.shape[0]
+def state_kernel(st_ref, out_ref, pair, send_sem, recv_sem, pair_sem):
+    chips = out_ref.shape[0]
     side = 4
-    me = (lax.axis_index("x") * side + lax.axis_index("y")) * 2 + lax.axis_index("core")
-
-    def device(j):
-        return {"x": j // (2 * side), "y": (j // 2) % side, "core": j % 2}
+    chip = lax.axis_index("x") * side + lax.axis_index("y")
+    core = lax.axis_index("core")
+    other = 1 - core
+
+    def device(k, c):
+        return {"x": k // side, "y": k % side, "core": c}
 
     barrier = pltpu.get_barrier_semaphore()
+    pl.semaphore_signal(barrier, inc=1, device_id=device(chip, other), device_id_type=MESH)
 
     def greet(o, carry):
-        pl.semaphore_signal(barrier, inc=1, device_id=device(lax.rem(me + o, count)), device_id_type=MESH)
+        pl.semaphore_signal(barrier, inc=1, device_id=device(lax.rem(chip + o, chips), core),
+                            device_id_type=MESH)
         return carry
 
-    lax.fori_loop(1, count, greet, 0)
-    pl.semaphore_wait(barrier, count - 1)
+    lax.fori_loop(1, chips, greet, 0)
+    pl.semaphore_wait(barrier, chips)
+
+    swap = pltpu.make_async_remote_copy(
+        src_ref=st_ref, dst_ref=pair.at[core], send_sem=pair_sem.at[0], recv_sem=pair_sem.at[1],
+        device_id=device(chip, other), device_id_type=MESH,
+    )
+    swap.start()
+    pair[core] = st_ref[...]
+    swap.wait()
 
     def copy(o):
-        j = lax.rem(me + o, count)
         return pltpu.make_async_remote_copy(
-            src_ref=st_ref.at[(me + o) // count],
-            dst_ref=out_ref.at[me],
+            src_ref=pair.at[:, (chip + o) // chips],
+            dst_ref=out_ref.at[chip],
             send_sem=send_sem.at[o - 1],
             recv_sem=recv_sem.at[o - 1],
-            device_id=device(j),
+            device_id=device(lax.rem(chip + o, chips), core),
             device_id_type=MESH,
         )
 
@@ -200,8 +211,9 @@
         copy(o).start()
         return carry
 
-    lax.fori_loop(1, count, start, 0)
-    out_ref[me] = jnp.zeros(out_ref.shape[1:], out_ref.dtype)
+    lax.fori_loop(1, chips, start, 0)
+    out_ref[chip, core] = jnp.zeros(out_ref.shape[2:], out_ref.dtype)
+    out_ref[chip, other] = pair[other, other]
 
     def finish(o, carry):
         cp = copy(o)
@@ -209,20 +221,25 @@
         cp.wait_recv()
         return carry
 
-    lax.fori_loop(1, count, finish, 0)
+    lax.fori_loop(1, chips, finish, 0)
 
 
 def exchange_states(states):
-    count = lax.axis_size(SEQ)
+    chips = lax.axis_size(SEQ) // 2
     return pl.pallas_call(
         state_kernel,
-        out_shape=jax.ShapeDtypeStruct((count,) + states.shape[1:], states.dtype),
+        out_shape=jax.ShapeDtypeStruct((chips, 2) + states.shape[1:], states.dtype),
         in_specs=[pl.BlockSpec(memory_space=pltpu.VMEM)],
         out_specs=pl.BlockSpec(memory_space=pltpu.VMEM),
-        scratch_shapes=[pltpu.SemaphoreType.DMA((count - 1,)), pltpu.SemaphoreType.DMA((count - 1,))],
+        scratch_shapes=[
+            pltpu.VMEM((2,) + states.shape, states.dtype),
+            pltpu.SemaphoreType.DMA((chips - 1,)),
+            pltpu.SemaphoreType.DMA((chips - 1,)),
+            pltpu.SemaphoreType.DMA((2,)),
+        ],
         compiler_params=pltpu.CompilerParams(collective_id=2, has_side_effects=True),
-        cost_estimate=pl.CostEstimate(flops=0, bytes_accessed=8 * states[0].size * count, transcendentals=0),
-    )(states)
+        cost_estimate=pl.CostEstimate(flops=0, bytes_accessed=8 * states[0].size * chips, transcendentals=0),
+    )(states).reshape((2 * chips,) + states.shape[1:])
 
 
 def ring_kernel(n, gp_ref, w_hbm, out_ref, wbuf, acc, snd, rcv, wsem, send_sem, recv_sem):

time: 248 us -> 248 us (level)
    pallas_call x1, Pallas kernels: 85.2 us -> 82.6 us  [ring_reduce(): pl.pallas_call(functools.partial(ring_kernel, n), out_shape=jax.ShapeDtyp...]
where the time goes in v14:
time: 248 us; the launch traced here: 246 us
  Pallas kernels  176 us (71%)
  matrix products  36.3 us (15%)
  other arithmetic  17.6 us (7%)
  local copies, waits for them, and re-layouts  15.1 us (6%)
    pallas_call x1, Pallas kernels, ring_reduce(): pl.pallas_call(functools.partial(ring_kernel, n), out_shape=jax.ShapeDtyp...  82.6 us
    pallas_call x1, Pallas kernels, gather_rows(): pl.pallas_call(gather_kernel, out_shape=jax.ShapeDtypeStruct((total, widt...  79.6 us
    dot_general x1, matrix products, local(): projected = jnp.dot(tokens, whole_w, preferred_element_type=f32)  20.1 us
    pallas_call x1, Pallas kernels, exchange_states(): pl.pallas_call(state_kernel, out_shape=jax.ShapeDtypeStruct((chips, 2) +...  13.8 us
    unnamed x22, local copies, waits for them, and re-layouts  10.2 us
    reduce_sum x1, other arithmetic, local(): jnp.sum(jnp.exp(-rates[r] * col) * grad_mix, axis=0)  8.97 us
    dot_general x2, matrix products, spectral_conv(): return jnp.dot(inv, prod, preferred_element_type=f32)  7.81 us
    dot_general x1, matrix products, local(): spec = jnp.dot(fwd, taps, precision=lax.Precision.HIGHEST)  6.93 us

profile of v14, /device:TPU:32, one launch (start us, length us, event | category | flops | bytes accessed | tf_op | source)
XLA Modules:
  0.0 246.1 jit_solution(10753784888087429500)
XLA Ops:
  0.6 1.1 slice_negate_fusion.15
  1.7 1.4 copy.15
  3.1 1.2 copy.16.shard_ref
  4.3 79.6 %shard_map.77.w_hbm = bf16[8192,1536]{1,0:T(8,128)(2,1)} custom-call(bf16[256,1536]{1,0:T(8,128)(2,1)} %copy.16.shard_ref), custom_call_target="tpu_custom_call" | custom-call | bytes 50331648 | tf_op jit(solution)/shard_map/pallas_call | solution.py:156
  83.8 20.1 %convolution_convert_fusion = bf16[512,1536]{1,0:T(8,128)(2,1)} fusion(bf16[512,8192]{1,0:T(8,128)(2,1)} %param.6, bf16[8192,1536]{1,0:T(8,128)(2,1)} %shard_map.77.w_hbm), kind=kOutput, calls=%fused_computation | convolution fusion | flops 12885688320 | bytes 35127296 | tf_op jit(solution)/shard_map/dot_general | solution.py:352
  103.9 1.7 copy.17
  105.7 2.0 copy.18
  107.7 0.0 copy-start.6
  107.7 0.0 copy-start.7
  107.7 9.0 %multiply_reduce_fusion = (bf16[512]{0:T(512)(128)(2,1)S(1)}, bf16[512]{0:T(512)(128)(2,1)S(1)}, bf16[512]{0:T(512)(128)(2,1)S(1)}, bf16[512]{0:T(512)(128)(2,1)...) fusion(f32[512]{0:T(512)S(1)} %bitcast.201, ...), kind=kLoop, calls=%fused_computation.59 | loop fusion | flops 25935872 | bytes 5834752 | tf_op jit(solution)/shard_map/reduce_sum | solution.py:375
  116.9 0.1 stack.180
  117.1 0.1 stack.198
  117.2 0.6 pad_maximum_fusion.3.st_ref
  117.8 13.8 %shard_map.78 = bf16[16,2,16,512]{3,2,1,0:T(8,128)(2,1)} custom-call(bf16[2,16,512]{2,1,0:T(8,128)(2,1)} %pad_maximum_fusion.3.st_ref), custom_call_target="tpu_custom_call" | custom-call | bytes 1048576 | tf_op jit(solution)/shard_map/pallas_call | solution.py:229
  131.7 0.0 copy-done.6
  131.7 1.6 fusion.6
  133.3 0.0 copy-done.7
  133.5 0.3 fusion.154
  133.8 0.3 fusion.140
  134.1 0.3 fusion.137
  134.4 0.3 fusion.138
  134.6 0.5 multiply_subtract_fusion.1
  135.1 0.1 bitcast_select_fusion.2
  135.3 0.0 copy-start.2
  135.3 6.9 %fusion = f32[1024,512]{1,0:T(8,128)S(1)} fusion(f32[512,512]{1,0:T(8,128)S(1)} %bitcast_select_fusion.2, f32[512,512]{1,0:T(8,128)S(1)} %bitcast.132, f32[512]{0:T(512)S(1)} %bitcast.202, f32[512]{0:T(512)S(1)} %bitcast.238, f32[512]{0:T(512)S(1)} %bitcast.146, f32[512]{0:T(512)S(1)} %bitcast.239, f32[512]{0:T(512)S(1)} %bitcast.150, f32[512]{0:T(512)S(1)} %bitcast.240, ...), kind=kOutput, calls=%fused_computation.2 | convolution fusion | flops 3234070528 | bytes 4259840 | tf_op jit(solution)/shard_map/dot_general | solution.py:402
  142.2 0.0 copy-start
  142.2 0.0 copy-done.2
  142.2 0.8 fusion.7
  143.0 0.5 copy-done
  143.5 0.0 copy-start.3
  143.5 0.1 multiply_add_fusion
  143.7 0.1 fusion.25
  143.8 0.9 copy-done.3
  144.8 0.0 copy-start.1
  144.8 0.0 slice-start
  144.8 0.7 fusion.18
  145.5 0.8 copy-done.1
  146.4 0.0 slice-done
  146.4 0.6 subtract_convert_fusion.2
  147.0 0.3 fusion.158
  147.4 0.3 fusion.146
  147.7 0.5 fusion.143
  148.2 0.3 fusion.144
  148.4 0.6 multiply_subtract_fusion
  149.0 0.0 copy-start.8
  149.0 0.4 fusion.27
  149.5 0.3 copy-done.8
  149.7 0.0 copy-start.4
  149.7 3.3 %fusion.2 = f32[512,512]{0,1:T(8,128)S(1)} fusion(bf16[512,512]{0,1:T(8,128)(2,1)S(1)} %get-tuple-element.142, bf16[512,512]{0,1:T(8,128)(2,1)S(1)} %get-tuple-element.148, bf16[512,512]{1,0:T(8,128)(2,1)S(1)} %get-tuple-element.67, bf16[512,512]{1,0:T(8,128)(2,1)S(1)} %get-tuple-element.68, f32[512,512]{0,1:T(8,128)S(1)} %copy-done.3, ...), kind=kOutput, calls=%fused_computation.6 | convolution fusion | flops 554172416 | bytes 4263936 | tf_op jit(solution)/shard_map/dot_general | solution.py:60
  153.0 0.0 copy-done.4
  153.1 4.5 %fusion.64 = (bf16[512,1,512]{0,2,1:T(8,128)(2,1)S(1)}, bf16[512,1,512]{0,2,1:T(8,128)(2,1)S(1)}, bf16[512,512]{0,1:T(8,128)(2,1)}, bf16[512,1,512]{0,2,1:T(8,128)(2,1)S(1)}) fusion(f32[512,512]{0,1:T(8,128)S(1)} %fusion.2, f32[512,3,512]{0,2,1:T(8,128)S(1)} %bitcast.135, bf16[512,512]{0,1:T(8,128)(2,1)S(1)} %copy-done.4, f32[512,512]{0,1:T(8,128)S(1)} %copy-done.2, ...), kind=kOutput, calls=%fused_computation.145 | convolution fusion | flops 556531712 | bytes 10031104 | tf_op jit(solution)/shard_map/dot_general | solution.py:60
  157.6 0.2 pad_maximum_fusion.2
  157.7 1.6 copy.19.gp_ref
  159.3 0.0 copy-start.5
  159.3 82.6 %shard_map.79 = bf16[512,2048]{1,0:T(8,128)(2,1)} custom-call(bf16[512,1536]{1,0:T(8,128)(2,1)} %copy.19.gp_ref, bf16[8192,1536]{1,0:T(8,128)(2,1)} %shard_map.77.w_hbm), custom_call_target="tpu_custom_call" | custom-call | flops 12884901888 | bytes 28835840 | tf_op jit(solution)/shard_map/pallas_call | solution.py:313
  241.9 0.0 copy-done.5
  241.9 1.0 copy.20
  242.9 3.2 %copy.22 = bf16[512,2048]{1,0:T(8,128)(2,1)} copy(bf16[512,2048]{1,0:T(8,128)(2,1)} %shard_map.79) | data formatting | bytes 4194304
  (48 shorter events, 0.4 us)
Async XLA Ops:
  107.7 24.0 %copy-start.6 = (f32[16,512]{1,0:T(8,128)S(1)}, f32[16,512]{1,0:T(8,128)}, u32[]{:S(2)}) copy-start(f32[16,512]{1,0:T(8,128)} %param.9) | copy-start | bytes 98308
  107.7 25.6 %copy-start.7 = (f32[16,512]{1,0:T(8,128)S(1)}, f32[16,512]{1,0:T(8,128)}, u32[]{:S(2)}) copy-start(f32[16,512]{1,0:T(8,128)} %param.8) | copy-start | bytes 98308
  135.3 7.0 %copy-start.2 = (f32[512,512]{0,1:T(8,128)S(1)}, f32[512,512]{0,1:T(8,128)}, u32[]{:S(2)}) copy-start(f32[512,512]{0,1:T(8,128)} %get-tuple-element.59) | copy-start | bytes 3145732
  142.2 1.3 copy-start
  143.5 1.2 copy-start.3
  144.8 1.6 copy-start.1
  144.8 1.6 slice-start
  149.0 0.7 copy-start.8
  149.7 3.3 %copy-start.4 = (bf16[512,512]{0,1:T(8,128)(2,1)S(1)}, bf16[512,512]{0,1:T(8,128)(2,1)}, u32[]{:S(2)}) copy-start(bf16[512,512]{0,1:T(8,128)(2,1)} %copy.18) | copy-start | bytes 1572868
  159.3 82.6 %copy-start.5 = (bf16[512,512]{0,1:T(8,128)(2,1)S(1)}, bf16[512,512]{0,1:T(8,128)(2,1)}, u32[]{:S(2)}) copy-start(bf16[512,512]{0,1:T(8,128)(2,1)} %get-tuple-element.66) | copy-start | bytes 1572868

commit v15 on v13

--- a/solution.py
+++ b/solution.py
@@ -263,6 +263,7 @@
         for d in (0, 1):
             loads[d].wait()
             product(d)
+        for d in (0, 1):
             if copies[d] is not None:
                 copies[d].wait_recv()
                 copies[d].wait_send()
@@ -282,6 +283,7 @@
     for d in (0, 1):
         loads[d].wait()
         product(d)
+    for d in (0, 1):
         copies[d].wait_recv()
         copies[d].wait_send()
         out_ref[:, pl.ds(d * half, half)] = (

time: 248 us -> 248 us (level)
  no operation moved by 1% of the time
where the time goes in v15:
time: 248 us
  Pallas kernels  178 us (72%)
  matrix products  36.3 us (15%)
  other arithmetic  17.5 us (7%)
  local copies, waits for them, and re-layouts  15.1 us (6%)
    pallas_call x1, Pallas kernels, ring_reduce(): pl.pallas_call(functools.partial(ring_kernel, n), out_shape=jax.ShapeDtyp...  85.2 us
    pallas_call x1, Pallas kernels, gather_rows(): pl.pallas_call(gather_kernel, out_shape=jax.ShapeDtypeStruct((total, widt...  79.6 us
    dot_general x1, matrix products, local(): projected = jnp.dot(tokens, whole_w, preferred_element_type=f32)  20.1 us
    pallas_call x1, Pallas kernels, exchange_states(): pl.pallas_call(state_kernel, out_shape=jax.ShapeDtypeStruct((count,) + st...  13 us
    unnamed x22, local copies, waits for them, and re-layouts  10.2 us
    reduce_sum x1, other arithmetic, local(): jnp.sum(jnp.exp(-rates[r] * col) * grad_mix, axis=0)  8.97 us
    dot_general x2, matrix products, spectral_conv(): return jnp.dot(inv, prod, preferred_element_type=f32)  7.81 us
    dot_general x1, matrix products, local(): spec = jnp.dot(fwd, taps, precision=lax.Precision.HIGHEST)  6.93 us

profile of v15, /device:TPU:32, one launch (start us, length us, event | category | flops | bytes accessed | tf_op | source)
XLA Modules:
  0.0 247.9 jit_solution(179178450851773588)
XLA Ops:
  0.6 1.1 slice_negate_fusion.15
  1.7 1.4 copy.15
  3.1 1.2 copy.16.shard_ref
  4.3 79.6 %shard_map.77.w_hbm = bf16[8192,1536]{1,0:T(8,128)(2,1)} custom-call(bf16[256,1536]{1,0:T(8,128)(2,1)} %copy.16.shard_ref), custom_call_target="tpu_custom_call" | custom-call | bytes 50331648 | tf_op jit(solution)/shard_map/pallas_call | solution.py:156
  83.8 20.1 %convolution_convert_fusion = bf16[512,1536]{1,0:T(8,128)(2,1)} fusion(bf16[512,8192]{1,0:T(8,128)(2,1)} %param.6, bf16[8192,1536]{1,0:T(8,128)(2,1)} %shard_map.77.w_hbm), kind=kOutput, calls=%fused_computation | convolution fusion | flops 12885688320 | bytes 35127296 | tf_op jit(solution)/shard_map/dot_general | solution.py:337
  103.9 1.7 copy.17
  105.7 2.0 copy.18
  107.7 0.0 copy-start.6
  107.7 0.0 copy-start.7
  107.7 9.0 %multiply_reduce_fusion = (bf16[512]{0:T(512)(128)(2,1)S(1)}, bf16[512]{0:T(512)(128)(2,1)S(1)}, bf16[512]{0:T(512)(128)(2,1)S(1)}, bf16[512]{0:T(512)(128)(2,1)...) fusion(f32[512]{0:T(512)S(1)} %bitcast.201, ...), kind=kLoop, calls=%fused_computation.59 | loop fusion | flops 25935872 | bytes 5834752 | tf_op jit(solution)/shard_map/reduce_sum | solution.py:360
  116.9 0.1 stack.180
  117.1 0.1 stack.198
  117.2 0.6 pad_maximum_fusion.3.st_ref
  117.8 13.0 %shard_map.78 = bf16[32,16,512]{2,1,0:T(8,128)(2,1)} custom-call(bf16[2,16,512]{2,1,0:T(8,128)(2,1)} %pad_maximum_fusion.3.st_ref), custom_call_target="tpu_custom_call" | custom-call | bytes 2097152 | tf_op jit(solution)/shard_map/pallas_call | solution.py:217
  130.8 0.0 copy-done.6
  130.9 1.6 fusion.6
  132.5 0.0 copy-done.7
  132.6 0.3 fusion.154
  133.0 0.3 fusion.140
  133.3 0.3 fusion.137
  133.5 0.3 fusion.138
  133.8 0.5 multiply_subtract_fusion.1
  134.3 0.1 bitcast_select_fusion.2
  134.4 0.0 copy-start.2
  134.4 6.9 %fusion = f32[1024,512]{1,0:T(8,128)S(1)} fusion(f32[512,512]{1,0:T(8,128)S(1)} %bitcast_select_fusion.2, f32[512,512]{1,0:T(8,128)S(1)} %bitcast.132, f32[512]{0:T(512)S(1)} %bitcast.202, f32[512]{0:T(512)S(1)} %bitcast.238, f32[512]{0:T(512)S(1)} %bitcast.146, f32[512]{0:T(512)S(1)} %bitcast.239, f32[512]{0:T(512)S(1)} %bitcast.150, f32[512]{0:T(512)S(1)} %bitcast.240, ...), kind=kOutput, calls=%fused_computation.2 | convolution fusion | flops 3234070528 | bytes 4259840 | tf_op jit(solution)/shard_map/dot_general | solution.py:387
  141.4 0.0 copy-start
  141.4 0.0 copy-done.2
  141.4 0.8 fusion.7
  142.2 0.5 copy-done
  142.7 0.0 copy-start.3
  142.7 0.1 multiply_add_fusion
  142.8 0.1 fusion.25
  143.0 0.9 copy-done.3
  143.9 0.0 copy-start.1
  143.9 0.0 slice-start
  143.9 0.7 fusion.18
  144.7 0.8 copy-done.1
  145.5 0.0 slice-done
  145.5 0.6 subtract_convert_fusion.2
  146.2 0.3 fusion.158
  146.5 0.5 fusion.146
  147.0 0.3 fusion.143
  147.3 0.3 fusion.144
  147.6 0.6 multiply_subtract_fusion
  148.2 0.0 copy-start.8
  148.2 0.4 fusion.27
  148.6 0.3 copy-done.8
  148.9 0.0 copy-start.4
  148.9 3.3 %fusion.2 = f32[512,512]{0,1:T(8,128)S(1)} fusion(bf16[512,512]{0,1:T(8,128)(2,1)S(1)} %get-tuple-element.142, bf16[512,512]{0,1:T(8,128)(2,1)S(1)} %get-tuple-element.148, bf16[512,512]{1,0:T(8,128)(2,1)S(1)} %get-tuple-element.67, bf16[512,512]{1,0:T(8,128)(2,1)S(1)} %get-tuple-element.68, f32[512,512]{0,1:T(8,128)S(1)} %copy-done.3, ...), kind=kOutput, calls=%fused_computation.6 | convolution fusion | flops 554172416 | bytes 4263936 | tf_op jit(solution)/shard_map/dot_general | solution.py:60
  152.2 0.0 copy-done.4
  152.2 4.5 %fusion.64 = (bf16[512,1,512]{0,2,1:T(8,128)(2,1)S(1)}, bf16[512,1,512]{0,2,1:T(8,128)(2,1)S(1)}, bf16[512,512]{0,1:T(8,128)(2,1)}, bf16[512,1,512]{0,2,1:T(8,128)(2,1)S(1)}) fusion(f32[512,512]{0,1:T(8,128)S(1)} %fusion.2, f32[512,3,512]{0,2,1:T(8,128)S(1)} %bitcast.135, bf16[512,512]{0,1:T(8,128)(2,1)S(1)} %copy-done.4, f32[512,512]{0,1:T(8,128)S(1)} %copy-done.2, ...), kind=kOutput, calls=%fused_computation.145 | convolution fusion | flops 556531712 | bytes 10031104 | tf_op jit(solution)/shard_map/dot_general | solution.py:60
  156.7 0.2 pad_maximum_fusion.2
  156.9 1.6 copy.19.gp_ref
  158.5 0.0 copy-start.5
  158.5 85.2 %shard_map.79 = bf16[512,2048]{1,0:T(8,128)(2,1)} custom-call(bf16[512,1536]{1,0:T(8,128)(2,1)} %copy.19.gp_ref, bf16[8192,1536]{1,0:T(8,128)(2,1)} %shard_map.77.w_hbm), custom_call_target="tpu_custom_call" | custom-call | flops 12884901888 | bytes 28835840 | tf_op jit(solution)/shard_map/pallas_call | solution.py:298
  243.7 0.0 copy-done.5
  243.7 1.0 copy.20
  244.7 3.2 %copy.22 = bf16[512,2048]{1,0:T(8,128)(2,1)} copy(bf16[512,2048]{1,0:T(8,128)(2,1)} %shard_map.79) | data formatting | bytes 4194304
  (48 shorter events, 0.4 us)
Async XLA Ops:
  107.7 23.1 %copy-start.6 = (f32[16,512]{1,0:T(8,128)S(1)}, f32[16,512]{1,0:T(8,128)}, u32[]{:S(2)}) copy-start(f32[16,512]{1,0:T(8,128)} %param.9) | copy-start | bytes 98308
  107.7 24.8 %copy-start.7 = (f32[16,512]{1,0:T(8,128)S(1)}, f32[16,512]{1,0:T(8,128)}, u32[]{:S(2)}) copy-start(f32[16,512]{1,0:T(8,128)} %param.8) | copy-start | bytes 98308
  134.4 7.0 %copy-start.2 = (f32[512,512]{0,1:T(8,128)S(1)}, f32[512,512]{0,1:T(8,128)}, u32[]{:S(2)}) copy-start(f32[512,512]{0,1:T(8,128)} %get-tuple-element.59) | copy-start | bytes 3145732
  141.4 1.3 copy-start
  142.7 1.2 copy-start.3
  143.9 1.6 copy-start.1
  143.9 1.6 slice-start
  148.2 0.7 copy-start.8
  148.9 3.3 %copy-start.4 = (bf16[512,512]{0,1:T(8,128)(2,1)S(1)}, bf16[512,512]{0,1:T(8,128)(2,1)}, u32[]{:S(2)}) copy-start(bf16[512,512]{0,1:T(8,128)(2,1)} %copy.18) | copy-start | bytes 1572868
  158.5 85.2 %copy-start.5 = (bf16[512,512]{0,1:T(8,128)(2,1)S(1)}, bf16[512,512]{0,1:T(8,128)(2,1)}, u32[]{:S(2)}) copy-start(bf16[512,512]{0,1:T(8,128)(2,1)} %get-tuple-element.66) | copy-start | bytes 1572868

commit v16 on v13

--- a/solution.py
+++ b/solution.py
@@ -112,9 +112,10 @@
     own.start()
     up = push(shard_ref, mine, device(a0 + 1, b0, core), 0)
     down = push(shard_ref, mine, device(a0 - 1, b0, core), 1)
+    push(shard_ref, mine, device(a0, b0 + 1, core), 3)
+    push(shard_ref, mine, device(a0, b0 - 1, core), 7)
+    push(shard_ref, mine, partner, 15)
     own.wait()
-    along_b(0)
-    push(mine, mine, partner, 15)
     up.wait_recv()
     fwd = push(slot(a0 - 1, b0), slot(a0 - 1, b0), device(a0 + 1, b0, core), 2)
     along_b(3)

time: 248 us -> 249 us (level)
  no operation moved by 1% of the time
where the time goes in v16:
time: 249 us; the launch traced here: 248 us
  Pallas kernels  178 us (71%)
  matrix products  36.3 us (15%)
  other arithmetic  17.5 us (7%)
  local copies, waits for them, and re-layouts  15.1 us (6%)
    pallas_call x1, Pallas kernels, ring_reduce(): pl.pallas_call(functools.partial(ring_kernel, n), out_shape=jax.ShapeDtyp...  84.6 us
    pallas_call x1, Pallas kernels, gather_rows(): pl.pallas_call(gather_kernel, out_shape=jax.ShapeDtypeStruct((total, widt...  79.8 us
    dot_general x1, matrix products, local(): projected = jnp.dot(tokens, whole_w, preferred_element_type=f32)  20.1 us
    pallas_call x1, Pallas kernels, exchange_states(): pl.pallas_call(state_kernel, out_shape=jax.ShapeDtypeStruct((count,) + st...  13.4 us
    unnamed x22, local copies, waits for them, and re-layouts  10.2 us
    reduce_sum x1, other arithmetic, local(): jnp.sum(jnp.exp(-rates[r] * col) * grad_mix, axis=0)  8.97 us
    dot_general x2, matrix products, spectral_conv(): return jnp.dot(inv, prod, preferred_element_type=f32)  7.81 us
    dot_general x1, matrix products, local(): spec = jnp.dot(fwd, taps, precision=lax.Precision.HIGHEST)  6.93 us

profile of v16, /device:TPU:32, one launch (start us, length us, event | category | flops | bytes accessed | tf_op | source)
XLA Modules:
  0.0 247.8 jit_solution(7633976217488354440)
XLA Ops:
  0.6 1.1 slice_negate_fusion.15
  1.7 1.4 copy.15
  3.1 1.2 copy.16.shard_ref
  4.3 79.8 %shard_map.77.w_hbm = bf16[8192,1536]{1,0:T(8,128)(2,1)} custom-call(bf16[256,1536]{1,0:T(8,128)(2,1)} %copy.16.shard_ref), custom_call_target="tpu_custom_call" | custom-call | bytes 50331648 | tf_op jit(solution)/shard_map/pallas_call | solution.py:157
  84.0 20.1 %convolution_convert_fusion = bf16[512,1536]{1,0:T(8,128)(2,1)} fusion(bf16[512,8192]{1,0:T(8,128)(2,1)} %param.6, bf16[8192,1536]{1,0:T(8,128)(2,1)} %shard_map.77.w_hbm), kind=kOutput, calls=%fused_computation | convolution fusion | flops 12885688320 | bytes 35127296 | tf_op jit(solution)/shard_map/dot_general | solution.py:336
  104.1 1.7 copy.17
  105.8 2.0 copy.18
  107.9 0.0 copy-start.6
  107.9 0.0 copy-start.7
  107.9 9.0 %multiply_reduce_fusion = (bf16[512]{0:T(512)(128)(2,1)S(1)}, bf16[512]{0:T(512)(128)(2,1)S(1)}, bf16[512]{0:T(512)(128)(2,1)S(1)}, bf16[512]{0:T(512)(128)(2,1)...) fusion(f32[512]{0:T(512)S(1)} %bitcast.201, ...), kind=kLoop, calls=%fused_computation.59 | loop fusion | flops 25935872 | bytes 5834752 | tf_op jit(solution)/shard_map/reduce_sum | solution.py:359
  117.0 0.1 stack.180
  117.3 0.1 stack.198
  117.4 0.6 pad_maximum_fusion.3.st_ref
  118.0 13.4 %shard_map.78 = bf16[32,16,512]{2,1,0:T(8,128)(2,1)} custom-call(bf16[2,16,512]{2,1,0:T(8,128)(2,1)} %pad_maximum_fusion.3.st_ref), custom_call_target="tpu_custom_call" | custom-call | bytes 2097152 | tf_op jit(solution)/shard_map/pallas_call | solution.py:218
  131.4 0.0 copy-done.6
  131.5 1.6 fusion.6
  133.1 0.0 copy-done.7
  133.2 0.3 fusion.154
  133.6 0.3 fusion.140
  133.9 0.3 fusion.137
  134.1 0.3 fusion.138
  134.4 0.5 multiply_subtract_fusion.1
  134.9 0.1 bitcast_select_fusion.2
  135.0 0.0 copy-start.2
  135.0 6.9 %fusion = f32[1024,512]{1,0:T(8,128)S(1)} fusion(f32[512,512]{1,0:T(8,128)S(1)} %bitcast_select_fusion.2, f32[512,512]{1,0:T(8,128)S(1)} %bitcast.132, f32[512]{0:T(512)S(1)} %bitcast.202, f32[512]{0:T(512)S(1)} %bitcast.238, f32[512]{0:T(512)S(1)} %bitcast.146, f32[512]{0:T(512)S(1)} %bitcast.239, f32[512]{0:T(512)S(1)} %bitcast.150, f32[512]{0:T(512)S(1)} %bitcast.240, ...), kind=kOutput, calls=%fused_computation.2 | convolution fusion | flops 3234070528 | bytes 4259840 | tf_op jit(solution)/shard_map/dot_general | solution.py:386
  142.0 0.0 copy-start
  142.0 0.0 copy-done.2
  142.0 0.8 fusion.7
  142.8 0.5 copy-done
  143.3 0.0 copy-start.3
  143.3 0.1 multiply_add_fusion
  143.5 0.1 fusion.25
  143.6 0.9 copy-done.3
  144.5 0.0 copy-start.1
  144.5 0.0 slice-start
  144.5 0.7 fusion.18
  145.3 0.8 copy-done.1
  146.1 0.0 slice-done
  146.1 0.6 subtract_convert_fusion.2
  146.8 0.3 fusion.158
  147.1 0.5 fusion.146
  147.7 0.3 fusion.143
  147.9 0.3 fusion.144
  148.2 0.6 multiply_subtract_fusion
  148.8 0.0 copy-start.8
  148.8 0.4 fusion.27
  149.2 0.3 copy-done.8
  149.5 0.0 copy-start.4
  149.5 3.3 %fusion.2 = f32[512,512]{0,1:T(8,128)S(1)} fusion(bf16[512,512]{0,1:T(8,128)(2,1)S(1)} %get-tuple-element.142, bf16[512,512]{0,1:T(8,128)(2,1)S(1)} %get-tuple-element.148, bf16[512,512]{1,0:T(8,128)(2,1)S(1)} %get-tuple-element.67, bf16[512,512]{1,0:T(8,128)(2,1)S(1)} %get-tuple-element.68, f32[512,512]{0,1:T(8,128)S(1)} %copy-done.3, ...), kind=kOutput, calls=%fused_computation.6 | convolution fusion | flops 554172416 | bytes 4263936 | tf_op jit(solution)/shard_map/dot_general | solution.py:60
  152.8 0.0 copy-done.4
  152.8 4.5 %fusion.64 = (bf16[512,1,512]{0,2,1:T(8,128)(2,1)S(1)}, bf16[512,1,512]{0,2,1:T(8,128)(2,1)S(1)}, bf16[512,512]{0,1:T(8,128)(2,1)}, bf16[512,1,512]{0,2,1:T(8,128)(2,1)S(1)}) fusion(f32[512,512]{0,1:T(8,128)S(1)} %fusion.2, f32[512,3,512]{0,2,1:T(8,128)S(1)} %bitcast.135, bf16[512,512]{0,1:T(8,128)(2,1)S(1)} %copy-done.4, f32[512,512]{0,1:T(8,128)S(1)} %copy-done.2, ...), kind=kOutput, calls=%fused_computation.145 | convolution fusion | flops 556531712 | bytes 10031104 | tf_op jit(solution)/shard_map/dot_general | solution.py:60
  157.3 0.2 pad_maximum_fusion.2
  157.5 1.6 copy.19.gp_ref
  159.1 0.0 copy-start.5
  159.1 84.6 %shard_map.79 = bf16[512,2048]{1,0:T(8,128)(2,1)} custom-call(bf16[512,1536]{1,0:T(8,128)(2,1)} %copy.19.gp_ref, bf16[8192,1536]{1,0:T(8,128)(2,1)} %shard_map.77.w_hbm), custom_call_target="tpu_custom_call" | custom-call | flops 12884901888 | bytes 28835840 | tf_op jit(solution)/shard_map/pallas_call | solution.py:297
  243.6 0.0 copy-done.5
  243.7 1.0 copy.20
  244.7 3.2 %copy.22 = bf16[512,2048]{1,0:T(8,128)(2,1)} copy(bf16[512,2048]{1,0:T(8,128)(2,1)} %shard_map.79) | data formatting | bytes 4194304
  (48 shorter events, 0.4 us)
Async XLA Ops:
  107.9 23.6 %copy-start.6 = (f32[16,512]{1,0:T(8,128)S(1)}, f32[16,512]{1,0:T(8,128)}, u32[]{:S(2)}) copy-start(f32[16,512]{1,0:T(8,128)} %param.9) | copy-start | bytes 98308
  107.9 25.2 %copy-start.7 = (f32[16,512]{1,0:T(8,128)S(1)}, f32[16,512]{1,0:T(8,128)}, u32[]{:S(2)}) copy-start(f32[16,512]{1,0:T(8,128)} %param.8) | copy-start | bytes 98308
  135.0 7.0 %copy-start.2 = (f32[512,512]{0,1:T(8,128)S(1)}, f32[512,512]{0,1:T(8,128)}, u32[]{:S(2)}) copy-start(f32[512,512]{0,1:T(8,128)} %get-tuple-element.59) | copy-start | bytes 3145732
  142.0 1.3 copy-start
  143.3 1.2 copy-start.3
  144.5 1.6 copy-start.1
  144.5 1.6 slice-start
  148.8 0.7 copy-start.8
  149.5 3.3 %copy-start.4 = (bf16[512,512]{0,1:T(8,128)(2,1)S(1)}, bf16[512,512]{0,1:T(8,128)(2,1)}, u32[]{:S(2)}) copy-start(bf16[512,512]{0,1:T(8,128)(2,1)} %copy.18) | copy-start | bytes 1572868
  159.1 84.6 %copy-start.5 = (bf16[512,512]{0,1:T(8,128)(2,1)S(1)}, bf16[512,512]{0,1:T(8,128)(2,1)}, u32[]{:S(2)}) copy-start(bf16[512,512]{0,1:T(8,128)(2,1)} %get-tuple-element.66) | copy-start | bytes 1572868
